TPU v7x, 32 devices: a whole 2x2x4 slice. The times are simulated.
32 devices in a mesh: dp: 8 (over y, x, core), tensor: 4 (over z).
Axes of the slice: x: 2, y: 2, z: 4, core: 2. Of those that a mesh axis runs over, the one named last changes fastest.
Arguments:
- acts: bfloat16 [8192, 256], P('dp'), may hold values from -6 to 6
- out_grad: bfloat16 [8192, 4096], P('dp', 'tensor'), may hold values from -6 to 6
- weight: float32 [256, 4096], P(None, 'tensor'), may hold values from -0.375 to 0.375
- error: float32 [8, 256, 4096], P('dp', None, 'tensor'), may hold values from -6 to 6
- start_q: float32 [4096, 64], P('tensor'), may hold values from -0.1875 to 0.1875
Outputs:
- new_weight: float32 [256, 4096], P(None, 'tensor')
- new_error: float32 [8, 256, 4096], P('dp', None, 'tensor')
- input_grad: float32 [8192, 256], P(('dp', 'tensor'))
All inputs are finite; a program needn't handle non-finite values.
Results may differ from a plain program's by a relative error of at most 0.0003.
Values sent between devices are 32-bit elements; how exact they have to be, the bound alone decides.
No kernel may reach another device: no remote copies, remote signals or barrier semaphores. Data moves between devices by JAX's collectives and lax.ppermute only.
A program may use at most 64 MiB of HBM per device.

v0:
```python
import functools
import math

import jax
import jax.numpy as jnp
from jax import lax
from jax.experimental import pallas as pl
from jax.experimental.pallas import tpu as pltpu
from jax.sharding import PartitionSpec as P


F32 = jnp.float32
BF16 = jnp.bfloat16
NN = (((1,), (0,)), ((), ()))
NT = (((1,), (1,)), ((), ()))
VMEM_BYTES = 67043328
SPARE = 27 << 19
VMEM = pl.BlockSpec(memory_space=pltpu.VMEM)
ANY = pl.BlockSpec(memory_space=pl.ANY)
HBM = pl.BlockSpec(memory_space=pltpu.HBM)


def swap(bit_even, bit_odd, size):
    return [(i, i ^ (bit_odd if i & 1 else bit_even)) for i in range(size)]


def split(x):
    high = x.astype(BF16)
    return high, (x - high.astype(F32)).astype(BF16)


def dot(a, b, dims):
    return lax.dot_general(a, b, dims, preferred_element_type=F32)


def dot3(a, b, dims):
    (ah, al), (bh, bl) = split(a), split(b)
    return dot(ah, bh, dims) + (dot(ah, bl, dims) + dot(al, bh, dims))


def rounds_of(n):
    flows = sorted(
        ((a, b) for a in range(n) for b in range(n) if a != b),
        key=lambda flow: (abs(flow[0] - flow[1]), flow),
    )

    def fill(chosen, order):
        for a, b in list(flows)[::order]:
            if a not in chosen and all(b != to for to, _ in chosen.values()):
                chosen[a] = (b, b)
                flows.remove((a, b))
        return chosen

    relay, last = {}, {}
    if n >= 4:
        for gone in ((0, n - 2), (n - 1, 1), (1, n - 2), (n - 2, 1)):
            flows.remove(gone)
        relay = fill({0: (1, n - 2), n - 1: (n - 2, 1)}, -1)
        last = fill({1: (n - 2, n - 2), n - 2: (1, 1)}, -1)
    plain = []
    while flows:
        plain.append(fill({}, 1))
    rounds = [relay, last, *plain] if relay else plain
    if len(rounds) == n - 1 and all(len(one) == n for one in rounds):
        return rounds, bool(relay)
    return [{a: ((a + k) % n,) * 2 for a in range(n)} for k in range(1, n)], False


def pick(me, table, n):
    index = jnp.int32(0)
    for a in range(n):
        index = jnp.where(me == a, table[a][1] if a in table else a, index)
    return index


def blocks_kernel(tables, n, chunks, acts, og, wt, acts_t, *rest):
    rows_v, outs = rest[:n], rest[n : 2 * n]
    acts_v, wt_v, wt_2, sems = rest[2 * n :]
    tok = acts.shape[0]
    _, cols = wt.shape
    block = tok // n
    width = cols // chunks
    me = lax.axis_index("tensor")
    places = [pl.multiple_of(pick(me, table, n) * block, block) for table in tables]

    def load(src, dst, at):
        copy = pltpu.make_async_copy(src, dst, sems.at[at])
        copy.start()
        return copy

    acts_in = [
        load(acts.at[pl.ds(at, block), :], acts_v.at[k * block : (k + 1) * block, :], k)
        for k, at in enumerate(places)
    ]
    wt_in = [
        load(wt.at[:, c * width : (c + 1) * width], wt_v.at[c], 2 * n + c) for c in range(chunks)
    ]
    rows_in = [load(og.at[pl.ds(at, block), :], rows_v[k], n + k) for k, at in enumerate(places)]
    for copy in acts_in:
        copy.wait()
    acts_t[...] = acts_v[...].T
    for c in range(chunks):
        wt_in[c].wait()
        high, low = split(wt_v[c])
        wt_2[:, c * width : (c + 1) * width] = high
        wt_2[:, cols + c * width : cols + (c + 1) * width] = low
    for copy in rows_in:
        copy.wait()
    for k in range(n):
        rows = rows_v[k][...]
        outs[k][...] = dot(jnp.concatenate([rows, rows], axis=1), wt_2[...], NT)


def blocks_of(acts, og, wt, rounds):
    n = len(rounds) + 1
    tok = og.shape[0]
    din, cols = wt.shape
    chunks = 2
    block = tok // n
    shape = jax.ShapeDtypeStruct
    out = pl.pallas_call(
        functools.partial(blocks_kernel, [{}, *rounds], n, chunks),
        out_shape=[shape((din, tok), BF16)]
        + [shape((block, cols), BF16)] * n
        + [shape((block, din), F32)] * n,
        in_specs=[HBM] * 3,
        out_specs=[VMEM] * (1 + 2 * n),
        scratch_shapes=[
            pltpu.VMEM((tok, din), BF16),
            pltpu.VMEM((chunks, din, cols // chunks), F32),
            pltpu.VMEM((din, 2 * cols), BF16),
            pltpu.SemaphoreType.DMA((2 * n + chunks,)),
        ],
        compiler_params=pltpu.CompilerParams(vmem_limit_bytes=VMEM_BYTES - SPARE),
        cost_estimate=pl.CostEstimate(
            flops=4 * tok * din * cols, bytes_accessed=4 << 20, transcendentals=0
        ),
        name="blocks",
    )(acts, og, wt)
    return out[0], out[1 : 1 + n], out[1 + n :]


def merged_kernel(acts_t, err, *rest):
    rows, (theirs, mine) = rest[:-2], rest[-2:]
    tok = acts_t.shape[1]
    half = theirs.shape[1]
    side = lax.rem(lax.axis_index("dp"), 2)
    scale = 1.0 / math.sqrt(tok)
    for where, out in ((1 - side, theirs), (side, mine)):
        span = pl.ds(pl.multiple_of(where * half, half), half)
        columns = jnp.concatenate([one[:, span] for one in rows], axis=0)
        out[...] = dot(acts_t[...], columns, NN) * scale + err[0, :, span]


def merged_of(acts_t, err, rows):
    din, cols = err.shape[1:]
    tok = acts_t.shape[1]
    return pl.pallas_call(
        merged_kernel,
        out_shape=[jax.ShapeDtypeStruct((din, cols // 2), F32)] * 2,
        in_specs=[VMEM] * (2 + len(rows)),
        out_specs=[VMEM] * 2,
        compiler_params=pltpu.CompilerParams(vmem_limit_bytes=8 << 20),
        cost_estimate=pl.CostEstimate(
            flops=2 * tok * din * cols, bytes_accessed=4 << 20, transcendentals=0
        ),
        name="merged",
    )(acts_t, err, *rows)


def is_between(n_tensor):
    me = lax.axis_index("tensor")
    return ((me == 1) | (me == n_tensor - 2)).astype(F32)


def onward_kernel(n_tensor, block, relayed, out):
    out[...] = block[...] + is_between(n_tensor) * relayed[...]


def gather_kernel(relays, first, *rest):
    total = first[...]
    if relays:
        total = total * (1.0 - is_between(relays))
    for part in rest[:-1]:
        total = total + part[...]
    rest[-1][...] = total


def summed(kernel, *parts):
    return pl.pallas_call(
        kernel,
        out_shape=jax.ShapeDtypeStruct(parts[0].shape, F32),
        in_specs=[VMEM] * len(parts),
        out_specs=VMEM,
        compiler_params=pltpu.CompilerParams(vmem_limit_bytes=4 << 20),
    )(*parts)


def left_kernel(qt, theirs, mine, o_ref):
    half = theirs.shape[1]
    side = lax.rem(lax.axis_index("dp"), 2)
    far = qt[:, pl.ds(pl.multiple_of((1 - side) * half, half), half)]
    near = qt[:, pl.ds(pl.multiple_of(side * half, half), half)]
    o_ref[...] = dot3(far, theirs[...], NT) + dot3(near, mine[...], NT)


def left_of(qt, theirs, mine):
    return pl.pallas_call(
        left_kernel,
        out_shape=jax.ShapeDtypeStruct((qt.shape[0], mine.shape[0]), F32),
        in_specs=[VMEM] * 3,
        out_specs=VMEM,
        compiler_params=pltpu.CompilerParams(vmem_limit_bytes=8 << 20),
        name="left",
    )(qt, theirs, mine)


def solve_kernel(replicas, a_ref, b_ref, y_ref):
    left = (a_ref[...] + b_ref[...]) * (1.0 / replicas)
    rank, din = left.shape
    gram = lax.dot_general(
        left, left, NT, precision=lax.Precision.HIGHEST, preferred_element_type=F32
    )
    tiles, lanes = rank // 8, 128
    spans = range(0, din, lanes)
    state = [
        [gram[8 * i : 8 * i + 8, :]] + [left[8 * i : 8 * i + 8, at : at + lanes] for at in spans]
        for i in range(tiles)
    ]
    sub = lax.broadcasted_iota(jnp.int32, (8, lanes), 0)
    for k in range(0, rank, 2):
        i, s = divmod(k, 8)
        first = [jnp.broadcast_to(row[0][:, k : k + 1], (8, lanes)) for row in state]
        second = [jnp.broadcast_to(row[0][:, k + 1 : k + 2], (8, lanes)) for row in state]
        a = first[i][s : s + 1, :]
        b = second[i][s : s + 1, :]
        d = second[i][s + 1 : s + 2, :]
        inverse = 1.0 / (a * d - b * b)
        p, q, r = d * inverse, b * inverse, a * inverse
        for part in range(len(state[0])):
            wide = state[0][part].shape[1]
            top = state[i][part][s : s + 1, :]
            low = state[i][part][s + 1 : s + 2, :]
            new_top = p[:, :wide] * top - q[:, :wide] * low
            new_low = r[:, :wide] * low - q[:, :wide] * top
            for j in range(tiles):
                old = state[j][part]
                new = old - first[j][:, :wide] * new_top - second[j][:, :wide] * new_low
                if j == i:
                    new = jnp.where(sub[:, :wide] == s, new_top, new)
                    new = jnp.where(sub[:, :wide] == s + 1, new_low, new)
                state[j][part] = new
    for j in range(tiles):
        for n, at in enumerate(spans):
            y_ref[8 * j : 8 * j + 8, at : at + lanes] = state[j][1 + n]


def solve(a, b, replicas):
    return pl.pallas_call(
        functools.partial(solve_kernel, replicas),
        out_shape=jax.ShapeDtypeStruct(a.shape, F32),
        in_specs=[VMEM] * 2,
        out_specs=VMEM,
        compiler_params=pltpu.CompilerParams(vmem_limit_bytes=4 << 20),
        cost_estimate=pl.CostEstimate(
            flops=1 << 30, bytes_accessed=1 << 20, transcendentals=0
        ),
        name="solve",
    )(a, b)


def begin_kernel(mine, came, *out):
    width = out[0].shape[1]
    for n, ref in enumerate(out):
        here = slice(n * width, (n + 1) * width)
        ref[...] = mine[:, here] + came[:, here]


def begin(mine, came):
    din, half = mine.shape
    return pl.pallas_call(
        begin_kernel,
        out_shape=[jax.ShapeDtypeStruct((din, half // 2), F32)] * 2,
        in_specs=[VMEM] * 2,
        out_specs=[VMEM] * 2,
        compiler_params=pltpu.CompilerParams(vmem_limit_bytes=4 << 20),
        name="begin",
    )(mine, came)


def right_kernel(replicas, left_a, left_b, *rest):
    out = rest[-1]
    left = (left_a[...] + left_b[...]) * (1.0 / replicas)
    width = rest[0].shape[1]
    for n in range(2):
        total = (rest[2 * n][...] + rest[2 * n + 1][...]) * (1.0 / replicas)
        out[:, n * width : (n + 1) * width] = dot3(left, total, NN)


def right_of(left, left_came, parts, replicas):
    width = parts[0].shape[1]
    return pl.pallas_call(
        functools.partial(right_kernel, replicas),
        out_shape=jax.ShapeDtypeStruct((left.shape[0], 2 * width), F32),
        in_specs=[VMEM] * 6,
        out_specs=VMEM,
        compiler_params=pltpu.CompilerParams(vmem_limit_bytes=8 << 20),
        name="right",
    )(left, left_came, *parts)


def back_kernel(near, chunks, o_ref, right, merged, wt, *rest):
    new_w, new_e, wv, ev, sems = rest[-5:]
    width = merged.shape[1] // chunks
    side = lax.rem(lax.axis_index("dp"), 2)
    base = (side if near else 1 - side) * chunks
    flipped = o_ref[...].T
    copies = []
    for c in range(chunks):
        span = pl.ds(pl.multiple_of((base + c) * width, width), width)
        here = slice(c * width, (c + 1) * width)
        delta = dot3(flipped, right[:, here], NN)
        ev[c] = merged[:, here] - delta
        wv[c] = wt[:, span] - delta
        for one in (
            pltpu.make_async_copy(ev.at[c], new_e.at[0, :, span], sems.at[2 * c]),
            pltpu.make_async_copy(wv.at[c], new_w.at[:, span], sems.at[2 * c + 1]),
        ):
            one.start()
            copies.append(one)
    for one in copies:
        one.wait()


def back(near, ortho, right, merged, wt, *kept):
    din, cols = wt.shape
    chunks = 2
    width = cols // 2 // chunks
    return pl.pallas_call(
        functools.partial(back_kernel, near, chunks),
        out_shape=[
            jax.ShapeDtypeStruct((din, cols), F32),
            jax.ShapeDtypeStruct((1, din, cols), F32),
        ],
        in_specs=[VMEM] * 4 + [ANY] * len(kept),
        out_specs=[ANY] * 2,
        input_output_aliases={4 + n: n for n in range(len(kept))},
        scratch_shapes=[
            pltpu.VMEM((chunks, din, width), F32),
            pltpu.VMEM((chunks, din, width), F32),
            pltpu.SemaphoreType.DMA((2 * chunks,)),
        ],
        compiler_params=pltpu.CompilerParams(vmem_limit_bytes=16 << 20),
        name="back_near" if near else "back_far",
    )(ortho, right, merged, wt, *kept)


def send(x, axis, pairs):
    return lax.ppermute(x, axis, pairs)


def step(acts, out_grad, weight, error, start_q):
    replicas = lax.axis_size("dp")
    n_tensor = lax.axis_size("tensor")
    bits = [1 << b for b in range(1, replicas.bit_length() - 1)]
    pair = swap(1, 1, replicas)

    table, relays = rounds_of(n_tensor)
    acts_t, rows, blocks = blocks_of(acts, out_grad, weight, table)

    def across(block, n):
        return send(block, "tensor", [(a, to) for a, (to, _) in sorted(table[n].items())])

    received = [across(blocks[1], 0)]
    theirs, mine = merged_of(acts_t, error, rows)
    came = send(theirs, "dp", pair)
    left = left_of(start_q.T, theirs, mine)
    left_came = send(left, "dp", pair)
    totals = begin(mine, came)
    comes = [None, None]
    for n, (one, other) in enumerate(zip(bits, bits[::-1]), 1):
        if n > 1:
            totals = [total + came for total, came in zip(totals, comes)]
        left = left + left_came
        left_came = send(left, "dp", swap(other, other, replicas))
        comes = [
            send(total, "dp", swap(bit, bit, replicas))
            for total, bit in zip(totals, (one, other))
        ]

    for n in range(1, n_tensor - 1):
        block = blocks[n + 1]
        if relays and n == 1:
            onward = functools.partial(onward_kernel, n_tensor)
            block = summed(onward, block, received[0])
        received.append(across(block, n))
    gather = functools.partial(gather_kernel, n_tensor if relays else None)
    input_grad = summed(gather, *received, blocks[0])

    basis = solve(left, left_came, replicas)
    parts = [totals[0], comes[0], totals[1], comes[1]]
    right = right_of(left, left_came, parts, replicas)
    other = send(right, "dp", pair)
    kept = back(True, basis, right, mine, weight)
    new_weight, new_error = back(False, basis, other, theirs, weight, *kept)
    return (new_weight, new_error, input_grad)


def solution(mesh):
    placed = (
        P("dp", None),
        P("dp", "tensor"),
        P(None, "tensor"),
        P("dp", None, "tensor"),
        P("tensor", None),
    )
    return jax.shard_map(
        step,
        mesh=mesh,
        in_specs=placed,
        out_specs=(P(None, "tensor"), P("dp", None, "tensor"), P(("dp", "tensor"), None)),
        check_vma=False,
    )
```

profile of v0, /device:TPU:0, one launch (start us, length us, event | category | flops | bytes accessed | tf_op | source)
XLA Modules:
  0.0 40.9 jit_solution(15503131805939740930)
XLA Ops:
  0.6 0.0 copy-start.1
  0.6 3.5 %blocks.1 = (bf16[256,1024]{1,0:T(8,128)(2,1)S(1)}, bf16[256,1024]{1,0:T(8,128)(2,1)S(1)}, bf16[256,1024]{1,0:T(8,128)(2,1)S(1)}, bf16[256,1024]{1,0:T(8,128)(2,...) custom-call(bf16[1024,256]{1,0:T(8,128)(2,1)} %acts.1, ...), custom_call_target="tpu_custom_call" | custom-call | flops 1073741824 | bytes 4194304 | tf_op jit(solution)/shard_map/blocks/pallas_call | solution.py:121
  4.2 0.0 copy-done.1
  4.2 0.7 %merged.1 = (f32[256,512]{1,0:T(8,128)S(1)}, f32[256,512]{1,0:T(8,128)S(1)}) custom-call(bf16[256,1024]{1,0:T(8,128)(2,1)S(1)} %get-tuple-element.20.acts_t, f32[1,256,1024]{2,1,0:T(8,128)S(1)} %copy-done.1, bf16[256,1024]{1,0:T(8,128)(2,1)S(1)} %get-tuple-element.21.rest_0_, bf16[256,1024]{1,0:T(8,128)(2,1)S(1)} %get-tuple-element.22.rest_1_, ...), custom_call_target="tpu_custom_call" | custom-call | flops 536870912 | bytes 4194304 | tf_op jit(solution)/shard_map/merged/pallas_call | solution.py:158
  4.9 0.0 copy-start.2
  5.0 0.6 %collective-permute-start.3 = (f32[256,512]{1,0:T(8,128)S(1)}, f32[256,512]{1,0:T(8,128)S(1)}, u32[]{:S(2)}, u32[]{:S(2)}) collective-permute-start(f32[256,512]{1,0:T(8,128)S(1)} %get-tuple-element.25.theirs.merged), channel_id=1, source_target_pairs={{0,4},{4,0},{8,12},{12,8},{16,20},{20,16},{24,28},{28,24},{1,5},{5... | collective-permute-start | bytes 1572872 | tf_op jit(solution)/shard_map/ppermute | solution.py:359
  5.5 1.5 %collective-permute-done.3.came = f32[256,512]{1,0:T(8,128)S(1)} collective-permute-done((f32[256,512]{1,0:T(8,128)S(1)}, f32[256,512]{1,0:T(8,128)S(1)}, u32[]{:S(2)}, u32[]{:S(2)}) %collective-permute-start.3) | collective-permute-done | bytes 524320 | tf_op jit(solution)/shard_map/ppermute | solution.py:359
  7.1 0.1 begin.1
  7.1 2.9 %collective-permute-start.4 = (f32[256,256]{1,0:T(8,128)S(1)}, f32[256,256]{1,0:T(8,128)S(1)}, u32[]{:S(2)}, u32[]{:S(2)}) collective-permute-start(f32[256,256]{1,0:T(8,128)S(1)} %get-tuple-element.27), channel_id=1, source_target_pairs={{0,8},{4,12},{8,0},{12,4},{16,24},{20,28},{24,16},{28,20},{1,9},{5... | collective-permute-start | bytes 786440 | tf_op jit(solution)/shard_map/ppermute | solution.py:359
  10.0 1.5 %collective-permute-start.6 = (f32[256,256]{1,0:T(8,128)S(1)}, f32[256,256]{1,0:T(8,128)S(1)}, u32[]{:S(2)}, u32[]{:S(2)}) collective-permute-start(f32[256,256]{1,0:T(8,128)S(1)} %get-tuple-element.28), channel_id=1, source_target_pairs={{0,16},{4,20},{8,24},{12,28},{16,0},{20,4},{24,8},{28,12},{1,17},{... | collective-permute-start | bytes 786440 | tf_op jit(solution)/shard_map/ppermute | solution.py:359
  11.6 1.6 %collective-permute-start.9 = (f32[256,256]{1,0:T(8,128)S(1)}, f32[256,256]{1,0:T(8,128)S(1)}, u32[]{:S(2)}, u32[]{:S(2)}) collective-permute-start(f32[256,256]{1,0:T(8,128)S(1)} %get-tuple-element.33), channel_id=1, source_target_pairs={{0,1},{1,3},{2,0},{3,2},{4,5},{5,7},{6,4},{7,6},{8,9},{9,11},{10,8... | collective-permute-start | bytes 786440 | tf_op jit(solution)/shard_map/ppermute | solution.py:359
  13.1 3.5 %collective-permute-done.4 = f32[256,256]{1,0:T(8,128)S(1)} collective-permute-done((f32[256,256]{1,0:T(8,128)S(1)}, f32[256,256]{1,0:T(8,128)S(1)}, u32[]{:S(2)}, u32[]{:S(2)}) %collective-permute-start.4) | collective-permute-done | bytes 262176 | tf_op jit(solution)/shard_map/ppermute | solution.py:359
  16.7 1.8 %collective-permute-start.5 = (f32[256,256]{1,0:T(8,128)S(1)}, f32[256,256]{1,0:T(8,128)S(1)}, u32[]{:S(2)}, u32[]{:S(2)}) collective-permute-start(f32[256,256]{1,0:T(8,128)S(1)} %add.14.rest_0_), channel_id=1, source_target_pairs={{0,16},{4,20},{8,24},{12,28},{16,0},{20,4},{24,8},{28,12},{1,17},{... | collective-permute-start | bytes 786440 | tf_op jit(solution)/shard_map/ppermute | solution.py:359
  18.5 0.0 collective-permute-done.6
  18.6 1.6 %collective-permute-start.7 = (f32[256,256]{1,0:T(8,128)S(1)}, f32[256,256]{1,0:T(8,128)S(1)}, u32[]{:S(2)}, u32[]{:S(2)}) collective-permute-start(f32[256,256]{1,0:T(8,128)S(1)} %add.15.rest_2_), channel_id=1, source_target_pairs={{0,8},{4,12},{8,0},{12,4},{16,24},{20,28},{24,16},{28,20},{1,9},{5... | collective-permute-start | bytes 786440 | tf_op jit(solution)/shard_map/ppermute | solution.py:359
  20.1 0.0 copy-done.2
  20.1 0.6 %left.1 = f32[64,256]{1,0:T(8,128)S(1)} custom-call(f32[64,1024]{1,0:T(8,128)S(1)} %bitcast.1, f32[256,512]{1,0:T(8,128)S(1)} %get-tuple-element.25.theirs.merged, f32[256,512]{1,0:T(8,128)S(1)} %get-tuple-element.26.mine.merged), custom_call_target="tpu_custom_call" | custom-call | tf_op jit(solution)/shard_map/left/pallas_call | solution.py:208
  20.7 0.1 collective-permute-start
  20.8 1.6 %collective-permute-start.11 = (f32[256,256]{1,0:T(8,128)S(1)}, f32[256,256]{1,0:T(8,128)S(1)}, u32[]{:S(2)}, u32[]{:S(2)}) collective-permute-start(f32[256,256]{1,0:T(8,128)S(1)} %get-tuple-element.35), channel_id=1, source_target_pairs={{0,1},{1,0},{2,3},{3,2},{4,5},{5,4},{6,7},{7,6},{8,9},{9,8},{10,11... | collective-permute-start | bytes 786440 | tf_op jit(solution)/shard_map/ppermute | solution.py:359
  22.4 0.0 collective-permute-done
  22.5 0.6 %collective-permute-start.1 = (f32[64,256]{1,0:T(8,128)S(1)}, f32[64,256]{1,0:T(8,128)S(1)}, u32[]{:S(2)}, u32[]{:S(2)}) collective-permute-start(f32[64,256]{1,0:T(8,128)S(1)} %add.12), channel_id=1, source_target_pairs={{0,16},{4,20},{8,24},{12,28},{16,0},{20,4},{24,8},{28,12},{1,17},{... | collective-permute-start | bytes 196616 | tf_op jit(solution)/shard_map/ppermute | solution.py:359
  23.0 0.0 collective-permute-done.9.relayed.first
  23.1 3.3 %collective-permute-start.10 = (f32[256,256]{1,0:T(8,128)S(1)}, f32[256,256]{1,0:T(8,128)S(1)}, u32[]{:S(2)}, u32[]{:S(2)}) collective-permute-start(f32[256,256]{1,0:T(8,128)S(1)} %shard_map.76), channel_id=1, source_target_pairs={{0,3},{1,2},{2,1},{3,0},{4,7},{5,6},{6,5},{7,4},{8,11},{9,10},{10,... | collective-permute-start | bytes 786440 | tf_op jit(solution)/shard_map/ppermute | solution.py:359
  26.3 0.5 %collective-permute-done.1 = f32[64,256]{1,0:T(8,128)S(1)} collective-permute-done((f32[64,256]{1,0:T(8,128)S(1)}, f32[64,256]{1,0:T(8,128)S(1)}, u32[]{:S(2)}, u32[]{:S(2)}) %collective-permute-start.1) | collective-permute-done | bytes 65568 | tf_op jit(solution)/shard_map/ppermute | solution.py:359
  26.8 0.7 %collective-permute-start.2 = (f32[64,256]{1,0:T(8,128)S(1)}, f32[64,256]{1,0:T(8,128)S(1)}, u32[]{:S(2)}, u32[]{:S(2)}) collective-permute-start(f32[64,256]{1,0:T(8,128)S(1)} %add.13.a_ref.left_a), channel_id=1, source_target_pairs={{0,8},{4,12},{8,0},{12,4},{16,24},{20,28},{24,16},{28,20},{1,9},{5... | collective-permute-start | bytes 196616 | tf_op jit(solution)/shard_map/ppermute | solution.py:359
  27.5 3.6 %collective-permute-done.2.b_ref.left_b = f32[64,256]{1,0:T(8,128)S(1)} collective-permute-done((f32[64,256]{1,0:T(8,128)S(1)}, f32[64,256]{1,0:T(8,128)S(1)}, u32[]{:S(2)}, u32[]{:S(2)}) %collective-permute-start.2) | collective-permute-done | bytes 65568 | tf_op jit(solution)/shard_map/ppermute | solution.py:359
  31.1 0.0 collective-permute-done.5.rest_1_
  31.1 0.0 collective-permute-done.7.rest_3_
  31.1 0.3 right.1
  31.5 0.0 copy-start
  31.5 0.1 collective-permute-start.8
  31.6 3.5 %solve.1.o_ref = f32[64,256]{1,0:T(8,128)S(1)} custom-call(f32[64,256]{1,0:T(8,128)S(1)} %add.13.a_ref.left_a, f32[64,256]{1,0:T(8,128)S(1)} %collective-permute-done.2.b_ref.left_b), custom_call_target="tpu_custom_call" | custom-call | flops 1073741824 | bytes 1048576 | tf_op jit(solution)/shard_map/solve/pallas_call | solution.py:259
  35.1 0.0 collective-permute-done.11.rest_1_
  35.1 2.2 %collective-permute-done.10.rest_0_ = f32[256,256]{1,0:T(8,128)S(1)} collective-permute-done((f32[256,256]{1,0:T(8,128)S(1)}, f32[256,256]{1,0:T(8,128)S(1)}, u32[]{:S(2)}, u32[]{:S(2)}) %collective-permute-start.10) | collective-permute-done | bytes 262176 | tf_op jit(solution)/shard_map/ppermute | solution.py:359
  37.3 0.8 %shard_map.77 = f32[256,256]{1,0:T(8,128)} custom-call(f32[256,256]{1,0:T(8,128)S(1)} %collective-permute-done.9.relayed.first, f32[256,256]{1,0:T(8,128)S(1)} %collective-permute-done.10.rest_0_, f32[256,256]{1,0:T(8,128)S(1)} %collective-permute-done.11.rest_1_, f32[256,256]{1,0:T(8,128)S(1)} %get-tuple-element.36.rest_2_), custom_call_target="tpu_custom_call" | custom-call | tf_op jit(solution)/shard_map/pallas_call | solution.py:190
  38.0 0.0 copy-done
  38.0 1.4 %back_near.1 = (f32[256,1024]{1,0:T(8,128)}, f32[1,256,1024]{2,1,0:T(8,128)}) custom-call(f32[64,256]{1,0:T(8,128)S(1)} %solve.1.o_ref, f32[64,512]{1,0:T(8,128)S(1)} %right.1, f32[256,512]{1,0:T(8,128)S(1)} %get-tuple-element.26.mine.merged, f32[256,1024]{1,0:T(8,128)S(1)} %copy-done), custom_call_target="tpu_custom_call" | custom-call | tf_op jit(solution)/shard_map/back_near/pallas_call | solution.py:339
  39.4 0.0 collective-permute-done.8.right
  39.5 1.4 %back_far.1 = (f32[256,1024]{1,0:T(8,128)}, f32[1,256,1024]{2,1,0:T(8,128)}) custom-call(f32[64,256]{1,0:T(8,128)S(1)} %solve.1.o_ref, f32[64,512]{1,0:T(8,128)S(1)} %collective-permute-done.8.right, f32[256,512]{1,0:T(8,128)S(1)} %get-tuple-element.25.theirs.merged, f32[256,1024]{1,0:T(8,128)S(1)} %copy-done, ...), custom_call_target="tpu_custom_call", output_to_operand_aliasing={{0}: (4, {}), {1}: (5, {})} | custom-call | tf_op jit(solution)/shard_map/back_far/pallas_call | solution.py:339
  (5 shorter events, 0.1 us)
Async XLA Ops:
  0.6 3.6 %copy-start.1 = (f32[1,256,1024]{2,1,0:T(8,128)S(1)}, f32[1,256,1024]{2,1,0:T(8,128)}, u32[]{:S(2)}) copy-start(f32[1,256,1024]{2,1,0:T(8,128)} %err.1) | copy-start | bytes 3145732
  4.9 15.2 %copy-start.2 = (f32[1024,64]{0,1:T(8,128)S(1)}, f32[1024,64]{0,1:T(8,128)}, u32[]{:S(2)}) copy-start(f32[1024,64]{0,1:T(8,128)} %param.9) | copy-start | bytes 786436
  5.0 2.1 %collective-permute-start.3 = (f32[256,512]{1,0:T(8,128)S(1)}, f32[256,512]{1,0:T(8,128)S(1)}, u32[]{:S(2)}, u32[]{:S(2)}) collective-permute-start(f32[256,512]{1,0:T(8,128)S(1)} %get-tuple-element.25.theirs.merged), channel_id=1, source_target_pairs={{0,4},{4,0},{8,12},{12,8},{16,20},{20,16},{24,28},{28,24},{1,5},{5... | collective-permute-start | bytes 1572872 | tf_op jit(solution)/shard_map/ppermute | solution.py:359
  7.1 9.5 %collective-permute-start.4 = (f32[256,256]{1,0:T(8,128)S(1)}, f32[256,256]{1,0:T(8,128)S(1)}, u32[]{:S(2)}, u32[]{:S(2)}) collective-permute-start(f32[256,256]{1,0:T(8,128)S(1)} %get-tuple-element.27), channel_id=1, source_target_pairs={{0,8},{4,12},{8,0},{12,4},{16,24},{20,28},{24,16},{28,20},{1,9},{5... | collective-permute-start | bytes 786440 | tf_op jit(solution)/shard_map/ppermute | solution.py:359
  10.0 8.5 %collective-permute-start.6 = (f32[256,256]{1,0:T(8,128)S(1)}, f32[256,256]{1,0:T(8,128)S(1)}, u32[]{:S(2)}, u32[]{:S(2)}) collective-permute-start(f32[256,256]{1,0:T(8,128)S(1)} %get-tuple-element.28), channel_id=1, source_target_pairs={{0,16},{4,20},{8,24},{12,28},{16,0},{20,4},{24,8},{28,12},{1,17},{... | collective-permute-start | bytes 786440 | tf_op jit(solution)/shard_map/ppermute | solution.py:359
  11.6 11.5 %collective-permute-start.9 = (f32[256,256]{1,0:T(8,128)S(1)}, f32[256,256]{1,0:T(8,128)S(1)}, u32[]{:S(2)}, u32[]{:S(2)}) collective-permute-start(f32[256,256]{1,0:T(8,128)S(1)} %get-tuple-element.33), channel_id=1, source_target_pairs={{0,1},{1,3},{2,0},{3,2},{4,5},{5,7},{6,4},{7,6},{8,9},{9,11},{10,8... | collective-permute-start | bytes 786440 | tf_op jit(solution)/shard_map/ppermute | solution.py:359
  16.7 14.5 %collective-permute-start.5 = (f32[256,256]{1,0:T(8,128)S(1)}, f32[256,256]{1,0:T(8,128)S(1)}, u32[]{:S(2)}, u32[]{:S(2)}) collective-permute-start(f32[256,256]{1,0:T(8,128)S(1)} %add.14.rest_0_), channel_id=1, source_target_pairs={{0,16},{4,20},{8,24},{12,28},{16,0},{20,4},{24,8},{28,12},{1,17},{... | collective-permute-start | bytes 786440 | tf_op jit(solution)/shard_map/ppermute | solution.py:359
  18.6 12.6 %collective-permute-start.7 = (f32[256,256]{1,0:T(8,128)S(1)}, f32[256,256]{1,0:T(8,128)S(1)}, u32[]{:S(2)}, u32[]{:S(2)}) collective-permute-start(f32[256,256]{1,0:T(8,128)S(1)} %add.15.rest_2_), channel_id=1, source_target_pairs={{0,8},{4,12},{8,0},{12,4},{16,24},{20,28},{24,16},{28,20},{1,9},{5... | collective-permute-start | bytes 786440 | tf_op jit(solution)/shard_map/ppermute | solution.py:359
  20.7 1.7 %collective-permute-start = (f32[64,256]{1,0:T(8,128)S(1)}, f32[64,256]{1,0:T(8,128)S(1)}, u32[]{:S(2)}, u32[]{:S(2)}) collective-permute-start(f32[64,256]{1,0:T(8,128)S(1)} %left.1), channel_id=1, source_target_pairs={{0,4},{4,0},{8,12},{12,8},{16,20},{20,16},{24,28},{28,24},{1,5},{5... | collective-permute-start | bytes 196616 | tf_op jit(solution)/shard_map/ppermute | solution.py:359
  20.8 14.2 %collective-permute-start.11 = (f32[256,256]{1,0:T(8,128)S(1)}, f32[256,256]{1,0:T(8,128)S(1)}, u32[]{:S(2)}, u32[]{:S(2)}) collective-permute-start(f32[256,256]{1,0:T(8,128)S(1)} %get-tuple-element.35), channel_id=1, source_target_pairs={{0,1},{1,0},{2,3},{3,2},{4,5},{5,4},{6,7},{7,6},{8,9},{9,8},{10,11... | collective-permute-start | bytes 786440 | tf_op jit(solution)/shard_map/ppermute | solution.py:359
  22.5 4.3 %collective-permute-start.1 = (f32[64,256]{1,0:T(8,128)S(1)}, f32[64,256]{1,0:T(8,128)S(1)}, u32[]{:S(2)}, u32[]{:S(2)}) collective-permute-start(f32[64,256]{1,0:T(8,128)S(1)} %add.12), channel_id=1, source_target_pairs={{0,16},{4,20},{8,24},{12,28},{16,0},{20,4},{24,8},{28,12},{1,17},{... | collective-permute-start | bytes 196616 | tf_op jit(solution)/shard_map/ppermute | solution.py:359
  23.1 14.2 %collective-permute-start.10 = (f32[256,256]{1,0:T(8,128)S(1)}, f32[256,256]{1,0:T(8,128)S(1)}, u32[]{:S(2)}, u32[]{:S(2)}) collective-permute-start(f32[256,256]{1,0:T(8,128)S(1)} %shard_map.76), channel_id=1, source_target_pairs={{0,3},{1,2},{2,1},{3,0},{4,7},{5,6},{6,5},{7,4},{8,11},{9,10},{10,... | collective-permute-start | bytes 786440 | tf_op jit(solution)/shard_map/ppermute | solution.py:359
  26.8 4.3 %collective-permute-start.2 = (f32[64,256]{1,0:T(8,128)S(1)}, f32[64,256]{1,0:T(8,128)S(1)}, u32[]{:S(2)}, u32[]{:S(2)}) collective-permute-start(f32[64,256]{1,0:T(8,128)S(1)} %add.13.a_ref.left_a), channel_id=1, source_target_pairs={{0,8},{4,12},{8,0},{12,4},{16,24},{20,28},{24,16},{28,20},{1,9},{5... | collective-permute-start | bytes 196616 | tf_op jit(solution)/shard_map/ppermute | solution.py:359
  31.5 6.6 %copy-start = (f32[256,1024]{1,0:T(8,128)S(1)}, f32[256,1024]{1,0:T(8,128)}, u32[]{:S(2)}) copy-start(f32[256,1024]{1,0:T(8,128)} %wt.5) | copy-start | bytes 3145732
  31.5 8.0 %collective-permute-start.8 = (f32[64,512]{1,0:T(8,128)S(1)}, f32[64,512]{1,0:T(8,128)S(1)}, u32[]{:S(2)}, u32[]{:S(2)}) collective-permute-start(f32[64,512]{1,0:T(8,128)S(1)} %right.1), channel_id=1, source_target_pairs={{0,4},{4,0},{8,12},{12,8},{16,20},{20,16},{24,28},{28,24},{1,5},{5... | collective-permute-start | bytes 393224 | tf_op jit(solution)/shard_map/ppermute | solution.py:359
where the time goes:
time: 41 us; the launch traced here: 40.9 us
  starting transfers between devices  16.3 us (40%)
  Pallas kernels  12.4 us (30%)
  waiting for transfers between devices  11.3 us (28%)
  between operations  0.77 us (2%)
    ppermute x12, starting transfers between devices, send(): return lax.ppermute(x, axis, pairs)  16.3 us
    ppermute x12, waiting for transfers between devices, send(): return lax.ppermute(x, axis, pairs)  11.3 us
    pallas_call x1, Pallas kernels, blocks_of(): pl.pallas_call(functools.partial(blocks_kernel, [{}, *rounds], n, chunks)...  3.55 us
    pallas_call x1, Pallas kernels, solve(): pl.pallas_call(functools.partial(solve_kernel, replicas), out_shape=jax.S...  3.49 us
    pallas_call x2, Pallas kernels, back(): pl.pallas_call(functools.partial(back_kernel, near, chunks), out_shape=[j...  2.83 us
  transfers between devices with their start and end apart: 12, of which 5 were waited for; matrix products, arithmetic and copies ran while one was open for 0% of the time, Pallas kernels for 16%

commit v1 on v0

--- a/solution.py
+++ b/solution.py
@@ -269,17 +269,24 @@
     )(a, b)
 
 
-def begin_kernel(mine, came, *out):
-    width = out[0].shape[1]
-    for n, ref in enumerate(out):
-        here = slice(n * width, (n + 1) * width)
-        ref[...] = mine[:, here] + came[:, here]
-
-
-def begin(mine, came):
+def quarter(bits, side, index):
+    even, odd = (lax.rem(index // bit, 2) for bit in (bits[0], bits[-1]))
+    return jnp.where(side == 0, even, odd)
+
+
+def begin_kernel(bits, mine, came, keep, give):
+    width = keep.shape[1]
+    index = lax.axis_index("dp")
+    own = quarter(bits, lax.rem(index, 2), index)
+    for which, out in ((own, keep), (1 - own, give)):
+        span = pl.ds(pl.multiple_of(which * width, width), width)
+        out[...] = mine[:, span] + came[:, span]
+
+
+def begin(mine, came, bits):
     din, half = mine.shape
     return pl.pallas_call(
-        begin_kernel,
+        functools.partial(begin_kernel, bits),
         out_shape=[jax.ShapeDtypeStruct((din, half // 2), F32)] * 2,
         in_specs=[VMEM] * 2,
         out_specs=[VMEM] * 2,
@@ -288,38 +295,35 @@
     )(mine, came)
 
 
-def right_kernel(replicas, left_a, left_b, *rest):
-    out = rest[-1]
+def right_kernel(replicas, left_a, left_b, total_a, total_b, out):
     left = (left_a[...] + left_b[...]) * (1.0 / replicas)
-    width = rest[0].shape[1]
-    for n in range(2):
-        total = (rest[2 * n][...] + rest[2 * n + 1][...]) * (1.0 / replicas)
-        out[:, n * width : (n + 1) * width] = dot3(left, total, NN)
-
-
-def right_of(left, left_came, parts, replicas):
-    width = parts[0].shape[1]
+    out[...] = dot3(left, (total_a[...] + total_b[...]) * (1.0 / replicas), NN)
+
+
+def right_of(left, left_came, total, came, replicas):
     return pl.pallas_call(
         functools.partial(right_kernel, replicas),
-        out_shape=jax.ShapeDtypeStruct((left.shape[0], 2 * width), F32),
-        in_specs=[VMEM] * 6,
+        out_shape=jax.ShapeDtypeStruct((left.shape[0], total.shape[1]), F32),
+        in_specs=[VMEM] * 4,
         out_specs=VMEM,
         compiler_params=pltpu.CompilerParams(vmem_limit_bytes=8 << 20),
         name="right",
-    )(left, left_came, *parts)
-
-
-def back_kernel(near, chunks, o_ref, right, merged, wt, *rest):
+    )(left, left_came, total, came)
+
+
+def back_kernel(near, bits, basis, right_a, right_b, merged, wt, *rest):
     new_w, new_e, wv, ev, sems = rest[-5:]
-    width = merged.shape[1] // chunks
-    side = lax.rem(lax.axis_index("dp"), 2)
-    base = (side if near else 1 - side) * chunks
-    flipped = o_ref[...].T
+    width = right_a.shape[1]
+    index = lax.axis_index("dp")
+    side = lax.rem(index, 2)
+    side = side if near else 1 - side
+    own = quarter(bits, side, index)
+    flipped = basis[...].T
     copies = []
-    for c in range(chunks):
-        span = pl.ds(pl.multiple_of((base + c) * width, width), width)
-        here = slice(c * width, (c + 1) * width)
-        delta = dot3(flipped, right[:, here], NN)
+    for c, (right, which) in enumerate(((right_a, own), (right_b, 1 - own))):
+        here = pl.ds(pl.multiple_of(which * width, width), width)
+        span = pl.ds(pl.multiple_of((2 * side + which) * width, width), width)
+        delta = dot3(flipped, right[...], NN)
         ev[c] = merged[:, here] - delta
         wv[c] = wt[:, span] - delta
         for one in (
@@ -332,27 +336,26 @@
         one.wait()
 
 
-def back(near, ortho, right, merged, wt, *kept):
+def back(near, bits, basis, right_a, right_b, merged, wt, *kept):
     din, cols = wt.shape
-    chunks = 2
-    width = cols // 2 // chunks
-    return pl.pallas_call(
-        functools.partial(back_kernel, near, chunks),
+    width = right_a.shape[1]
+    return pl.pallas_call(
+        functools.partial(back_kernel, near, bits),
         out_shape=[
             jax.ShapeDtypeStruct((din, cols), F32),
             jax.ShapeDtypeStruct((1, din, cols), F32),
         ],
-        in_specs=[VMEM] * 4 + [ANY] * len(kept),
+        in_specs=[VMEM] * 5 + [ANY] * len(kept),
         out_specs=[ANY] * 2,
-        input_output_aliases={4 + n: n for n in range(len(kept))},
+        input_output_aliases={5 + n: n for n in range(len(kept))},
         scratch_shapes=[
-            pltpu.VMEM((chunks, din, width), F32),
-            pltpu.VMEM((chunks, din, width), F32),
-            pltpu.SemaphoreType.DMA((2 * chunks,)),
+            pltpu.VMEM((2, din, width), F32),
+            pltpu.VMEM((2, din, width), F32),
+            pltpu.SemaphoreType.DMA((4,)),
         ],
         compiler_params=pltpu.CompilerParams(vmem_limit_bytes=16 << 20),
         name="back_near" if near else "back_far",
-    )(ortho, right, merged, wt, *kept)
+    )(basis, right_a, right_b, merged, wt, *kept)
 
 
 def send(x, axis, pairs):
@@ -375,18 +378,14 @@
     theirs, mine = merged_of(acts_t, error, rows)
     came = send(theirs, "dp", pair)
     left = left_of(start_q.T, theirs, mine)
+    total, give = begin(mine, came, bits)
+    came = send(give, "dp", swap(bits[0], bits[-1], replicas))
+    left = left + send(left, "dp", swap(bits[-1], bits[0], replicas))
+    for n, (one, other) in enumerate(zip(bits[1:], bits[-2::-1]), 2):
+        total = total + came
+        came = send(total, "dp", swap(one, other, replicas))
+        left = left + send(left, "dp", swap(other, one, replicas))
     left_came = send(left, "dp", pair)
-    totals = begin(mine, came)
-    comes = [None, None]
-    for n, (one, other) in enumerate(zip(bits, bits[::-1]), 1):
-        if n > 1:
-            totals = [total + came for total, came in zip(totals, comes)]
-        left = left + left_came
-        left_came = send(left, "dp", swap(other, other, replicas))
-        comes = [
-            send(total, "dp", swap(bit, bit, replicas))
-            for total, bit in zip(totals, (one, other))
-        ]
 
     for n in range(1, n_tensor - 1):
         block = blocks[n + 1]
@@ -397,12 +396,15 @@
     gather = functools.partial(gather_kernel, n_tensor if relays else None)
     input_grad = summed(gather, *received, blocks[0])
 
+    right = right_of(left, left_came, total, came, replicas)
+    beside = send(right, "dp", swap(bits[0], bits[-1], replicas))
+    across_pair = send(right, "dp", pair)
     basis = solve(left, left_came, replicas)
-    parts = [totals[0], comes[0], totals[1], comes[1]]
-    right = right_of(left, left_came, parts, replicas)
-    other = send(right, "dp", pair)
-    kept = back(True, basis, right, mine, weight)
-    new_weight, new_error = back(False, basis, other, theirs, weight, *kept)
+    beside_across = send(beside, "dp", pair)
+    kept = back(True, bits, basis, right, beside, mine, weight)
+    new_weight, new_error = back(
+        False, bits, basis, across_pair, beside_across, theirs, weight, *kept
+    )
     return (new_weight, new_error, input_grad)
 
 

time: 41 us -> 41.6 us (1.015)
  waiting for transfers between devices: 11.3 us -> 13.4 us
  starting transfers between devices: 16.3 us -> 15 us
    ppermute x12, waiting for transfers between devices: 11.3 us -> 13.4 us  [send(): return lax.ppermute(x, axis, pairs)]
    ppermute x12, starting transfers between devices: 16.3 us -> 15 us  [send(): return lax.ppermute(x, axis, pairs)]
  transfers between devices with their start and end apart: 12 -> 12, of which waited for: 5 -> 6; matrix products, arithmetic and copies ran while one was open for 0% -> 0% of each run, Pallas kernels for 16% -> 16%
where the time goes in v1:
time: 41.6 us; the launch traced here: 41.4 us
  starting transfers between devices  15 us (36%)
  waiting for transfers between devices  13.4 us (32%)
  Pallas kernels  12.2 us (29%)
  between operations  0.76 us (2%)
    ppermute x12, starting transfers between devices, send(): return lax.ppermute(x, axis, pairs)  15 us
    ppermute x12, waiting for transfers between devices, send(): return lax.ppermute(x, axis, pairs)  13.4 us
    pallas_call x1, Pallas kernels, blocks_of(): pl.pallas_call(functools.partial(blocks_kernel, [{}, *rounds], n, chunks)...  3.55 us
    pallas_call x1, Pallas kernels, solve(): pl.pallas_call(functools.partial(solve_kernel, replicas), out_shape=jax.S...  3.49 us
    pallas_call x2, Pallas kernels, back(): pl.pallas_call(functools.partial(back_kernel, near, bits), out_shape=[jax...  2.83 us
  transfers between devices with their start and end apart: 12, of which 6 were waited for; matrix products, arithmetic and copies ran while one was open for 0% of the time, Pallas kernels for 16%

profile of v1, /device:TPU:0, one launch (start us, length us, event | category | flops | bytes accessed | tf_op | source)
XLA Modules:
  0.0 41.4 jit_solution(11192119568982792510)
XLA Ops:
  0.6 0.0 copy-start.1
  0.6 3.5 %blocks.1 = (bf16[256,1024]{1,0:T(8,128)(2,1)S(1)}, bf16[256,1024]{1,0:T(8,128)(2,1)S(1)}, bf16[256,1024]{1,0:T(8,128)(2,1)S(1)}, bf16[256,1024]{1,0:T(8,128)(2,...) custom-call(bf16[1024,256]{1,0:T(8,128)(2,1)} %acts.1, ...), custom_call_target="tpu_custom_call" | custom-call | flops 1073741824 | bytes 4194304 | tf_op jit(solution)/shard_map/blocks/pallas_call | solution.py:121
  4.2 0.0 copy-done.1
  4.2 0.0 copy-start.2
  4.2 0.7 %merged.1 = (f32[256,512]{1,0:T(8,128)S(1)}, f32[256,512]{1,0:T(8,128)S(1)}) custom-call(bf16[256,1024]{1,0:T(8,128)(2,1)S(1)} %get-tuple-element.20.acts_t, f32[1,256,1024]{2,1,0:T(8,128)S(1)} %copy-done.1, bf16[256,1024]{1,0:T(8,128)(2,1)S(1)} %get-tuple-element.21.rest_0_, bf16[256,1024]{1,0:T(8,128)(2,1)S(1)} %get-tuple-element.22.rest_1_, ...), custom_call_target="tpu_custom_call" | custom-call | flops 536870912 | bytes 4194304 | tf_op jit(solution)/shard_map/merged/pallas_call | solution.py:158
  5.0 0.6 %collective-permute-start.3 = (f32[256,512]{1,0:T(8,128)S(1)}, f32[256,512]{1,0:T(8,128)S(1)}, u32[]{:S(2)}, u32[]{:S(2)}) collective-permute-start(f32[256,512]{1,0:T(8,128)S(1)} %get-tuple-element.25.theirs.merged), channel_id=1, source_target_pairs={{0,4},{4,0},{8,12},{12,8},{16,20},{20,16},{24,28},{28,24},{1,5},{5... | collective-permute-start | bytes 1572872 | tf_op jit(solution)/shard_map/ppermute | solution.py:362
  5.5 1.5 %collective-permute-done.3.came = f32[256,512]{1,0:T(8,128)S(1)} collective-permute-done((f32[256,512]{1,0:T(8,128)S(1)}, f32[256,512]{1,0:T(8,128)S(1)}, u32[]{:S(2)}, u32[]{:S(2)}) %collective-permute-start.3) | collective-permute-done | bytes 524320 | tf_op jit(solution)/shard_map/ppermute | solution.py:362
  7.1 0.1 begin.1
  7.1 2.9 %collective-permute-start.4 = (f32[256,256]{1,0:T(8,128)S(1)}, f32[256,256]{1,0:T(8,128)S(1)}, u32[]{:S(2)}, u32[]{:S(2)}) collective-permute-start(f32[256,256]{1,0:T(8,128)S(1)} %get-tuple-element.28), channel_id=1, source_target_pairs={{0,8},{4,20},{8,0},{12,28},{16,24},{20,4},{24,16},{28,12},{1,9},{5... | collective-permute-start | bytes 786440 | tf_op jit(solution)/shard_map/ppermute | solution.py:362
  10.0 1.6 %collective-permute-start.9 = (f32[256,256]{1,0:T(8,128)S(1)}, f32[256,256]{1,0:T(8,128)S(1)}, u32[]{:S(2)}, u32[]{:S(2)}) collective-permute-start(f32[256,256]{1,0:T(8,128)S(1)} %get-tuple-element.33), channel_id=1, source_target_pairs={{0,1},{1,3},{2,0},{3,2},{4,5},{5,7},{6,4},{7,6},{8,9},{9,11},{10,8... | collective-permute-start | bytes 786440 | tf_op jit(solution)/shard_map/ppermute | solution.py:362
  11.6 2.8 %collective-permute-done.4 = f32[256,256]{1,0:T(8,128)S(1)} collective-permute-done((f32[256,256]{1,0:T(8,128)S(1)}, f32[256,256]{1,0:T(8,128)S(1)}, u32[]{:S(2)}, u32[]{:S(2)}) %collective-permute-start.4) | collective-permute-done | bytes 262176 | tf_op jit(solution)/shard_map/ppermute | solution.py:362
  14.4 2.1 %collective-permute-start.5 = (f32[256,256]{1,0:T(8,128)S(1)}, f32[256,256]{1,0:T(8,128)S(1)}, u32[]{:S(2)}, u32[]{:S(2)}) collective-permute-start(f32[256,256]{1,0:T(8,128)S(1)} %add.11.total_a), channel_id=1, source_target_pairs={{0,16},{4,12},{8,24},{12,4},{16,0},{20,28},{24,8},{28,20},{1,17},{... | collective-permute-start | bytes 786440 | tf_op jit(solution)/shard_map/ppermute | solution.py:362
  16.5 0.0 copy-done.2
  16.5 0.6 %left.1 = f32[64,256]{1,0:T(8,128)S(1)} custom-call(f32[64,1024]{1,0:T(8,128)S(1)} %bitcast.1, f32[256,512]{1,0:T(8,128)S(1)} %get-tuple-element.25.theirs.merged, f32[256,512]{1,0:T(8,128)S(1)} %get-tuple-element.26.mine.merged), custom_call_target="tpu_custom_call" | custom-call | tf_op jit(solution)/shard_map/left/pallas_call | solution.py:208
  17.1 0.1 collective-permute-start
  17.2 4.4 %collective-permute-done = f32[64,256]{1,0:T(8,128)S(1)} collective-permute-done((f32[64,256]{1,0:T(8,128)S(1)}, f32[64,256]{1,0:T(8,128)S(1)}, u32[]{:S(2)}, u32[]{:S(2)}) %collective-permute-start) | collective-permute-done | bytes 65568 | tf_op jit(solution)/shard_map/ppermute | solution.py:362
  21.6 2.1 %collective-permute-start.1 = (f32[64,256]{1,0:T(8,128)S(1)}, f32[64,256]{1,0:T(8,128)S(1)}, u32[]{:S(2)}, u32[]{:S(2)}) collective-permute-start(f32[64,256]{1,0:T(8,128)S(1)} %add.9), channel_id=1, source_target_pairs={{0,8},{4,20},{8,0},{12,28},{16,24},{20,4},{24,16},{28,12},{1,9},{5... | collective-permute-start | bytes 196616 | tf_op jit(solution)/shard_map/ppermute | solution.py:362
  23.7 1.6 %collective-permute-start.11 = (f32[256,256]{1,0:T(8,128)S(1)}, f32[256,256]{1,0:T(8,128)S(1)}, u32[]{:S(2)}, u32[]{:S(2)}) collective-permute-start(f32[256,256]{1,0:T(8,128)S(1)} %get-tuple-element.35), channel_id=1, source_target_pairs={{0,1},{1,0},{2,3},{3,2},{4,5},{5,4},{6,7},{7,6},{8,9},{9,8},{10,11... | collective-permute-start | bytes 786440 | tf_op jit(solution)/shard_map/ppermute | solution.py:362
  25.2 0.0 collective-permute-done.9.relayed.first
  25.3 2.5 %collective-permute-start.10 = (f32[256,256]{1,0:T(8,128)S(1)}, f32[256,256]{1,0:T(8,128)S(1)}, u32[]{:S(2)}, u32[]{:S(2)}) collective-permute-start(f32[256,256]{1,0:T(8,128)S(1)} %shard_map.76), channel_id=1, source_target_pairs={{0,3},{1,2},{2,1},{3,0},{4,7},{5,6},{6,5},{7,4},{8,11},{9,10},{10,... | collective-permute-start | bytes 786440 | tf_op jit(solution)/shard_map/ppermute | solution.py:362
  27.8 0.0 collective-permute-done.1
  27.8 0.1 collective-permute-start.2
  27.9 1.2 %collective-permute-done.2.b_ref.left_b = f32[64,256]{1,0:T(8,128)S(1)} collective-permute-done((f32[64,256]{1,0:T(8,128)S(1)}, f32[64,256]{1,0:T(8,128)S(1)}, u32[]{:S(2)}, u32[]{:S(2)}) %collective-permute-start.2) | collective-permute-done | bytes 65568 | tf_op jit(solution)/shard_map/ppermute | solution.py:362
  29.2 0.0 collective-permute-done.5.total_b
  29.2 0.2 right.1.right_a
  29.4 0.0 copy-start
  29.4 0.6 %collective-permute-start.7 = (f32[64,256]{1,0:T(8,128)S(1)}, f32[64,256]{1,0:T(8,128)S(1)}, u32[]{:S(2)}, u32[]{:S(2)}) collective-permute-start(f32[64,256]{1,0:T(8,128)S(1)} %right.1.right_a), channel_id=1, source_target_pairs={{0,8},{4,20},{8,0},{12,28},{16,24},{20,4},{24,16},{28,12},{1,9},{5... | collective-permute-start | bytes 196616 | tf_op jit(solution)/shard_map/ppermute | solution.py:362
  30.0 0.9 %collective-permute-start.6 = (f32[64,256]{1,0:T(8,128)S(1)}, f32[64,256]{1,0:T(8,128)S(1)}, u32[]{:S(2)}, u32[]{:S(2)}) collective-permute-start(f32[64,256]{1,0:T(8,128)S(1)} %right.1.right_a), channel_id=1, source_target_pairs={{0,4},{4,0},{8,12},{12,8},{16,20},{20,16},{24,28},{28,24},{1,5},{5... | collective-permute-start | bytes 196616 | tf_op jit(solution)/shard_map/ppermute | solution.py:362
  30.8 2.9 %collective-permute-done.7.right_b = f32[64,256]{1,0:T(8,128)S(1)} collective-permute-done((f32[64,256]{1,0:T(8,128)S(1)}, f32[64,256]{1,0:T(8,128)S(1)}, u32[]{:S(2)}, u32[]{:S(2)}) %collective-permute-start.7) | collective-permute-done | bytes 65568 | tf_op jit(solution)/shard_map/ppermute | solution.py:362
  33.7 0.0 collective-permute-start.8
  33.7 3.5 %solve.1.basis = f32[64,256]{1,0:T(8,128)S(1)} custom-call(f32[64,256]{1,0:T(8,128)S(1)} %add.10.a_ref.left_a, f32[64,256]{1,0:T(8,128)S(1)} %collective-permute-done.2.b_ref.left_b), custom_call_target="tpu_custom_call" | custom-call | flops 1073741824 | bytes 1048576 | tf_op jit(solution)/shard_map/solve/pallas_call | solution.py:259
  37.2 0.0 collective-permute-done.11.rest_1_
  37.2 0.6 %collective-permute-done.10.rest_0_ = f32[256,256]{1,0:T(8,128)S(1)} collective-permute-done((f32[256,256]{1,0:T(8,128)S(1)}, f32[256,256]{1,0:T(8,128)S(1)}, u32[]{:S(2)}, u32[]{:S(2)}) %collective-permute-start.10) | collective-permute-done | bytes 262176 | tf_op jit(solution)/shard_map/ppermute | solution.py:362
  37.8 0.8 %shard_map.77 = f32[256,256]{1,0:T(8,128)} custom-call(f32[256,256]{1,0:T(8,128)S(1)} %collective-permute-done.9.relayed.first, f32[256,256]{1,0:T(8,128)S(1)} %collective-permute-done.10.rest_0_, f32[256,256]{1,0:T(8,128)S(1)} %collective-permute-done.11.rest_1_, f32[256,256]{1,0:T(8,128)S(1)} %get-tuple-element.36.rest_2_), custom_call_target="tpu_custom_call" | custom-call | tf_op jit(solution)/shard_map/pallas_call | solution.py:190
  38.6 0.0 copy-done
  38.6 1.4 %back_near.1 = (f32[256,1024]{1,0:T(8,128)}, f32[1,256,1024]{2,1,0:T(8,128)}) custom-call(f32[64,256]{1,0:T(8,128)S(1)} %solve.1.basis, f32[64,256]{1,0:T(8,128)S(1)} %right.1.right_a, f32[64,256]{1,0:T(8,128)S(1)} %collective-permute-done.7.right_b, f32[256,512]{1,0:T(8,128)S(1)} %get-tuple-element.26.mine.merged, f32[256,1024]{1,0:T(8,128)S(1)} %copy-done), custom_call_target="tpu_custom_call" | custom-call | tf_op jit(solution)/shard_map/back_near/pallas_call | solution.py:342
  40.0 0.0 collective-permute-done.6.right_a
  40.0 0.0 collective-permute-done.8.right_b
  40.0 1.4 %back_far.1 = (f32[256,1024]{1,0:T(8,128)}, f32[1,256,1024]{2,1,0:T(8,128)}) custom-call(f32[64,256]{1,0:T(8,128)S(1)} %solve.1.basis, f32[64,256]{1,0:T(8,128)S(1)} %collective-permute-done.6.right_a, f32[64,256]{1,0:T(8,128)S(1)} %collective-permute-done.8.right_b, ...), custom_call_target="tpu_custom_call", output_to_operand_aliasing={{0}: (5, {}), {1}: (6, {})} | custom-call | tf_op jit(solution)/shard_map/back_far/pallas_call | solution.py:342
  (4 shorter events, 0.1 us)
Async XLA Ops:
  0.6 3.6 %copy-start.1 = (f32[1,256,1024]{2,1,0:T(8,128)S(1)}, f32[1,256,1024]{2,1,0:T(8,128)}, u32[]{:S(2)}) copy-start(f32[1,256,1024]{2,1,0:T(8,128)} %err.1) | copy-start | bytes 3145732
  4.2 12.3 %copy-start.2 = (f32[1024,64]{0,1:T(8,128)S(1)}, f32[1024,64]{0,1:T(8,128)}, u32[]{:S(2)}) copy-start(f32[1024,64]{0,1:T(8,128)} %param.9) | copy-start | bytes 786436
  5.0 2.1 %collective-permute-start.3 = (f32[256,512]{1,0:T(8,128)S(1)}, f32[256,512]{1,0:T(8,128)S(1)}, u32[]{:S(2)}, u32[]{:S(2)}) collective-permute-start(f32[256,512]{1,0:T(8,128)S(1)} %get-tuple-element.25.theirs.merged), channel_id=1, source_target_pairs={{0,4},{4,0},{8,12},{12,8},{16,20},{20,16},{24,28},{28,24},{1,5},{5... | collective-permute-start | bytes 1572872 | tf_op jit(solution)/shard_map/ppermute | solution.py:362
  7.1 7.3 %collective-permute-start.4 = (f32[256,256]{1,0:T(8,128)S(1)}, f32[256,256]{1,0:T(8,128)S(1)}, u32[]{:S(2)}, u32[]{:S(2)}) collective-permute-start(f32[256,256]{1,0:T(8,128)S(1)} %get-tuple-element.28), channel_id=1, source_target_pairs={{0,8},{4,20},{8,0},{12,28},{16,24},{20,4},{24,16},{28,12},{1,9},{5... | collective-permute-start | bytes 786440 | tf_op jit(solution)/shard_map/ppermute | solution.py:362
  10.0 15.2 %collective-permute-start.9 = (f32[256,256]{1,0:T(8,128)S(1)}, f32[256,256]{1,0:T(8,128)S(1)}, u32[]{:S(2)}, u32[]{:S(2)}) collective-permute-start(f32[256,256]{1,0:T(8,128)S(1)} %get-tuple-element.33), channel_id=1, source_target_pairs={{0,1},{1,3},{2,0},{3,2},{4,5},{5,7},{6,4},{7,6},{8,9},{9,11},{10,8... | collective-permute-start | bytes 786440 | tf_op jit(solution)/shard_map/ppermute | solution.py:362
  14.4 14.7 %collective-permute-start.5 = (f32[256,256]{1,0:T(8,128)S(1)}, f32[256,256]{1,0:T(8,128)S(1)}, u32[]{:S(2)}, u32[]{:S(2)}) collective-permute-start(f32[256,256]{1,0:T(8,128)S(1)} %add.11.total_a), channel_id=1, source_target_pairs={{0,16},{4,12},{8,24},{12,4},{16,0},{20,28},{24,8},{28,20},{1,17},{... | collective-permute-start | bytes 786440 | tf_op jit(solution)/shard_map/ppermute | solution.py:362
  17.1 4.5 %collective-permute-start = (f32[64,256]{1,0:T(8,128)S(1)}, f32[64,256]{1,0:T(8,128)S(1)}, u32[]{:S(2)}, u32[]{:S(2)}) collective-permute-start(f32[64,256]{1,0:T(8,128)S(1)} %left.1), channel_id=1, source_target_pairs={{0,16},{4,12},{8,24},{12,4},{16,0},{20,28},{24,8},{28,20},{1,17},{... | collective-permute-start | bytes 196616 | tf_op jit(solution)/shard_map/ppermute | solution.py:362
  21.6 6.2 %collective-permute-start.1 = (f32[64,256]{1,0:T(8,128)S(1)}, f32[64,256]{1,0:T(8,128)S(1)}, u32[]{:S(2)}, u32[]{:S(2)}) collective-permute-start(f32[64,256]{1,0:T(8,128)S(1)} %add.9), channel_id=1, source_target_pairs={{0,8},{4,20},{8,0},{12,28},{16,24},{20,4},{24,16},{28,12},{1,9},{5... | collective-permute-start | bytes 196616 | tf_op jit(solution)/shard_map/ppermute | solution.py:362
  23.7 13.5 %collective-permute-start.11 = (f32[256,256]{1,0:T(8,128)S(1)}, f32[256,256]{1,0:T(8,128)S(1)}, u32[]{:S(2)}, u32[]{:S(2)}) collective-permute-start(f32[256,256]{1,0:T(8,128)S(1)} %get-tuple-element.35), channel_id=1, source_target_pairs={{0,1},{1,0},{2,3},{3,2},{4,5},{5,4},{6,7},{7,6},{8,9},{9,8},{10,11... | collective-permute-start | bytes 786440 | tf_op jit(solution)/shard_map/ppermute | solution.py:362
  25.3 12.5 %collective-permute-start.10 = (f32[256,256]{1,0:T(8,128)S(1)}, f32[256,256]{1,0:T(8,128)S(1)}, u32[]{:S(2)}, u32[]{:S(2)}) collective-permute-start(f32[256,256]{1,0:T(8,128)S(1)} %shard_map.76), channel_id=1, source_target_pairs={{0,3},{1,2},{2,1},{3,0},{4,7},{5,6},{6,5},{7,4},{8,11},{9,10},{10,... | collective-permute-start | bytes 786440 | tf_op jit(solution)/shard_map/ppermute | solution.py:362
  27.8 1.3 %collective-permute-start.2 = (f32[64,256]{1,0:T(8,128)S(1)}, f32[64,256]{1,0:T(8,128)S(1)}, u32[]{:S(2)}, u32[]{:S(2)}) collective-permute-start(f32[64,256]{1,0:T(8,128)S(1)} %add.10.a_ref.left_a), channel_id=1, source_target_pairs={{0,4},{4,0},{8,12},{12,8},{16,20},{20,16},{24,28},{28,24},{1,5},{5... | collective-permute-start | bytes 196616 | tf_op jit(solution)/shard_map/ppermute | solution.py:362
  29.4 9.2 %copy-start = (f32[256,1024]{1,0:T(8,128)S(1)}, f32[256,1024]{1,0:T(8,128)}, u32[]{:S(2)}) copy-start(f32[256,1024]{1,0:T(8,128)} %wt.5) | copy-start | bytes 3145732
  29.4 4.3 %collective-permute-start.7 = (f32[64,256]{1,0:T(8,128)S(1)}, f32[64,256]{1,0:T(8,128)S(1)}, u32[]{:S(2)}, u32[]{:S(2)}) collective-permute-start(f32[64,256]{1,0:T(8,128)S(1)} %right.1.right_a), channel_id=1, source_target_pairs={{0,8},{4,20},{8,0},{12,28},{16,24},{20,4},{24,16},{28,12},{1,9},{5... | collective-permute-start | bytes 196616 | tf_op jit(solution)/shard_map/ppermute | solution.py:362
  30.0 10.0 %collective-permute-start.6 = (f32[64,256]{1,0:T(8,128)S(1)}, f32[64,256]{1,0:T(8,128)S(1)}, u32[]{:S(2)}, u32[]{:S(2)}) collective-permute-start(f32[64,256]{1,0:T(8,128)S(1)} %right.1.right_a), channel_id=1, source_target_pairs={{0,4},{4,0},{8,12},{12,8},{16,20},{20,16},{24,28},{28,24},{1,5},{5... | collective-permute-start | bytes 196616 | tf_op jit(solution)/shard_map/ppermute | solution.py:362
  33.7 6.3 %collective-permute-start.8 = (f32[64,256]{1,0:T(8,128)S(1)}, f32[64,256]{1,0:T(8,128)S(1)}, u32[]{:S(2)}, u32[]{:S(2)}) collective-permute-start(f32[64,256]{1,0:T(8,128)S(1)} %collective-permute-done.7.right_b), channel_id=1, source_target_pairs={{0,4},{4,0},{8,12},{12,8},{16,20},{20,16},{24,28},{28,24},{1,5},{5... | collective-permute-start | bytes 196616 | tf_op jit(solution)/shard_map/ppermute | solution.py:362

commit v2 on v1

--- a/solution.py
+++ b/solution.py
@@ -311,20 +311,23 @@
     )(left, left_came, total, came)
 
 
-def back_kernel(near, bits, basis, right_a, right_b, merged, wt, *rest):
+def back_kernel(pieces, bits, basis, wt, *rest):
+    count = len(pieces)
+    rights, merged = rest[:count], rest[count : 2 * count]
     new_w, new_e, wv, ev, sems = rest[-5:]
-    width = right_a.shape[1]
+    width = rights[0].shape[1]
     index = lax.axis_index("dp")
-    side = lax.rem(index, 2)
-    side = side if near else 1 - side
-    own = quarter(bits, side, index)
     flipped = basis[...].T
     copies = []
-    for c, (right, which) in enumerate(((right_a, own), (right_b, 1 - own))):
+    for c, (near, same) in enumerate(pieces):
+        side = lax.rem(index, 2)
+        side = side if near else 1 - side
+        own = quarter(bits, side, index)
+        which = own if same else 1 - own
         here = pl.ds(pl.multiple_of(which * width, width), width)
         span = pl.ds(pl.multiple_of((2 * side + which) * width, width), width)
-        delta = dot3(flipped, right[...], NN)
-        ev[c] = merged[:, here] - delta
+        delta = dot3(flipped, rights[c][...], NN)
+        ev[c] = merged[c][:, here] - delta
         wv[c] = wt[:, span] - delta
         for one in (
             pltpu.make_async_copy(ev.at[c], new_e.at[0, :, span], sems.at[2 * c]),
@@ -336,26 +339,27 @@
         one.wait()
 
 
-def back(near, bits, basis, right_a, right_b, merged, wt, *kept):
+def back(pieces, bits, basis, wt, rights, merged, *kept):
     din, cols = wt.shape
-    width = right_a.shape[1]
-    return pl.pallas_call(
-        functools.partial(back_kernel, near, bits),
+    count = len(pieces)
+    width = rights[0].shape[1]
+    first = 2 + 2 * count
+    return pl.pallas_call(
+        functools.partial(back_kernel, pieces, bits),
         out_shape=[
             jax.ShapeDtypeStruct((din, cols), F32),
             jax.ShapeDtypeStruct((1, din, cols), F32),
         ],
-        in_specs=[VMEM] * 5 + [ANY] * len(kept),
+        in_specs=[VMEM] * first + [ANY] * len(kept),
         out_specs=[ANY] * 2,
-        input_output_aliases={5 + n: n for n in range(len(kept))},
+        input_output_aliases={first + n: n for n in range(len(kept))},
         scratch_shapes=[
-            pltpu.VMEM((2, din, width), F32),
-            pltpu.VMEM((2, din, width), F32),
-            pltpu.SemaphoreType.DMA((4,)),
+            pltpu.VMEM((count, din, width), F32),
+            pltpu.VMEM((count, din, width), F32),
+            pltpu.SemaphoreType.DMA((2 * count,)),
         ],
         compiler_params=pltpu.CompilerParams(vmem_limit_bytes=16 << 20),
-        name="back_near" if near else "back_far",
-    )(basis, right_a, right_b, merged, wt, *kept)
+    )(basis, wt, *rights, *merged, *kept)
 
 
 def send(x, axis, pairs):
@@ -396,14 +400,16 @@
     gather = functools.partial(gather_kernel, n_tensor if relays else None)
     input_grad = summed(gather, *received, blocks[0])
 
+    basis = solve(left, left_came, replicas)
     right = right_of(left, left_came, total, came, replicas)
     beside = send(right, "dp", swap(bits[0], bits[-1], replicas))
+    diagonal = send(right, "dp", swap(bits[0] | 1, bits[-1] | 1, replicas))
     across_pair = send(right, "dp", pair)
-    basis = solve(left, left_came, replicas)
-    beside_across = send(beside, "dp", pair)
-    kept = back(True, bits, basis, right, beside, mine, weight)
+    pieces = ((True, True), (True, False), (False, True))
+    rights = (right, beside, across_pair)
+    kept = back(pieces, bits, basis, weight, rights, (mine, mine, theirs))
     new_weight, new_error = back(
-        False, bits, basis, across_pair, beside_across, theirs, weight, *kept
+        ((False, False),), bits, basis, weight, (diagonal,), (theirs,), *kept
     )
     return (new_weight, new_error, input_grad)
 

time: 41.6 us -> 38 us (0.913)
  waiting for transfers between devices: 13.4 us -> 8.35 us
  starting transfers between devices: 15 us -> 16.6 us
    ppermute x12, waiting for transfers between devices: 13.4 us -> 8.35 us  [send(): return lax.ppermute(x, axis, pairs)]
    ppermute x12, starting transfers between devices: 15 us -> 16.6 us  [send(): return lax.ppermute(x, axis, pairs)]
  transfers between devices with their start and end apart: 12 -> 12, of which waited for: 6 -> 4; matrix products, arithmetic and copies ran while one was open for 0% -> 0% of each run, Pallas kernels for 16% -> 17%
where the time goes in v2:
time: 38 us; the launch traced here: 37.9 us
  starting transfers between devices  16.6 us (44%)
  Pallas kernels  12.1 us (32%)
  waiting for transfers between devices  8.35 us (22%)
  between operations  0.76 us (2%)
    ppermute x12, starting transfers between devices, send(): return lax.ppermute(x, axis, pairs)  16.6 us
    ppermute x12, waiting for transfers between devices, send(): return lax.ppermute(x, axis, pairs)  8.35 us
    pallas_call x1, Pallas kernels, blocks_of(): pl.pallas_call(functools.partial(blocks_kernel, [{}, *rounds], n, chunks)...  3.55 us
    pallas_call x1, Pallas kernels, solve(): pl.pallas_call(functools.partial(solve_kernel, replicas), out_shape=jax.S...  3.49 us
    pallas_call x2, Pallas kernels, back(): pl.pallas_call(functools.partial(back_kernel, pieces, bits), out_shape=[j...  2.67 us
    pallas_call x2, Pallas kernels, summed(): pl.pallas_call(kernel, out_shape=jax.ShapeDtypeStruct(parts[0].shape, F32...  0.8 us
  transfers between devices with their start and end apart: 12, of which 4 were waited for; matrix products, arithmetic and copies ran while one was open for 0% of the time, Pallas kernels for 17%

profile of v2, /device:TPU:0, one launch (start us, length us, event | category | flops | bytes accessed | tf_op | source)
XLA Modules:
  0.0 37.9 jit_solution(10135214077309019054)
XLA Ops:
  0.6 0.0 copy-start.1
  0.6 3.5 %blocks.1 = (bf16[256,1024]{1,0:T(8,128)(2,1)S(1)}, bf16[256,1024]{1,0:T(8,128)(2,1)S(1)}, bf16[256,1024]{1,0:T(8,128)(2,1)S(1)}, bf16[256,1024]{1,0:T(8,128)(2,...) custom-call(bf16[1024,256]{1,0:T(8,128)(2,1)} %acts.1, ...), custom_call_target="tpu_custom_call" | custom-call | flops 1073741824 | bytes 4194304 | tf_op jit(solution)/shard_map/blocks/pallas_call | solution.py:121
  4.2 0.0 copy-done.1
  4.2 0.0 copy-start.2
  4.2 0.7 %merged.1 = (f32[256,512]{1,0:T(8,128)S(1)}, f32[256,512]{1,0:T(8,128)S(1)}) custom-call(bf16[256,1024]{1,0:T(8,128)(2,1)S(1)} %get-tuple-element.20.acts_t, f32[1,256,1024]{2,1,0:T(8,128)S(1)} %copy-done.1, bf16[256,1024]{1,0:T(8,128)(2,1)S(1)} %get-tuple-element.21.rest_0_, bf16[256,1024]{1,0:T(8,128)(2,1)S(1)} %get-tuple-element.22.rest_1_, ...), custom_call_target="tpu_custom_call" | custom-call | flops 536870912 | bytes 4194304 | tf_op jit(solution)/shard_map/merged/pallas_call | solution.py:158
  5.0 0.6 %collective-permute-start.3 = (f32[256,512]{1,0:T(8,128)S(1)}, f32[256,512]{1,0:T(8,128)S(1)}, u32[]{:S(2)}, u32[]{:S(2)}) collective-permute-start(f32[256,512]{1,0:T(8,128)S(1)} %get-tuple-element.25.theirs.rest_5_.rest_1_), channel_id=1, source_target_pairs={{0,4},{4,0},{8,12},{12,8},{16,20},{20,16},{24,28},{28,24},{1,5},{5... | collective-permute-start | bytes 1572872 | tf_op jit(solution)/shard_map/ppermute | solution.py:366
  5.5 1.5 %collective-permute-done.3.came = f32[256,512]{1,0:T(8,128)S(1)} collective-permute-done((f32[256,512]{1,0:T(8,128)S(1)}, f32[256,512]{1,0:T(8,128)S(1)}, u32[]{:S(2)}, u32[]{:S(2)}) %collective-permute-start.3) | collective-permute-done | bytes 524320 | tf_op jit(solution)/shard_map/ppermute | solution.py:366
  7.1 0.1 begin.1
  7.1 2.9 %collective-permute-start.4 = (f32[256,256]{1,0:T(8,128)S(1)}, f32[256,256]{1,0:T(8,128)S(1)}, u32[]{:S(2)}, u32[]{:S(2)}) collective-permute-start(f32[256,256]{1,0:T(8,128)S(1)} %get-tuple-element.28), channel_id=1, source_target_pairs={{0,8},{4,20},{8,0},{12,28},{16,24},{20,4},{24,16},{28,12},{1,9},{5... | collective-permute-start | bytes 786440 | tf_op jit(solution)/shard_map/ppermute | solution.py:366
  10.0 1.6 %collective-permute-start.9 = (f32[256,256]{1,0:T(8,128)S(1)}, f32[256,256]{1,0:T(8,128)S(1)}, u32[]{:S(2)}, u32[]{:S(2)}) collective-permute-start(f32[256,256]{1,0:T(8,128)S(1)} %get-tuple-element.33), channel_id=1, source_target_pairs={{0,1},{1,3},{2,0},{3,2},{4,5},{5,7},{6,4},{7,6},{8,9},{9,11},{10,8... | collective-permute-start | bytes 786440 | tf_op jit(solution)/shard_map/ppermute | solution.py:366
  11.6 2.8 %collective-permute-done.4 = f32[256,256]{1,0:T(8,128)S(1)} collective-permute-done((f32[256,256]{1,0:T(8,128)S(1)}, f32[256,256]{1,0:T(8,128)S(1)}, u32[]{:S(2)}, u32[]{:S(2)}) %collective-permute-start.4) | collective-permute-done | bytes 262176 | tf_op jit(solution)/shard_map/ppermute | solution.py:366
  14.4 2.1 %collective-permute-start.5 = (f32[256,256]{1,0:T(8,128)S(1)}, f32[256,256]{1,0:T(8,128)S(1)}, u32[]{:S(2)}, u32[]{:S(2)}) collective-permute-start(f32[256,256]{1,0:T(8,128)S(1)} %add.11.total_a), channel_id=1, source_target_pairs={{0,16},{4,12},{8,24},{12,4},{16,0},{20,28},{24,8},{28,20},{1,17},{... | collective-permute-start | bytes 786440 | tf_op jit(solution)/shard_map/ppermute | solution.py:366
  16.5 0.0 copy-done.2
  16.5 0.6 %left.1 = f32[64,256]{1,0:T(8,128)S(1)} custom-call(f32[64,1024]{1,0:T(8,128)S(1)} %bitcast.1, f32[256,512]{1,0:T(8,128)S(1)} %get-tuple-element.25.theirs.rest_5_.rest_1_, f32[256,512]{1,0:T(8,128)S(1)} %get-tuple-element.26.mine.rest_3_.rest_4_), custom_call_target="tpu_custom_call" | custom-call | tf_op jit(solution)/shard_map/left/pallas_call | solution.py:208
  17.1 0.1 collective-permute-start
  17.2 2.1 %collective-permute-start.11 = (f32[256,256]{1,0:T(8,128)S(1)}, f32[256,256]{1,0:T(8,128)S(1)}, u32[]{:S(2)}, u32[]{:S(2)}) collective-permute-start(f32[256,256]{1,0:T(8,128)S(1)} %get-tuple-element.35), channel_id=1, source_target_pairs={{0,1},{1,0},{2,3},{3,2},{4,5},{5,4},{6,7},{7,6},{8,9},{9,8},{10,11... | collective-permute-start | bytes 786440 | tf_op jit(solution)/shard_map/ppermute | solution.py:366
  19.3 0.0 collective-permute-done.9.relayed.first
  19.3 3.4 %collective-permute-start.10 = (f32[256,256]{1,0:T(8,128)S(1)}, f32[256,256]{1,0:T(8,128)S(1)}, u32[]{:S(2)}, u32[]{:S(2)}) collective-permute-start(f32[256,256]{1,0:T(8,128)S(1)} %shard_map.78), channel_id=1, source_target_pairs={{0,3},{1,2},{2,1},{3,0},{4,7},{5,6},{6,5},{7,4},{8,11},{9,10},{10,... | collective-permute-start | bytes 786440 | tf_op jit(solution)/shard_map/ppermute | solution.py:366
  22.7 0.0 collective-permute-done
  22.8 1.6 %collective-permute-start.1 = (f32[64,256]{1,0:T(8,128)S(1)}, f32[64,256]{1,0:T(8,128)S(1)}, u32[]{:S(2)}, u32[]{:S(2)}) collective-permute-start(f32[64,256]{1,0:T(8,128)S(1)} %add.9), channel_id=1, source_target_pairs={{0,8},{4,20},{8,0},{12,28},{16,24},{20,4},{24,16},{28,12},{1,9},{5... | collective-permute-start | bytes 196616 | tf_op jit(solution)/shard_map/ppermute | solution.py:366
  24.3 2.8 %collective-permute-done.1 = f32[64,256]{1,0:T(8,128)S(1)} collective-permute-done((f32[64,256]{1,0:T(8,128)S(1)}, f32[64,256]{1,0:T(8,128)S(1)}, u32[]{:S(2)}, u32[]{:S(2)}) %collective-permute-start.1) | collective-permute-done | bytes 65568 | tf_op jit(solution)/shard_map/ppermute | solution.py:366
  27.1 0.1 collective-permute-start.2
  27.2 1.2 %collective-permute-done.2.b_ref.left_b = f32[64,256]{1,0:T(8,128)S(1)} collective-permute-done((f32[64,256]{1,0:T(8,128)S(1)}, f32[64,256]{1,0:T(8,128)S(1)}, u32[]{:S(2)}, u32[]{:S(2)}) %collective-permute-start.2) | collective-permute-done | bytes 65568 | tf_op jit(solution)/shard_map/ppermute | solution.py:366
  28.4 0.0 collective-permute-done.5.total_b
  28.4 0.2 right.1.rest_0_
  28.6 0.0 copy-start
  28.6 0.2 collective-permute-start.8
  28.9 1.5 %collective-permute-start.7 = (f32[64,256]{1,0:T(8,128)S(1)}, f32[64,256]{1,0:T(8,128)S(1)}, u32[]{:S(2)}, u32[]{:S(2)}) collective-permute-start(f32[64,256]{1,0:T(8,128)S(1)} %right.1.rest_0_), channel_id=1, source_target_pairs={{0,8},{4,20},{8,0},{12,28},{16,24},{20,4},{24,16},{28,12},{1,9},{5... | collective-permute-start | bytes 196616 | tf_op jit(solution)/shard_map/ppermute | solution.py:366
  30.3 0.6 %collective-permute-start.6 = (f32[64,256]{1,0:T(8,128)S(1)}, f32[64,256]{1,0:T(8,128)S(1)}, u32[]{:S(2)}, u32[]{:S(2)}) collective-permute-start(f32[64,256]{1,0:T(8,128)S(1)} %right.1.rest_0_), channel_id=1, source_target_pairs={{0,12},{4,16},{8,4},{12,24},{16,28},{20,0},{24,20},{28,8},{1,13},{... | collective-permute-start | bytes 196616 | tf_op jit(solution)/shard_map/ppermute | solution.py:366
  30.9 3.5 %solve.1.basis = f32[64,256]{1,0:T(8,128)S(1)} custom-call(f32[64,256]{1,0:T(8,128)S(1)} %add.10.a_ref.left_a, f32[64,256]{1,0:T(8,128)S(1)} %collective-permute-done.2.b_ref.left_b), custom_call_target="tpu_custom_call" | custom-call | flops 1073741824 | bytes 1048576 | tf_op jit(solution)/shard_map/solve/pallas_call | solution.py:259
  34.4 0.0 collective-permute-done.11.rest_1_
  34.4 0.0 collective-permute-done.10.rest_0_
  34.4 0.8 %shard_map.79 = f32[256,256]{1,0:T(8,128)} custom-call(f32[256,256]{1,0:T(8,128)S(1)} %collective-permute-done.9.relayed.first, f32[256,256]{1,0:T(8,128)S(1)} %collective-permute-done.10.rest_0_, f32[256,256]{1,0:T(8,128)S(1)} %collective-permute-done.11.rest_1_, f32[256,256]{1,0:T(8,128)S(1)} %get-tuple-element.36.rest_2_), custom_call_target="tpu_custom_call" | custom-call | tf_op jit(solution)/shard_map/pallas_call | solution.py:190
  35.2 0.0 collective-permute-done.8.rest_2_
  35.2 0.0 collective-permute-done.7.rest_1_
  35.2 0.0 copy-done
  35.2 1.5 %shard_map.76 = (f32[256,1024]{1,0:T(8,128)}, f32[1,256,1024]{2,1,0:T(8,128)}) custom-call(f32[64,256]{1,0:T(8,128)S(1)} %solve.1.basis, f32[256,1024]{1,0:T(8,128)S(1)} %copy-done, f32[64,256]{1,0:T(8,128)S(1)} %right.1.rest_0_, f32[64,256]{1,0:T(8,128)S(1)} %collective-permute-done.7.rest_1_, f32[64,256]{1,0:T(8,128)S(1)} %collective-permute-done.8.rest_2_, ...), custom_call_target="tpu_custom_call" | custom-call | tf_op jit(solution)/shard_map/pallas_call | solution.py:347
  36.8 0.0 collective-permute-done.6.rest_0_
  36.8 1.1 %shard_map.77 = (f32[256,1024]{1,0:T(8,128)}, f32[1,256,1024]{2,1,0:T(8,128)}) custom-call(f32[64,256]{1,0:T(8,128)S(1)} %solve.1.basis, f32[256,1024]{1,0:T(8,128)S(1)} %copy-done, f32[64,256]{1,0:T(8,128)S(1)} %collective-permute-done.6.rest_0_, ...), custom_call_target="tpu_custom_call", output_to_operand_aliasing={{0}: (4, {}), {1}: (5, {})} | custom-call | tf_op jit(solution)/shard_map/pallas_call | solution.py:347
  (4 shorter events, 0.1 us)
Async XLA Ops:
  0.6 3.6 %copy-start.1 = (f32[1,256,1024]{2,1,0:T(8,128)S(1)}, f32[1,256,1024]{2,1,0:T(8,128)}, u32[]{:S(2)}) copy-start(f32[1,256,1024]{2,1,0:T(8,128)} %err.1) | copy-start | bytes 3145732
  4.2 12.3 %copy-start.2 = (f32[1024,64]{0,1:T(8,128)S(1)}, f32[1024,64]{0,1:T(8,128)}, u32[]{:S(2)}) copy-start(f32[1024,64]{0,1:T(8,128)} %param.9) | copy-start | bytes 786436
  5.0 2.1 %collective-permute-start.3 = (f32[256,512]{1,0:T(8,128)S(1)}, f32[256,512]{1,0:T(8,128)S(1)}, u32[]{:S(2)}, u32[]{:S(2)}) collective-permute-start(f32[256,512]{1,0:T(8,128)S(1)} %get-tuple-element.25.theirs.rest_5_.rest_1_), channel_id=1, source_target_pairs={{0,4},{4,0},{8,12},{12,8},{16,20},{20,16},{24,28},{28,24},{1,5},{5... | collective-permute-start | bytes 1572872 | tf_op jit(solution)/shard_map/ppermute | solution.py:366
  7.1 7.3 %collective-permute-start.4 = (f32[256,256]{1,0:T(8,128)S(1)}, f32[256,256]{1,0:T(8,128)S(1)}, u32[]{:S(2)}, u32[]{:S(2)}) collective-permute-start(f32[256,256]{1,0:T(8,128)S(1)} %get-tuple-element.28), channel_id=1, source_target_pairs={{0,8},{4,20},{8,0},{12,28},{16,24},{20,4},{24,16},{28,12},{1,9},{5... | collective-permute-start | bytes 786440 | tf_op jit(solution)/shard_map/ppermute | solution.py:366
  10.0 9.3 %collective-permute-start.9 = (f32[256,256]{1,0:T(8,128)S(1)}, f32[256,256]{1,0:T(8,128)S(1)}, u32[]{:S(2)}, u32[]{:S(2)}) collective-permute-start(f32[256,256]{1,0:T(8,128)S(1)} %get-tuple-element.33), channel_id=1, source_target_pairs={{0,1},{1,3},{2,0},{3,2},{4,5},{5,7},{6,4},{7,6},{8,9},{9,11},{10,8... | collective-permute-start | bytes 786440 | tf_op jit(solution)/shard_map/ppermute | solution.py:366
  14.4 14.0 %collective-permute-start.5 = (f32[256,256]{1,0:T(8,128)S(1)}, f32[256,256]{1,0:T(8,128)S(1)}, u32[]{:S(2)}, u32[]{:S(2)}) collective-permute-start(f32[256,256]{1,0:T(8,128)S(1)} %add.11.total_a), channel_id=1, source_target_pairs={{0,16},{4,12},{8,24},{12,4},{16,0},{20,28},{24,8},{28,20},{1,17},{... | collective-permute-start | bytes 786440 | tf_op jit(solution)/shard_map/ppermute | solution.py:366
  17.1 5.6 %collective-permute-start = (f32[64,256]{1,0:T(8,128)S(1)}, f32[64,256]{1,0:T(8,128)S(1)}, u32[]{:S(2)}, u32[]{:S(2)}) collective-permute-start(f32[64,256]{1,0:T(8,128)S(1)} %left.1), channel_id=1, source_target_pairs={{0,16},{4,12},{8,24},{12,4},{16,0},{20,28},{24,8},{28,20},{1,17},{... | collective-permute-start | bytes 196616 | tf_op jit(solution)/shard_map/ppermute | solution.py:366
  17.2 17.2 %collective-permute-start.11 = (f32[256,256]{1,0:T(8,128)S(1)}, f32[256,256]{1,0:T(8,128)S(1)}, u32[]{:S(2)}, u32[]{:S(2)}) collective-permute-start(f32[256,256]{1,0:T(8,128)S(1)} %get-tuple-element.35), channel_id=1, source_target_pairs={{0,1},{1,0},{2,3},{3,2},{4,5},{5,4},{6,7},{7,6},{8,9},{9,8},{10,11... | collective-permute-start | bytes 786440 | tf_op jit(solution)/shard_map/ppermute | solution.py:366
  19.3 15.1 %collective-permute-start.10 = (f32[256,256]{1,0:T(8,128)S(1)}, f32[256,256]{1,0:T(8,128)S(1)}, u32[]{:S(2)}, u32[]{:S(2)}) collective-permute-start(f32[256,256]{1,0:T(8,128)S(1)} %shard_map.78), channel_id=1, source_target_pairs={{0,3},{1,2},{2,1},{3,0},{4,7},{5,6},{6,5},{7,4},{8,11},{9,10},{10,... | collective-permute-start | bytes 786440 | tf_op jit(solution)/shard_map/ppermute | solution.py:366
  22.8 4.3 %collective-permute-start.1 = (f32[64,256]{1,0:T(8,128)S(1)}, f32[64,256]{1,0:T(8,128)S(1)}, u32[]{:S(2)}, u32[]{:S(2)}) collective-permute-start(f32[64,256]{1,0:T(8,128)S(1)} %add.9), channel_id=1, source_target_pairs={{0,8},{4,20},{8,0},{12,28},{16,24},{20,4},{24,16},{28,12},{1,9},{5... | collective-permute-start | bytes 196616 | tf_op jit(solution)/shard_map/ppermute | solution.py:366
  27.1 1.3 %collective-permute-start.2 = (f32[64,256]{1,0:T(8,128)S(1)}, f32[64,256]{1,0:T(8,128)S(1)}, u32[]{:S(2)}, u32[]{:S(2)}) collective-permute-start(f32[64,256]{1,0:T(8,128)S(1)} %add.10.a_ref.left_a), channel_id=1, source_target_pairs={{0,4},{4,0},{8,12},{12,8},{16,20},{20,16},{24,28},{28,24},{1,5},{5... | collective-permute-start | bytes 196616 | tf_op jit(solution)/shard_map/ppermute | solution.py:366
  28.6 6.6 %copy-start = (f32[256,1024]{1,0:T(8,128)S(1)}, f32[256,1024]{1,0:T(8,128)}, u32[]{:S(2)}) copy-start(f32[256,1024]{1,0:T(8,128)} %wt.5) | copy-start | bytes 3145732
  28.6 6.6 %collective-permute-start.8 = (f32[64,256]{1,0:T(8,128)S(1)}, f32[64,256]{1,0:T(8,128)S(1)}, u32[]{:S(2)}, u32[]{:S(2)}) collective-permute-start(f32[64,256]{1,0:T(8,128)S(1)} %right.1.rest_0_), channel_id=1, source_target_pairs={{0,4},{4,0},{8,12},{12,8},{16,20},{20,16},{24,28},{28,24},{1,5},{5... | collective-permute-start | bytes 196616 | tf_op jit(solution)/shard_map/ppermute | solution.py:366
  28.9 6.3 %collective-permute-start.7 = (f32[64,256]{1,0:T(8,128)S(1)}, f32[64,256]{1,0:T(8,128)S(1)}, u32[]{:S(2)}, u32[]{:S(2)}) collective-permute-start(f32[64,256]{1,0:T(8,128)S(1)} %right.1.rest_0_), channel_id=1, source_target_pairs={{0,8},{4,20},{8,0},{12,28},{16,24},{20,4},{24,16},{28,12},{1,9},{5... | collective-permute-start | bytes 196616 | tf_op jit(solution)/shard_map/ppermute | solution.py:366
  30.3 6.4 %collective-permute-start.6 = (f32[64,256]{1,0:T(8,128)S(1)}, f32[64,256]{1,0:T(8,128)S(1)}, u32[]{:S(2)}, u32[]{:S(2)}) collective-permute-start(f32[64,256]{1,0:T(8,128)S(1)} %right.1.rest_0_), channel_id=1, source_target_pairs={{0,12},{4,16},{8,4},{12,24},{16,28},{20,0},{24,20},{28,8},{1,13},{... | collective-permute-start | bytes 196616 | tf_op jit(solution)/shard_map/ppermute | solution.py:366

commit v3 on v2

--- a/solution.py
+++ b/solution.py
@@ -362,10 +362,6 @@
     )(basis, wt, *rights, *merged, *kept)
 
 
-def send(x, axis, pairs):
-    return lax.ppermute(x, axis, pairs)
-
-
 def step(acts, out_grad, weight, error, start_q):
     replicas = lax.axis_size("dp")
     n_tensor = lax.axis_size("tensor")
@@ -375,36 +371,42 @@
     table, relays = rounds_of(n_tensor)
     acts_t, rows, blocks = blocks_of(acts, out_grad, weight, table)
 
-    def across(block, n):
-        return send(block, "tensor", [(a, to) for a, (to, _) in sorted(table[n].items())])
+    def across(block, n, only=range(n_tensor)):
+        hops = [(a, to) for a, (to, _) in sorted(table[n].items()) if a in only]
+        return lax.ppermute(block, "tensor", hops)
 
     received = [across(blocks[1], 0)]
     theirs, mine = merged_of(acts_t, error, rows)
-    came = send(theirs, "dp", pair)
+    came = lax.ppermute(theirs, "dp", pair)
     left = left_of(start_q.T, theirs, mine)
     total, give = begin(mine, came, bits)
-    came = send(give, "dp", swap(bits[0], bits[-1], replicas))
-    left = left + send(left, "dp", swap(bits[-1], bits[0], replicas))
+    came = lax.ppermute(give, "dp", swap(bits[0], bits[-1], replicas))
+    left = left + lax.ppermute(left, "dp", swap(bits[-1], bits[0], replicas))
     for n, (one, other) in enumerate(zip(bits[1:], bits[-2::-1]), 2):
         total = total + came
-        came = send(total, "dp", swap(one, other, replicas))
-        left = left + send(left, "dp", swap(other, one, replicas))
-    left_came = send(left, "dp", pair)
+        came = lax.ppermute(total, "dp", swap(one, other, replicas))
+        left = left + lax.ppermute(left, "dp", swap(other, one, replicas))
+    left_came = lax.ppermute(left, "dp", pair)
 
     for n in range(1, n_tensor - 1):
         block = blocks[n + 1]
         if relays and n == 1:
+            between = (1, n_tensor - 2)
+            ends = [a for a in range(n_tensor) if a not in between]
+            received.append(across(block, n, ends))
             onward = functools.partial(onward_kernel, n_tensor)
             block = summed(onward, block, received[0])
-        received.append(across(block, n))
+            received.append(across(block, n, between))
+        else:
+            received.append(across(block, n))
     gather = functools.partial(gather_kernel, n_tensor if relays else None)
     input_grad = summed(gather, *received, blocks[0])
 
     basis = solve(left, left_came, replicas)
     right = right_of(left, left_came, total, came, replicas)
-    beside = send(right, "dp", swap(bits[0], bits[-1], replicas))
-    diagonal = send(right, "dp", swap(bits[0] | 1, bits[-1] | 1, replicas))
-    across_pair = send(right, "dp", pair)
+    beside = lax.ppermute(right, "dp", swap(bits[0], bits[-1], replicas))
+    diagonal = lax.ppermute(right, "dp", swap(bits[0] | 1, bits[-1] | 1, replicas))
+    across_pair = lax.ppermute(right, "dp", pair)
     pieces = ((True, True), (True, False), (False, True))
     rights = (right, beside, across_pair)
     kept = back(pieces, bits, basis, weight, rights, (mine, mine, theirs))

time: 38 us -> 40.4 us (1.063)
  starting transfers between devices: 16.6 us -> 18.9 us
    ppermute x12 -> x13, starting transfers between devices: 16.6 us -> 18.9 us  [the longest x4 8.2 us: across(): return lax.ppermute(block, 'tensor', hops)]
    ppermute x12 -> x13, waiting for transfers between devices: 8.35 us -> 8.35 us  [the longest x1 2.78 us: step(): came = lax.ppermute(give, 'dp', swap(bits[0], bits[-1], replicas))]
  transfers between devices with their start and end apart: 12 -> 13, of which waited for: 4 -> 4; matrix products, arithmetic and copies ran while one was open for 0% -> 0% of each run, Pallas kernels for 17% -> 17%
where the time goes in v3:
time: 40.4 us; the launch traced here: 40.2 us
  starting transfers between devices  18.9 us (47%)
  Pallas kernels  12.1 us (30%)
  waiting for transfers between devices  8.35 us (21%)
  between operations  0.8 us (2%)
    ppermute x4, starting transfers between devices, across(): return lax.ppermute(block, 'tensor', hops)  8.2 us
    pallas_call x1, Pallas kernels, blocks_of(): pl.pallas_call(functools.partial(blocks_kernel, [{}, *rounds], n, chunks)...  3.55 us
    pallas_call x1, Pallas kernels, solve(): pl.pallas_call(functools.partial(solve_kernel, replicas), out_shape=jax.S...  3.49 us
    ppermute x1, starting transfers between devices, step(): came = lax.ppermute(give, 'dp', swap(bits[0], bits[-1], replicas))  2.9 us
    ppermute x1, waiting for transfers between devices, step(): came = lax.ppermute(give, 'dp', swap(bits[0], bits[-1], replicas))  2.78 us
    ppermute x1, waiting for transfers between devices, step(): left = left + lax.ppermute(left, 'dp', swap(other, one, replicas))  2.77 us
    pallas_call x2, Pallas kernels, back(): pl.pallas_call(functools.partial(back_kernel, pieces, bits), out_shape=[j...  2.67 us
    ppermute x1, starting transfers between devices, step(): came = lax.ppermute(total, 'dp', swap(one, other, replicas))  2.11 us
  transfers between devices with their start and end apart: 13, of which 4 were waited for; matrix products, arithmetic and copies ran while one was open for 0% of the time, Pallas kernels for 17%

profile of v3, /device:TPU:0, one launch (start us, length us, event | category | flops | bytes accessed | tf_op | source)
XLA Modules:
  0.0 40.2 jit_solution(11167330460137124746)
XLA Ops:
  0.6 0.0 copy-start.1
  0.6 3.5 %blocks.1 = (bf16[256,1024]{1,0:T(8,128)(2,1)S(1)}, bf16[256,1024]{1,0:T(8,128)(2,1)S(1)}, bf16[256,1024]{1,0:T(8,128)(2,1)S(1)}, bf16[256,1024]{1,0:T(8,128)(2,...) custom-call(bf16[1024,256]{1,0:T(8,128)(2,1)} %acts.1, ...), custom_call_target="tpu_custom_call" | custom-call | flops 1073741824 | bytes 4194304 | tf_op jit(solution)/shard_map/blocks/pallas_call | solution.py:121
  4.2 0.0 copy-done.1
  4.2 0.0 copy-start.2
  4.2 0.7 %merged.1 = (f32[256,512]{1,0:T(8,128)S(1)}, f32[256,512]{1,0:T(8,128)S(1)}) custom-call(bf16[256,1024]{1,0:T(8,128)(2,1)S(1)} %get-tuple-element.20.acts_t, f32[1,256,1024]{2,1,0:T(8,128)S(1)} %copy-done.1, bf16[256,1024]{1,0:T(8,128)(2,1)S(1)} %get-tuple-element.21.rest_0_, bf16[256,1024]{1,0:T(8,128)(2,1)S(1)} %get-tuple-element.22.rest_1_, ...), custom_call_target="tpu_custom_call" | custom-call | flops 536870912 | bytes 4194304 | tf_op jit(solution)/shard_map/merged/pallas_call | solution.py:158
  5.0 0.6 %collective-permute-start.3 = (f32[256,512]{1,0:T(8,128)S(1)}, f32[256,512]{1,0:T(8,128)S(1)}, u32[]{:S(2)}, u32[]{:S(2)}) collective-permute-start(f32[256,512]{1,0:T(8,128)S(1)} %get-tuple-element.25.theirs.rest_5_.rest_1_), channel_id=1, source_target_pairs={{0,4},{4,0},{8,12},{12,8},{16,20},{20,16},{24,28},{28,24},{1,5},{5... | collective-permute-start | bytes 1572872 | tf_op jit(solution)/shard_map/ppermute | solution.py:380
  5.5 1.5 %collective-permute-done.3.came = f32[256,512]{1,0:T(8,128)S(1)} collective-permute-done((f32[256,512]{1,0:T(8,128)S(1)}, f32[256,512]{1,0:T(8,128)S(1)}, u32[]{:S(2)}, u32[]{:S(2)}) %collective-permute-start.3) | collective-permute-done | bytes 524320 | tf_op jit(solution)/shard_map/ppermute | solution.py:380
  7.1 0.1 begin.1
  7.1 2.9 %collective-permute-start.4 = (f32[256,256]{1,0:T(8,128)S(1)}, f32[256,256]{1,0:T(8,128)S(1)}, u32[]{:S(2)}, u32[]{:S(2)}) collective-permute-start(f32[256,256]{1,0:T(8,128)S(1)} %get-tuple-element.28), channel_id=1, source_target_pairs={{0,8},{4,20},{8,0},{12,28},{16,24},{20,4},{24,16},{28,12},{1,9},{5... | collective-permute-start | bytes 786440 | tf_op jit(solution)/shard_map/ppermute | solution.py:383
  10.0 1.6 %collective-permute-start.9 = (f32[256,256]{1,0:T(8,128)S(1)}, f32[256,256]{1,0:T(8,128)S(1)}, u32[]{:S(2)}, u32[]{:S(2)}) collective-permute-start(f32[256,256]{1,0:T(8,128)S(1)} %get-tuple-element.33), channel_id=1, source_target_pairs={{0,1},{1,3},{2,0},{3,2},{4,5},{5,7},{6,4},{7,6},{8,9},{9,11},{10,8... | collective-permute-start | bytes 786440 | tf_op jit(solution)/shard_map/ppermute | solution.py:376
  11.6 2.8 %collective-permute-done.4 = f32[256,256]{1,0:T(8,128)S(1)} collective-permute-done((f32[256,256]{1,0:T(8,128)S(1)}, f32[256,256]{1,0:T(8,128)S(1)}, u32[]{:S(2)}, u32[]{:S(2)}) %collective-permute-start.4) | collective-permute-done | bytes 262176 | tf_op jit(solution)/shard_map/ppermute | solution.py:383
  14.4 2.1 %collective-permute-start.5 = (f32[256,256]{1,0:T(8,128)S(1)}, f32[256,256]{1,0:T(8,128)S(1)}, u32[]{:S(2)}, u32[]{:S(2)}) collective-permute-start(f32[256,256]{1,0:T(8,128)S(1)} %add.11.total_a), channel_id=1, source_target_pairs={{0,16},{4,12},{8,24},{12,4},{16,0},{20,28},{24,8},{28,20},{1,17},{... | collective-permute-start | bytes 786440 | tf_op jit(solution)/shard_map/ppermute | solution.py:387
  16.5 1.6 %collective-permute-start.12 = (f32[256,256]{1,0:T(8,128)S(1)}, f32[256,256]{1,0:T(8,128)S(1)}, u32[]{:S(2)}, u32[]{:S(2)}) collective-permute-start(f32[256,256]{1,0:T(8,128)S(1)} %get-tuple-element.35), channel_id=1, source_target_pairs={{0,1},{1,0},{2,3},{3,2},{4,5},{5,4},{6,7},{7,6},{8,9},{9,8},{10,11... | collective-permute-start | bytes 786440 | tf_op jit(solution)/shard_map/ppermute | solution.py:376
  18.1 0.0 copy-done.2
  18.1 0.6 %left.1 = f32[64,256]{1,0:T(8,128)S(1)} custom-call(f32[64,1024]{1,0:T(8,128)S(1)} %bitcast.1, f32[256,512]{1,0:T(8,128)S(1)} %get-tuple-element.25.theirs.rest_5_.rest_1_, f32[256,512]{1,0:T(8,128)S(1)} %get-tuple-element.26.mine.rest_3_.rest_4_), custom_call_target="tpu_custom_call" | custom-call | tf_op jit(solution)/shard_map/left/pallas_call | solution.py:208
  18.7 0.6 %collective-permute-start = (f32[64,256]{1,0:T(8,128)S(1)}, f32[64,256]{1,0:T(8,128)S(1)}, u32[]{:S(2)}, u32[]{:S(2)}) collective-permute-start(f32[64,256]{1,0:T(8,128)S(1)} %left.1), channel_id=1, source_target_pairs={{0,16},{4,12},{8,24},{12,4},{16,0},{20,28},{24,8},{28,20},{1,17},{... | collective-permute-start | bytes 196616 | tf_op jit(solution)/shard_map/ppermute | solution.py:384
  19.3 4.4 %collective-permute-start.10 = (f32[256,256]{1,0:T(8,128)S(1)}, f32[256,256]{1,0:T(8,128)S(1)}, u32[]{:S(2)}, u32[]{:S(2)}) collective-permute-start(f32[256,256]{1,0:T(8,128)S(1)} %get-tuple-element.34.block), channel_id=1, source_target_pairs={{0,3},{3,0},{4,7},{7,4},{8,11},{11,8},{12,15},{15,12},{16,19},{19,... | collective-permute-start | bytes 786440 | tf_op jit(solution)/shard_map/ppermute | solution.py:376
  23.7 0.0 collective-permute-done.9.relayed.first
  23.7 0.7 %collective-permute-start.11 = (f32[256,256]{1,0:T(8,128)S(1)}, f32[256,256]{1,0:T(8,128)S(1)}, u32[]{:S(2)}, u32[]{:S(2)}) collective-permute-start(f32[256,256]{1,0:T(8,128)S(1)} %shard_map.78), channel_id=1, source_target_pairs={{1,2},{2,1},{5,6},{6,5},{9,10},{10,9},{13,14},{14,13},{17,18},{18,... | collective-permute-start | bytes 786440 | tf_op jit(solution)/shard_map/ppermute | solution.py:376
  24.4 0.0 collective-permute-done
  24.4 1.6 %collective-permute-start.1 = (f32[64,256]{1,0:T(8,128)S(1)}, f32[64,256]{1,0:T(8,128)S(1)}, u32[]{:S(2)}, u32[]{:S(2)}) collective-permute-start(f32[64,256]{1,0:T(8,128)S(1)} %add.9), channel_id=1, source_target_pairs={{0,8},{4,20},{8,0},{12,28},{16,24},{20,4},{24,16},{28,12},{1,9},{5... | collective-permute-start | bytes 196616 | tf_op jit(solution)/shard_map/ppermute | solution.py:388
  26.0 2.8 %collective-permute-done.1 = f32[64,256]{1,0:T(8,128)S(1)} collective-permute-done((f32[64,256]{1,0:T(8,128)S(1)}, f32[64,256]{1,0:T(8,128)S(1)}, u32[]{:S(2)}, u32[]{:S(2)}) %collective-permute-start.1) | collective-permute-done | bytes 65568 | tf_op jit(solution)/shard_map/ppermute | solution.py:388
  28.8 0.1 collective-permute-start.2
  28.9 1.2 %collective-permute-done.2.b_ref.left_b = f32[64,256]{1,0:T(8,128)S(1)} collective-permute-done((f32[64,256]{1,0:T(8,128)S(1)}, f32[64,256]{1,0:T(8,128)S(1)}, u32[]{:S(2)}, u32[]{:S(2)}) %collective-permute-start.2) | collective-permute-done | bytes 65568 | tf_op jit(solution)/shard_map/ppermute | solution.py:389
  30.1 0.0 collective-permute-done.5.total_b
  30.1 0.2 right.1.rest_0_
  30.3 0.0 copy-start
  30.3 0.2 collective-permute-start.8
  30.5 1.5 %collective-permute-start.7 = (f32[64,256]{1,0:T(8,128)S(1)}, f32[64,256]{1,0:T(8,128)S(1)}, u32[]{:S(2)}, u32[]{:S(2)}) collective-permute-start(f32[64,256]{1,0:T(8,128)S(1)} %right.1.rest_0_), channel_id=1, source_target_pairs={{0,8},{4,20},{8,0},{12,28},{16,24},{20,4},{24,16},{28,12},{1,9},{5... | collective-permute-start | bytes 196616 | tf_op jit(solution)/shard_map/ppermute | solution.py:407
  32.0 0.0 collective-permute-done.12.rest_2_
  32.0 1.2 %collective-permute-start.6 = (f32[64,256]{1,0:T(8,128)S(1)}, f32[64,256]{1,0:T(8,128)S(1)}, u32[]{:S(2)}, u32[]{:S(2)}) collective-permute-start(f32[64,256]{1,0:T(8,128)S(1)} %right.1.rest_0_), channel_id=1, source_target_pairs={{0,12},{4,16},{8,4},{12,24},{16,28},{20,0},{24,20},{28,8},{1,13},{... | collective-permute-start | bytes 196616 | tf_op jit(solution)/shard_map/ppermute | solution.py:408
  33.2 3.5 %solve.1.basis = f32[64,256]{1,0:T(8,128)S(1)} custom-call(f32[64,256]{1,0:T(8,128)S(1)} %add.10.a_ref.left_a, f32[64,256]{1,0:T(8,128)S(1)} %collective-permute-done.2.b_ref.left_b), custom_call_target="tpu_custom_call" | custom-call | flops 1073741824 | bytes 1048576 | tf_op jit(solution)/shard_map/solve/pallas_call | solution.py:259
  36.7 0.0 collective-permute-done.10.rest_0_
  36.7 0.0 collective-permute-done.11.rest_1_
  36.7 0.8 %shard_map.79 = f32[256,256]{1,0:T(8,128)} custom-call(f32[256,256]{1,0:T(8,128)S(1)} %collective-permute-done.9.relayed.first, f32[256,256]{1,0:T(8,128)S(1)} %collective-permute-done.10.rest_0_, f32[256,256]{1,0:T(8,128)S(1)} %collective-permute-done.11.rest_1_, f32[256,256]{1,0:T(8,128)S(1)} %collective-permute-done.12.rest_2_, ...), custom_call_target="tpu_custom_call" | custom-call | tf_op jit(solution)/shard_map/pallas_call | solution.py:190
  37.5 0.0 collective-permute-done.8.rest_2_
  37.5 0.0 collective-permute-done.7.rest_1_
  37.5 0.0 copy-done
  37.5 1.5 %shard_map.76 = (f32[256,1024]{1,0:T(8,128)}, f32[1,256,1024]{2,1,0:T(8,128)}) custom-call(f32[64,256]{1,0:T(8,128)S(1)} %solve.1.basis, f32[256,1024]{1,0:T(8,128)S(1)} %copy-done, f32[64,256]{1,0:T(8,128)S(1)} %right.1.rest_0_, f32[64,256]{1,0:T(8,128)S(1)} %collective-permute-done.7.rest_1_, f32[64,256]{1,0:T(8,128)S(1)} %collective-permute-done.8.rest_2_, ...), custom_call_target="tpu_custom_call" | custom-call | tf_op jit(solution)/shard_map/pallas_call | solution.py:347
  39.1 0.0 collective-permute-done.6.rest_0_
  39.1 1.1 %shard_map.77 = (f32[256,1024]{1,0:T(8,128)}, f32[1,256,1024]{2,1,0:T(8,128)}) custom-call(f32[64,256]{1,0:T(8,128)S(1)} %solve.1.basis, f32[256,1024]{1,0:T(8,128)S(1)} %copy-done, f32[64,256]{1,0:T(8,128)S(1)} %collective-permute-done.6.rest_0_, ...), custom_call_target="tpu_custom_call", output_to_operand_aliasing={{0}: (4, {}), {1}: (5, {})} | custom-call | tf_op jit(solution)/shard_map/pallas_call | solution.py:347
  (4 shorter events, 0.1 us)
Async XLA Ops:
  0.6 3.6 %copy-start.1 = (f32[1,256,1024]{2,1,0:T(8,128)S(1)}, f32[1,256,1024]{2,1,0:T(8,128)}, u32[]{:S(2)}) copy-start(f32[1,256,1024]{2,1,0:T(8,128)} %err.1) | copy-start | bytes 3145732
  4.2 13.9 %copy-start.2 = (f32[1024,64]{0,1:T(8,128)S(1)}, f32[1024,64]{0,1:T(8,128)}, u32[]{:S(2)}) copy-start(f32[1024,64]{0,1:T(8,128)} %param.9) | copy-start | bytes 786436
  5.0 2.1 %collective-permute-start.3 = (f32[256,512]{1,0:T(8,128)S(1)}, f32[256,512]{1,0:T(8,128)S(1)}, u32[]{:S(2)}, u32[]{:S(2)}) collective-permute-start(f32[256,512]{1,0:T(8,128)S(1)} %get-tuple-element.25.theirs.rest_5_.rest_1_), channel_id=1, source_target_pairs={{0,4},{4,0},{8,12},{12,8},{16,20},{20,16},{24,28},{28,24},{1,5},{5... | collective-permute-start | bytes 1572872 | tf_op jit(solution)/shard_map/ppermute | solution.py:380
  7.1 7.3 %collective-permute-start.4 = (f32[256,256]{1,0:T(8,128)S(1)}, f32[256,256]{1,0:T(8,128)S(1)}, u32[]{:S(2)}, u32[]{:S(2)}) collective-permute-start(f32[256,256]{1,0:T(8,128)S(1)} %get-tuple-element.28), channel_id=1, source_target_pairs={{0,8},{4,20},{8,0},{12,28},{16,24},{20,4},{24,16},{28,12},{1,9},{5... | collective-permute-start | bytes 786440 | tf_op jit(solution)/shard_map/ppermute | solution.py:383
  10.0 13.6 %collective-permute-start.9 = (f32[256,256]{1,0:T(8,128)S(1)}, f32[256,256]{1,0:T(8,128)S(1)}, u32[]{:S(2)}, u32[]{:S(2)}) collective-permute-start(f32[256,256]{1,0:T(8,128)S(1)} %get-tuple-element.33), channel_id=1, source_target_pairs={{0,1},{1,3},{2,0},{3,2},{4,5},{5,7},{6,4},{7,6},{8,9},{9,11},{10,8... | collective-permute-start | bytes 786440 | tf_op jit(solution)/shard_map/ppermute | solution.py:376
  14.4 15.7 %collective-permute-start.5 = (f32[256,256]{1,0:T(8,128)S(1)}, f32[256,256]{1,0:T(8,128)S(1)}, u32[]{:S(2)}, u32[]{:S(2)}) collective-permute-start(f32[256,256]{1,0:T(8,128)S(1)} %add.11.total_a), channel_id=1, source_target_pairs={{0,16},{4,12},{8,24},{12,4},{16,0},{20,28},{24,8},{28,20},{1,17},{... | collective-permute-start | bytes 786440 | tf_op jit(solution)/shard_map/ppermute | solution.py:387
  16.5 15.5 %collective-permute-start.12 = (f32[256,256]{1,0:T(8,128)S(1)}, f32[256,256]{1,0:T(8,128)S(1)}, u32[]{:S(2)}, u32[]{:S(2)}) collective-permute-start(f32[256,256]{1,0:T(8,128)S(1)} %get-tuple-element.35), channel_id=1, source_target_pairs={{0,1},{1,0},{2,3},{3,2},{4,5},{5,4},{6,7},{7,6},{8,9},{9,8},{10,11... | collective-permute-start | bytes 786440 | tf_op jit(solution)/shard_map/ppermute | solution.py:376
  18.7 5.7 %collective-permute-start = (f32[64,256]{1,0:T(8,128)S(1)}, f32[64,256]{1,0:T(8,128)S(1)}, u32[]{:S(2)}, u32[]{:S(2)}) collective-permute-start(f32[64,256]{1,0:T(8,128)S(1)} %left.1), channel_id=1, source_target_pairs={{0,16},{4,12},{8,24},{12,4},{16,0},{20,28},{24,8},{28,20},{1,17},{... | collective-permute-start | bytes 196616 | tf_op jit(solution)/shard_map/ppermute | solution.py:384
  19.3 17.4 %collective-permute-start.10 = (f32[256,256]{1,0:T(8,128)S(1)}, f32[256,256]{1,0:T(8,128)S(1)}, u32[]{:S(2)}, u32[]{:S(2)}) collective-permute-start(f32[256,256]{1,0:T(8,128)S(1)} %get-tuple-element.34.block), channel_id=1, source_target_pairs={{0,3},{3,0},{4,7},{7,4},{8,11},{11,8},{12,15},{15,12},{16,19},{19,... | collective-permute-start | bytes 786440 | tf_op jit(solution)/shard_map/ppermute | solution.py:376
  23.7 13.0 %collective-permute-start.11 = (f32[256,256]{1,0:T(8,128)S(1)}, f32[256,256]{1,0:T(8,128)S(1)}, u32[]{:S(2)}, u32[]{:S(2)}) collective-permute-start(f32[256,256]{1,0:T(8,128)S(1)} %shard_map.78), channel_id=1, source_target_pairs={{1,2},{2,1},{5,6},{6,5},{9,10},{10,9},{13,14},{14,13},{17,18},{18,... | collective-permute-start | bytes 786440 | tf_op jit(solution)/shard_map/ppermute | solution.py:376
  24.4 4.3 %collective-permute-start.1 = (f32[64,256]{1,0:T(8,128)S(1)}, f32[64,256]{1,0:T(8,128)S(1)}, u32[]{:S(2)}, u32[]{:S(2)}) collective-permute-start(f32[64,256]{1,0:T(8,128)S(1)} %add.9), channel_id=1, source_target_pairs={{0,8},{4,20},{8,0},{12,28},{16,24},{20,4},{24,16},{28,12},{1,9},{5... | collective-permute-start | bytes 196616 | tf_op jit(solution)/shard_map/ppermute | solution.py:388
  28.8 1.3 %collective-permute-start.2 = (f32[64,256]{1,0:T(8,128)S(1)}, f32[64,256]{1,0:T(8,128)S(1)}, u32[]{:S(2)}, u32[]{:S(2)}) collective-permute-start(f32[64,256]{1,0:T(8,128)S(1)} %add.10.a_ref.left_a), channel_id=1, source_target_pairs={{0,4},{4,0},{8,12},{12,8},{16,20},{20,16},{24,28},{28,24},{1,5},{5... | collective-permute-start | bytes 196616 | tf_op jit(solution)/shard_map/ppermute | solution.py:389
  30.3 7.2 %copy-start = (f32[256,1024]{1,0:T(8,128)S(1)}, f32[256,1024]{1,0:T(8,128)}, u32[]{:S(2)}) copy-start(f32[256,1024]{1,0:T(8,128)} %wt.5) | copy-start | bytes 3145732
  30.3 7.2 %collective-permute-start.8 = (f32[64,256]{1,0:T(8,128)S(1)}, f32[64,256]{1,0:T(8,128)S(1)}, u32[]{:S(2)}, u32[]{:S(2)}) collective-permute-start(f32[64,256]{1,0:T(8,128)S(1)} %right.1.rest_0_), channel_id=1, source_target_pairs={{0,4},{4,0},{8,12},{12,8},{16,20},{20,16},{24,28},{28,24},{1,5},{5... | collective-permute-start | bytes 196616 | tf_op jit(solution)/shard_map/ppermute | solution.py:409
  30.5 7.0 %collective-permute-start.7 = (f32[64,256]{1,0:T(8,128)S(1)}, f32[64,256]{1,0:T(8,128)S(1)}, u32[]{:S(2)}, u32[]{:S(2)}) collective-permute-start(f32[64,256]{1,0:T(8,128)S(1)} %right.1.rest_0_), channel_id=1, source_target_pairs={{0,8},{4,20},{8,0},{12,28},{16,24},{20,4},{24,16},{28,12},{1,9},{5... | collective-permute-start | bytes 196616 | tf_op jit(solution)/shard_map/ppermute | solution.py:407
  32.0 7.1 %collective-permute-start.6 = (f32[64,256]{1,0:T(8,128)S(1)}, f32[64,256]{1,0:T(8,128)S(1)}, u32[]{:S(2)}, u32[]{:S(2)}) collective-permute-start(f32[64,256]{1,0:T(8,128)S(1)} %right.1.rest_0_), channel_id=1, source_target_pairs={{0,12},{4,16},{8,4},{12,24},{16,28},{20,0},{24,20},{28,8},{1,13},{... | collective-permute-start | bytes 196616 | tf_op jit(solution)/shard_map/ppermute | solution.py:408

commit v4 on v2

--- a/solution.py
+++ b/solution.py
@@ -14,7 +14,7 @@
 NN = (((1,), (0,)), ((), ()))
 NT = (((1,), (1,)), ((), ()))
 VMEM_BYTES = 67043328
-SPARE = 27 << 19
+SPARE = 28 << 19
 VMEM = pl.BlockSpec(memory_space=pltpu.VMEM)
 ANY = pl.BlockSpec(memory_space=pl.ANY)
 HBM = pl.BlockSpec(memory_space=pltpu.HBM)
@@ -73,9 +73,13 @@
     return index
 
 
-def blocks_kernel(tables, n, chunks, acts, og, wt, acts_t, *rest):
-    rows_v, outs = rest[:n], rest[n : 2 * n]
-    acts_v, wt_v, wt_2, sems = rest[2 * n :]
+def part_of(rows, high, low):
+    both = jnp.concatenate([high[...], low[...]], axis=1)
+    return dot(jnp.concatenate([rows, rows], axis=1), both, NT)
+
+
+def first_kernel(tables, n, chunks, acts, og, wt, acts_t, high_v, low_v, out, *rest):
+    rows_v, (acts_v, wt_v, sems) = rest[:n], rest[n:]
     tok = acts.shape[0]
     _, cols = wt.shape
     block = tok // n
@@ -102,42 +106,66 @@
     for c in range(chunks):
         wt_in[c].wait()
         high, low = split(wt_v[c])
-        wt_2[:, c * width : (c + 1) * width] = high
-        wt_2[:, cols + c * width : cols + (c + 1) * width] = low
-    for copy in rows_in:
+        high_v[:, c * width : (c + 1) * width] = high
+        low_v[:, c * width : (c + 1) * width] = low
+    rows_in[0].wait()
+    out[...] = part_of(rows_v[0][...], high_v, low_v)
+    for copy in rows_in[1:]:
         copy.wait()
-    for k in range(n):
-        rows = rows_v[k][...]
-        outs[k][...] = dot(jnp.concatenate([rows, rows], axis=1), wt_2[...], NT)
-
-
-def blocks_of(acts, og, wt, rounds):
-    n = len(rounds) + 1
+
+
+def first_of(acts, og, wt, tables):
+    n = len(tables)
     tok = og.shape[0]
     din, cols = wt.shape
     chunks = 2
     block = tok // n
     shape = jax.ShapeDtypeStruct
-    out = pl.pallas_call(
-        functools.partial(blocks_kernel, [{}, *rounds], n, chunks),
-        out_shape=[shape((din, tok), BF16)]
-        + [shape((block, cols), BF16)] * n
-        + [shape((block, din), F32)] * n,
+    acts_t, high, low, out, *rows = pl.pallas_call(
+        functools.partial(first_kernel, tables, n, chunks),
+        out_shape=[
+            shape((din, tok), BF16),
+            shape((din, cols), BF16),
+            shape((din, cols), BF16),
+            shape((block, din), F32),
+        ]
+        + [shape((block, cols), BF16)] * n,
         in_specs=[HBM] * 3,
-        out_specs=[VMEM] * (1 + 2 * n),
+        out_specs=[VMEM] * (4 + n),
         scratch_shapes=[
             pltpu.VMEM((tok, din), BF16),
             pltpu.VMEM((chunks, din, cols // chunks), F32),
-            pltpu.VMEM((din, 2 * cols), BF16),
             pltpu.SemaphoreType.DMA((2 * n + chunks,)),
         ],
         compiler_params=pltpu.CompilerParams(vmem_limit_bytes=VMEM_BYTES - SPARE),
         cost_estimate=pl.CostEstimate(
-            flops=4 * tok * din * cols, bytes_accessed=4 << 20, transcendentals=0
+            flops=4 * block * din * cols, bytes_accessed=4 << 20, transcendentals=0
         ),
-        name="blocks",
+        name="first",
     )(acts, og, wt)
-    return out[0], out[1 : 1 + n], out[1 + n :]
+    return acts_t, (high, low), out, rows
+
+
+def rest_kernel(high, low, *rest):
+    count = len(rest) // 2
+    for rows, out in zip(rest[:count], rest[count:]):
+        out[...] = part_of(rows[...], high, low)
+
+
+def rest_of(halves, rows):
+    block, cols = rows[0].shape
+    din = halves[0].shape[0]
+    return pl.pallas_call(
+        rest_kernel,
+        out_shape=[jax.ShapeDtypeStruct((block, din), F32)] * len(rows),
+        in_specs=[VMEM] * (2 + len(rows)),
+        out_specs=[VMEM] * len(rows),
+        compiler_params=pltpu.CompilerParams(vmem_limit_bytes=12 << 20),
+        cost_estimate=pl.CostEstimate(
+            flops=4 * len(rows) * block * din * cols, bytes_accessed=4 << 20, transcendentals=0
+        ),
+        name="rest",
+    )(*halves, *rows)
 
 
 def merged_kernel(acts_t, err, *rest):
@@ -373,12 +401,13 @@
     pair = swap(1, 1, replicas)
 
     table, relays = rounds_of(n_tensor)
-    acts_t, rows, blocks = blocks_of(acts, out_grad, weight, table)
+    tables = [table[0], {}, *table[1:]]
+    acts_t, halves, first, rows = first_of(acts, out_grad, weight, tables)
 
     def across(block, n):
         return send(block, "tensor", [(a, to) for a, (to, _) in sorted(table[n].items())])
 
-    received = [across(blocks[1], 0)]
+    received = [across(first, 0)]
     theirs, mine = merged_of(acts_t, error, rows)
     came = send(theirs, "dp", pair)
     left = left_of(start_q.T, theirs, mine)
@@ -391,8 +420,9 @@
         left = left + send(left, "dp", swap(other, one, replicas))
     left_came = send(left, "dp", pair)
 
+    blocks = rest_of(halves, rows[1:])
     for n in range(1, n_tensor - 1):
-        block = blocks[n + 1]
+        block = blocks[n]
         if relays and n == 1:
             onward = functools.partial(onward_kernel, n_tensor)
             block = summed(onward, block, received[0])

time: 38 us -> 37.7 us (level)
    pallas_call x1 -> x2, Pallas kernels: 3.55 us -> 3.28 us  [the longest x1 2.27 us: first_of(): pl.pallas_call(functools.partial(first_kernel, tables, n, chunks), out_sh...]
  transfers between devices with their start and end apart: 12 -> 12, of which waited for: 4 -> 4; matrix products, arithmetic and copies ran while one was open for 0% -> 0% of each run, Pallas kernels for 17% -> 20%
where the time goes in v4:
time: 37.7 us; the launch traced here: 37.6 us
  starting transfers between devices  16.5 us (44%)
  Pallas kernels  11.8 us (31%)
  waiting for transfers between devices  8.35 us (22%)
  between operations  0.76 us (2%)
    ppermute x12, starting transfers between devices, send(): return lax.ppermute(x, axis, pairs)  16.5 us
    ppermute x12, waiting for transfers between devices, send(): return lax.ppermute(x, axis, pairs)  8.35 us
    pallas_call x1, Pallas kernels, solve(): pl.pallas_call(functools.partial(solve_kernel, replicas), out_shape=jax.S...  3.49 us
    pallas_call x2, Pallas kernels, back(): pl.pallas_call(functools.partial(back_kernel, pieces, bits), out_shape=[j...  2.67 us
    pallas_call x1, Pallas kernels, first_of(): pl.pallas_call(functools.partial(first_kernel, tables, n, chunks), out_sh...  2.27 us
    pallas_call x1, Pallas kernels, rest_of(): pl.pallas_call(rest_kernel, out_shape=[jax.ShapeDtypeStruct((block, din),...  1.01 us
    pallas_call x2, Pallas kernels, summed(): pl.pallas_call(kernel, out_shape=jax.ShapeDtypeStruct(parts[0].shape, F32...  0.79 us
  transfers between devices with their start and end apart: 12, of which 4 were waited for; matrix products, arithmetic and copies ran while one was open for 0% of the time, Pallas kernels for 20%

profile of v4, /device:TPU:0, one launch (start us, length us, event | category | flops | bytes accessed | tf_op | source)
XLA Modules:
  0.0 37.6 jit_solution(10809775007725566363)
XLA Ops:
  0.6 0.0 copy-start.1
  0.6 2.3 %first.1 = (bf16[256,1024]{1,0:T(8,128)(2,1)S(1)}, bf16[256,1024]{1,0:T(8,128)(2,1)S(1)}, bf16[256,1024]{1,0:T(8,128)(2,1)S(1)}, f32[256,256]{1,0:T(8,128)S(1)},...) custom-call(bf16[1024,256]{1,0:T(8,128)(2,1)} %acts.1, ...), custom_call_target="tpu_custom_call" | custom-call | flops 268435456 | bytes 4194304 | tf_op jit(solution)/shard_map/first/pallas_call | solution.py:124
  2.9 0.1 copy-done.1
  3.1 0.0 copy-start.2
  3.1 0.7 %merged.1 = (f32[256,512]{1,0:T(8,128)S(1)}, f32[256,512]{1,0:T(8,128)S(1)}) custom-call(bf16[256,1024]{1,0:T(8,128)(2,1)S(1)} %get-tuple-element.22.acts_t, f32[1,256,1024]{2,1,0:T(8,128)S(1)} %copy-done.1, bf16[256,1024]{1,0:T(8,128)(2,1)S(1)} %get-tuple-element.23.rest_0_, bf16[256,1024]{1,0:T(8,128)(2,1)S(1)} %get-tuple-element.24.rest_1_.rest_0_, ...), custom_call_target="tpu_custom_call" | custom-call | flops 536870912 | bytes 4194304 | tf_op jit(solution)/shard_map/merged/pallas_call | solution.py:186
  3.8 0.6 %collective-permute-start.3 = (f32[256,512]{1,0:T(8,128)S(1)}, f32[256,512]{1,0:T(8,128)S(1)}, u32[]{:S(2)}, u32[]{:S(2)}) collective-permute-start(f32[256,512]{1,0:T(8,128)S(1)} %get-tuple-element.27.theirs.rest_5_.rest_1_), channel_id=1, source_target_pairs={{0,4},{4,0},{8,12},{12,8},{16,20},{20,16},{24,28},{28,24},{1,5},{5... | collective-permute-start | bytes 1572872 | tf_op jit(solution)/shard_map/ppermute | solution.py:394
  4.3 1.5 %collective-permute-done.3.came = f32[256,512]{1,0:T(8,128)S(1)} collective-permute-done((f32[256,512]{1,0:T(8,128)S(1)}, f32[256,512]{1,0:T(8,128)S(1)}, u32[]{:S(2)}, u32[]{:S(2)}) %collective-permute-start.3) | collective-permute-done | bytes 524320 | tf_op jit(solution)/shard_map/ppermute | solution.py:394
  5.9 0.1 begin.1
  6.0 2.9 %collective-permute-start.4 = (f32[256,256]{1,0:T(8,128)S(1)}, f32[256,256]{1,0:T(8,128)S(1)}, u32[]{:S(2)}, u32[]{:S(2)}) collective-permute-start(f32[256,256]{1,0:T(8,128)S(1)} %get-tuple-element.30), channel_id=1, source_target_pairs={{0,8},{4,20},{8,0},{12,28},{16,24},{20,4},{24,16},{28,12},{1,9},{5... | collective-permute-start | bytes 786440 | tf_op jit(solution)/shard_map/ppermute | solution.py:394
  8.9 1.6 %collective-permute-start.9 = (f32[256,256]{1,0:T(8,128)S(1)}, f32[256,256]{1,0:T(8,128)S(1)}, u32[]{:S(2)}, u32[]{:S(2)}) collective-permute-start(f32[256,256]{1,0:T(8,128)S(1)} %get-tuple-element.35), channel_id=1, source_target_pairs={{0,1},{1,3},{2,0},{3,2},{4,5},{5,7},{6,4},{7,6},{8,9},{9,11},{10,8... | collective-permute-start | bytes 786440 | tf_op jit(solution)/shard_map/ppermute | solution.py:394
  10.4 2.8 %collective-permute-done.4 = f32[256,256]{1,0:T(8,128)S(1)} collective-permute-done((f32[256,256]{1,0:T(8,128)S(1)}, f32[256,256]{1,0:T(8,128)S(1)}, u32[]{:S(2)}, u32[]{:S(2)}) %collective-permute-start.4) | collective-permute-done | bytes 262176 | tf_op jit(solution)/shard_map/ppermute | solution.py:394
  13.2 2.1 %collective-permute-start.5 = (f32[256,256]{1,0:T(8,128)S(1)}, f32[256,256]{1,0:T(8,128)S(1)}, u32[]{:S(2)}, u32[]{:S(2)}) collective-permute-start(f32[256,256]{1,0:T(8,128)S(1)} %add.11.total_a), channel_id=1, source_target_pairs={{0,16},{4,12},{8,24},{12,4},{16,0},{20,28},{24,8},{28,20},{1,17},{... | collective-permute-start | bytes 786440 | tf_op jit(solution)/shard_map/ppermute | solution.py:394
  15.4 0.0 copy-done.2
  15.4 0.6 %left.1 = f32[64,256]{1,0:T(8,128)S(1)} custom-call(f32[64,1024]{1,0:T(8,128)S(1)} %bitcast.1, f32[256,512]{1,0:T(8,128)S(1)} %get-tuple-element.27.theirs.rest_5_.rest_1_, f32[256,512]{1,0:T(8,128)S(1)} %get-tuple-element.28.mine.rest_3_.rest_4_), custom_call_target="tpu_custom_call" | custom-call | tf_op jit(solution)/shard_map/left/pallas_call | solution.py:236
  16.0 0.1 collective-permute-start
  16.0 1.0 %rest.1 = (f32[256,256]{1,0:T(8,128)S(1)}, f32[256,256]{1,0:T(8,128)S(1)}, f32[256,256]{1,0:T(8,128)S(1)}) custom-call(bf16[256,1024]{1,0:T(8,128)(2,1)S(1)} %get-tuple-element.36.high, bf16[256,1024]{1,0:T(8,128)(2,1)S(1)} %get-tuple-element.37.low, bf16[256,1024]{1,0:T(8,128)(2,1)S(1)} %get-tuple-element.24.rest_1_.rest_0_, ...), custom_call_target="tpu_custom_call" | custom-call | flops 805306368 | bytes 4194304 | tf_op jit(solution)/shard_map/rest/pallas_call | solution.py:158
  17.1 2.1 %collective-permute-start.11 = (f32[256,256]{1,0:T(8,128)S(1)}, f32[256,256]{1,0:T(8,128)S(1)}, u32[]{:S(2)}, u32[]{:S(2)}) collective-permute-start(f32[256,256]{1,0:T(8,128)S(1)} %get-tuple-element.39), channel_id=1, source_target_pairs={{0,1},{1,0},{2,3},{3,2},{4,5},{5,4},{6,7},{7,6},{8,9},{9,8},{10,11... | collective-permute-start | bytes 786440 | tf_op jit(solution)/shard_map/ppermute | solution.py:394
  19.2 0.0 collective-permute-done.9.relayed.first
  19.2 2.5 %collective-permute-start.10 = (f32[256,256]{1,0:T(8,128)S(1)}, f32[256,256]{1,0:T(8,128)S(1)}, u32[]{:S(2)}, u32[]{:S(2)}) collective-permute-start(f32[256,256]{1,0:T(8,128)S(1)} %shard_map.78), channel_id=1, source_target_pairs={{0,3},{1,2},{2,1},{3,0},{4,7},{5,6},{6,5},{7,4},{8,11},{9,10},{10,... | collective-permute-start | bytes 786440 | tf_op jit(solution)/shard_map/ppermute | solution.py:394
  21.8 0.0 collective-permute-done
  21.8 1.6 %collective-permute-start.1 = (f32[64,256]{1,0:T(8,128)S(1)}, f32[64,256]{1,0:T(8,128)S(1)}, u32[]{:S(2)}, u32[]{:S(2)}) collective-permute-start(f32[64,256]{1,0:T(8,128)S(1)} %add.9), channel_id=1, source_target_pairs={{0,8},{4,20},{8,0},{12,28},{16,24},{20,4},{24,16},{28,12},{1,9},{5... | collective-permute-start | bytes 196616 | tf_op jit(solution)/shard_map/ppermute | solution.py:394
  23.3 2.8 %collective-permute-done.1 = f32[64,256]{1,0:T(8,128)S(1)} collective-permute-done((f32[64,256]{1,0:T(8,128)S(1)}, f32[64,256]{1,0:T(8,128)S(1)}, u32[]{:S(2)}, u32[]{:S(2)}) %collective-permute-start.1) | collective-permute-done | bytes 65568 | tf_op jit(solution)/shard_map/ppermute | solution.py:394
  26.1 0.1 collective-permute-start.2
  26.2 1.2 %collective-permute-done.2.b_ref.left_b = f32[64,256]{1,0:T(8,128)S(1)} collective-permute-done((f32[64,256]{1,0:T(8,128)S(1)}, f32[64,256]{1,0:T(8,128)S(1)}, u32[]{:S(2)}, u32[]{:S(2)}) %collective-permute-start.2) | collective-permute-done | bytes 65568 | tf_op jit(solution)/shard_map/ppermute | solution.py:394
  27.4 0.0 collective-permute-done.5.total_b
  27.4 0.2 right.1.rest_0_
  27.6 0.0 copy-start
  27.7 0.2 collective-permute-start.8
  27.9 1.5 %collective-permute-start.7 = (f32[64,256]{1,0:T(8,128)S(1)}, f32[64,256]{1,0:T(8,128)S(1)}, u32[]{:S(2)}, u32[]{:S(2)}) collective-permute-start(f32[64,256]{1,0:T(8,128)S(1)} %right.1.rest_0_), channel_id=1, source_target_pairs={{0,8},{4,20},{8,0},{12,28},{16,24},{20,4},{24,16},{28,12},{1,9},{5... | collective-permute-start | bytes 196616 | tf_op jit(solution)/shard_map/ppermute | solution.py:394
  29.4 1.2 %collective-permute-start.6 = (f32[64,256]{1,0:T(8,128)S(1)}, f32[64,256]{1,0:T(8,128)S(1)}, u32[]{:S(2)}, u32[]{:S(2)}) collective-permute-start(f32[64,256]{1,0:T(8,128)S(1)} %right.1.rest_0_), channel_id=1, source_target_pairs={{0,12},{4,16},{8,4},{12,24},{16,28},{20,0},{24,20},{28,8},{1,13},{... | collective-permute-start | bytes 196616 | tf_op jit(solution)/shard_map/ppermute | solution.py:394
  30.6 3.5 %solve.1.basis = f32[64,256]{1,0:T(8,128)S(1)} custom-call(f32[64,256]{1,0:T(8,128)S(1)} %add.10.a_ref.left_a, f32[64,256]{1,0:T(8,128)S(1)} %collective-permute-done.2.b_ref.left_b), custom_call_target="tpu_custom_call" | custom-call | flops 1073741824 | bytes 1048576 | tf_op jit(solution)/shard_map/solve/pallas_call | solution.py:287
  34.1 0.0 collective-permute-done.11.rest_1_
  34.1 0.0 collective-permute-done.10.rest_0_
  34.1 0.8 %shard_map.79 = f32[256,256]{1,0:T(8,128)} custom-call(f32[256,256]{1,0:T(8,128)S(1)} %collective-permute-done.9.relayed.first, f32[256,256]{1,0:T(8,128)S(1)} %collective-permute-done.10.rest_0_, f32[256,256]{1,0:T(8,128)S(1)} %collective-permute-done.11.rest_1_, f32[256,256]{1,0:T(8,128)S(1)} %get-tuple-element.40.rest_2_), custom_call_target="tpu_custom_call" | custom-call | tf_op jit(solution)/shard_map/pallas_call | solution.py:218
  34.9 0.0 collective-permute-done.8.rest_2_
  34.9 0.0 collective-permute-done.7.rest_1_
  34.9 0.0 copy-done
  34.9 1.5 %shard_map.76 = (f32[256,1024]{1,0:T(8,128)}, f32[1,256,1024]{2,1,0:T(8,128)}) custom-call(f32[64,256]{1,0:T(8,128)S(1)} %solve.1.basis, f32[256,1024]{1,0:T(8,128)S(1)} %copy-done, f32[64,256]{1,0:T(8,128)S(1)} %right.1.rest_0_, f32[64,256]{1,0:T(8,128)S(1)} %collective-permute-done.7.rest_1_, f32[64,256]{1,0:T(8,128)S(1)} %collective-permute-done.8.rest_2_, ...), custom_call_target="tpu_custom_call" | custom-call | tf_op jit(solution)/shard_map/pallas_call | solution.py:375
  36.4 0.0 collective-permute-done.6.rest_0_
  36.4 1.1 %shard_map.77 = (f32[256,1024]{1,0:T(8,128)}, f32[1,256,1024]{2,1,0:T(8,128)}) custom-call(f32[64,256]{1,0:T(8,128)S(1)} %solve.1.basis, f32[256,1024]{1,0:T(8,128)S(1)} %copy-done, f32[64,256]{1,0:T(8,128)S(1)} %collective-permute-done.6.rest_0_, ...), custom_call_target="tpu_custom_call", output_to_operand_aliasing={{0}: (4, {}), {1}: (5, {})} | custom-call | tf_op jit(solution)/shard_map/pallas_call | solution.py:375
  (4 shorter events, 0.1 us)
Async XLA Ops:
  0.6 2.4 %copy-start.1 = (f32[1,256,1024]{2,1,0:T(8,128)S(1)}, f32[1,256,1024]{2,1,0:T(8,128)}, u32[]{:S(2)}) copy-start(f32[1,256,1024]{2,1,0:T(8,128)} %err.1) | copy-start | bytes 3145732
  3.1 12.3 %copy-start.2 = (f32[1024,64]{0,1:T(8,128)S(1)}, f32[1024,64]{0,1:T(8,128)}, u32[]{:S(2)}) copy-start(f32[1024,64]{0,1:T(8,128)} %param.9) | copy-start | bytes 786436
  3.8 2.1 %collective-permute-start.3 = (f32[256,512]{1,0:T(8,128)S(1)}, f32[256,512]{1,0:T(8,128)S(1)}, u32[]{:S(2)}, u32[]{:S(2)}) collective-permute-start(f32[256,512]{1,0:T(8,128)S(1)} %get-tuple-element.27.theirs.rest_5_.rest_1_), channel_id=1, source_target_pairs={{0,4},{4,0},{8,12},{12,8},{16,20},{20,16},{24,28},{28,24},{1,5},{5... | collective-permute-start | bytes 1572872 | tf_op jit(solution)/shard_map/ppermute | solution.py:394
  6.0 7.3 %collective-permute-start.4 = (f32[256,256]{1,0:T(8,128)S(1)}, f32[256,256]{1,0:T(8,128)S(1)}, u32[]{:S(2)}, u32[]{:S(2)}) collective-permute-start(f32[256,256]{1,0:T(8,128)S(1)} %get-tuple-element.30), channel_id=1, source_target_pairs={{0,8},{4,20},{8,0},{12,28},{16,24},{20,4},{24,16},{28,12},{1,9},{5... | collective-permute-start | bytes 786440 | tf_op jit(solution)/shard_map/ppermute | solution.py:394
  8.9 10.3 %collective-permute-start.9 = (f32[256,256]{1,0:T(8,128)S(1)}, f32[256,256]{1,0:T(8,128)S(1)}, u32[]{:S(2)}, u32[]{:S(2)}) collective-permute-start(f32[256,256]{1,0:T(8,128)S(1)} %get-tuple-element.35), channel_id=1, source_target_pairs={{0,1},{1,3},{2,0},{3,2},{4,5},{5,7},{6,4},{7,6},{8,9},{9,11},{10,8... | collective-permute-start | bytes 786440 | tf_op jit(solution)/shard_map/ppermute | solution.py:394
  13.2 14.2 %collective-permute-start.5 = (f32[256,256]{1,0:T(8,128)S(1)}, f32[256,256]{1,0:T(8,128)S(1)}, u32[]{:S(2)}, u32[]{:S(2)}) collective-permute-start(f32[256,256]{1,0:T(8,128)S(1)} %add.11.total_a), channel_id=1, source_target_pairs={{0,16},{4,12},{8,24},{12,4},{16,0},{20,28},{24,8},{28,20},{1,17},{... | collective-permute-start | bytes 786440 | tf_op jit(solution)/shard_map/ppermute | solution.py:394
  16.0 5.8 %collective-permute-start = (f32[64,256]{1,0:T(8,128)S(1)}, f32[64,256]{1,0:T(8,128)S(1)}, u32[]{:S(2)}, u32[]{:S(2)}) collective-permute-start(f32[64,256]{1,0:T(8,128)S(1)} %left.1), channel_id=1, source_target_pairs={{0,16},{4,12},{8,24},{12,4},{16,0},{20,28},{24,8},{28,20},{1,17},{... | collective-permute-start | bytes 196616 | tf_op jit(solution)/shard_map/ppermute | solution.py:394
  17.1 17.0 %collective-permute-start.11 = (f32[256,256]{1,0:T(8,128)S(1)}, f32[256,256]{1,0:T(8,128)S(1)}, u32[]{:S(2)}, u32[]{:S(2)}) collective-permute-start(f32[256,256]{1,0:T(8,128)S(1)} %get-tuple-element.39), channel_id=1, source_target_pairs={{0,1},{1,0},{2,3},{3,2},{4,5},{5,4},{6,7},{7,6},{8,9},{9,8},{10,11... | collective-permute-start | bytes 786440 | tf_op jit(solution)/shard_map/ppermute | solution.py:394
  19.2 14.9 %collective-permute-start.10 = (f32[256,256]{1,0:T(8,128)S(1)}, f32[256,256]{1,0:T(8,128)S(1)}, u32[]{:S(2)}, u32[]{:S(2)}) collective-permute-start(f32[256,256]{1,0:T(8,128)S(1)} %shard_map.78), channel_id=1, source_target_pairs={{0,3},{1,2},{2,1},{3,0},{4,7},{5,6},{6,5},{7,4},{8,11},{9,10},{10,... | collective-permute-start | bytes 786440 | tf_op jit(solution)/shard_map/ppermute | solution.py:394
  21.8 4.3 %collective-permute-start.1 = (f32[64,256]{1,0:T(8,128)S(1)}, f32[64,256]{1,0:T(8,128)S(1)}, u32[]{:S(2)}, u32[]{:S(2)}) collective-permute-start(f32[64,256]{1,0:T(8,128)S(1)} %add.9), channel_id=1, source_target_pairs={{0,8},{4,20},{8,0},{12,28},{16,24},{20,4},{24,16},{28,12},{1,9},{5... | collective-permute-start | bytes 196616 | tf_op jit(solution)/shard_map/ppermute | solution.py:394
  26.1 1.3 %collective-permute-start.2 = (f32[64,256]{1,0:T(8,128)S(1)}, f32[64,256]{1,0:T(8,128)S(1)}, u32[]{:S(2)}, u32[]{:S(2)}) collective-permute-start(f32[64,256]{1,0:T(8,128)S(1)} %add.10.a_ref.left_a), channel_id=1, source_target_pairs={{0,4},{4,0},{8,12},{12,8},{16,20},{20,16},{24,28},{28,24},{1,5},{5... | collective-permute-start | bytes 196616 | tf_op jit(solution)/shard_map/ppermute | solution.py:394
  27.6 7.2 %copy-start = (f32[256,1024]{1,0:T(8,128)S(1)}, f32[256,1024]{1,0:T(8,128)}, u32[]{:S(2)}) copy-start(f32[256,1024]{1,0:T(8,128)} %wt.5) | copy-start | bytes 3145732
  27.7 7.2 %collective-permute-start.8 = (f32[64,256]{1,0:T(8,128)S(1)}, f32[64,256]{1,0:T(8,128)S(1)}, u32[]{:S(2)}, u32[]{:S(2)}) collective-permute-start(f32[64,256]{1,0:T(8,128)S(1)} %right.1.rest_0_), channel_id=1, source_target_pairs={{0,4},{4,0},{8,12},{12,8},{16,20},{20,16},{24,28},{28,24},{1,5},{5... | collective-permute-start | bytes 196616 | tf_op jit(solution)/shard_map/ppermute | solution.py:394
  27.9 7.0 %collective-permute-start.7 = (f32[64,256]{1,0:T(8,128)S(1)}, f32[64,256]{1,0:T(8,128)S(1)}, u32[]{:S(2)}, u32[]{:S(2)}) collective-permute-start(f32[64,256]{1,0:T(8,128)S(1)} %right.1.rest_0_), channel_id=1, source_target_pairs={{0,8},{4,20},{8,0},{12,28},{16,24},{20,4},{24,16},{28,12},{1,9},{5... | collective-permute-start | bytes 196616 | tf_op jit(solution)/shard_map/ppermute | solution.py:394
  29.4 7.0 %collective-permute-start.6 = (f32[64,256]{1,0:T(8,128)S(1)}, f32[64,256]{1,0:T(8,128)S(1)}, u32[]{:S(2)}, u32[]{:S(2)}) collective-permute-start(f32[64,256]{1,0:T(8,128)S(1)} %right.1.rest_0_), channel_id=1, source_target_pairs={{0,12},{4,16},{8,4},{12,24},{16,28},{20,0},{24,20},{28,8},{1,13},{... | collective-permute-start | bytes 196616 | tf_op jit(solution)/shard_map/ppermute | solution.py:394

commit v5 on v4

--- a/solution.py
+++ b/solution.py
@@ -390,10 +390,6 @@
     )(basis, wt, *rights, *merged, *kept)
 
 
-def send(x, axis, pairs):
-    return lax.ppermute(x, axis, pairs)
-
-
 def step(acts, out_grad, weight, error, start_q):
     replicas = lax.axis_size("dp")
     n_tensor = lax.axis_size("tensor")
@@ -404,43 +400,48 @@
     tables = [table[0], {}, *table[1:]]
     acts_t, halves, first, rows = first_of(acts, out_grad, weight, tables)
 
-    def across(block, n):
-        return send(block, "tensor", [(a, to) for a, (to, _) in sorted(table[n].items())])
+    def across(block, n, only=range(n_tensor)):
+        hops = [(a, to) for a, (to, _) in sorted(table[n].items()) if a in only]
+        return lax.ppermute(block, "tensor", hops)
 
     received = [across(first, 0)]
     theirs, mine = merged_of(acts_t, error, rows)
-    came = send(theirs, "dp", pair)
+    came = lax.ppermute(theirs, "dp", pair)
     left = left_of(start_q.T, theirs, mine)
     total, give = begin(mine, came, bits)
-    came = send(give, "dp", swap(bits[0], bits[-1], replicas))
-    left = left + send(left, "dp", swap(bits[-1], bits[0], replicas))
+    came = lax.ppermute(give, "dp", swap(bits[0], bits[-1], replicas))
+    left = left + lax.ppermute(left, "dp", swap(bits[-1], bits[0], replicas))
     for n, (one, other) in enumerate(zip(bits[1:], bits[-2::-1]), 2):
         total = total + came
-        came = send(total, "dp", swap(one, other, replicas))
-        left = left + send(left, "dp", swap(other, one, replicas))
-    left_came = send(left, "dp", pair)
+        came = lax.ppermute(total, "dp", swap(one, other, replicas))
+        left = left + lax.ppermute(left, "dp", swap(other, one, replicas))
+    left_came = lax.ppermute(left, "dp", pair)
 
     blocks = rest_of(halves, rows[1:])
     for n in range(1, n_tensor - 1):
         block = blocks[n]
         if relays and n == 1:
+            between = (1, n_tensor - 2)
+            ends = [a for a in range(n_tensor) if a not in between]
+            received.append(across(block, n, ends))
             onward = functools.partial(onward_kernel, n_tensor)
             block = summed(onward, block, received[0])
-        received.append(across(block, n))
+            received.append(across(block, n, between))
+        else:
+            received.append(across(block, n))
     gather = functools.partial(gather_kernel, n_tensor if relays else None)
     input_grad = summed(gather, *received, blocks[0])
 
     basis = solve(left, left_came, replicas)
     right = right_of(left, left_came, total, came, replicas)
-    beside = send(right, "dp", swap(bits[0], bits[-1], replicas))
-    diagonal = send(right, "dp", swap(bits[0] | 1, bits[-1] | 1, replicas))
-    across_pair = send(right, "dp", pair)
-    pieces = ((True, True), (True, False), (False, True))
-    rights = (right, beside, across_pair)
-    kept = back(pieces, bits, basis, weight, rights, (mine, mine, theirs))
-    new_weight, new_error = back(
-        ((False, False),), bits, basis, weight, (diagonal,), (theirs,), *kept
-    )
+    across_pair = lax.ppermute(right, "dp", pair)
+    beside = lax.ppermute(right, "dp", swap(bits[0], bits[-1], replicas))
+    diagonal = lax.ppermute(right, "dp", swap(bits[0] | 1, bits[-1] | 1, replicas))
+    halves = (mine, theirs)
+    rights = (right, across_pair)
+    kept = back(((True, True), (False, True)), bits, basis, weight, rights, halves)
+    pieces, rights = ((True, False), (False, False)), (beside, diagonal)
+    new_weight, new_error = back(pieces, bits, basis, weight, rights, halves, *kept)
     return (new_weight, new_error, input_grad)
 
 

time: 37.7 us -> 39.8 us (1.056)
  starting transfers between devices: 16.5 us -> 18.3 us
    ppermute x12 -> x13, starting transfers between devices: 16.5 us -> 18.3 us  [the longest x4 8.27 us: across(): return lax.ppermute(block, 'tensor', hops)]
    ppermute x12 -> x13, waiting for transfers between devices: 8.35 us -> 8.35 us  [the longest x1 2.77 us: step(): came = lax.ppermute(give, 'dp', swap(bits[0], bits[-1], replicas))]
  transfers between devices with their start and end apart: 12 -> 13, of which waited for: 4 -> 4; matrix products, arithmetic and copies ran while one was open for 0% -> 0% of each run, Pallas kernels for 20% -> 19%
where the time goes in v5:
time: 39.8 us; the launch traced here: 39.6 us
  starting transfers between devices  18.3 us (46%)
  Pallas kernels  12 us (30%)
  waiting for transfers between devices  8.35 us (21%)
  between operations  0.81 us (2%)
    ppermute x4, starting transfers between devices, across(): return lax.ppermute(block, 'tensor', hops)  8.27 us
    pallas_call x1, Pallas kernels, solve(): pl.pallas_call(functools.partial(solve_kernel, replicas), out_shape=jax.S...  3.49 us
    ppermute x1, starting transfers between devices, step(): came = lax.ppermute(give, 'dp', swap(bits[0], bits[-1], replicas))  2.9 us
    pallas_call x2, Pallas kernels, back(): pl.pallas_call(functools.partial(back_kernel, pieces, bits), out_shape=[j...  2.83 us
    ppermute x1, waiting for transfers between devices, step(): came = lax.ppermute(give, 'dp', swap(bits[0], bits[-1], replicas))  2.77 us
    ppermute x1, waiting for transfers between devices, step(): left = left + lax.ppermute(left, 'dp', swap(other, one, replicas))  2.77 us
    pallas_call x1, Pallas kernels, first_of(): pl.pallas_call(functools.partial(first_kernel, tables, n, chunks), out_sh...  2.27 us
    ppermute x1, starting transfers between devices, step(): came = lax.ppermute(total, 'dp', swap(one, other, replicas))  2.11 us
  transfers between devices with their start and end apart: 13, of which 4 were waited for; matrix products, arithmetic and copies ran while one was open for 0% of the time, Pallas kernels for 19%

profile of v5, /device:TPU:0, one launch (start us, length us, event | category | flops | bytes accessed | tf_op | source)
XLA Modules:
  0.0 39.6 jit_solution(3378725291936779933)
XLA Ops:
  0.6 0.0 copy-start.1
  0.6 2.3 %first.1 = (bf16[256,1024]{1,0:T(8,128)(2,1)S(1)}, bf16[256,1024]{1,0:T(8,128)(2,1)S(1)}, bf16[256,1024]{1,0:T(8,128)(2,1)S(1)}, f32[256,256]{1,0:T(8,128)S(1)},...) custom-call(bf16[1024,256]{1,0:T(8,128)(2,1)} %acts.1, ...), custom_call_target="tpu_custom_call" | custom-call | flops 268435456 | bytes 4194304 | tf_op jit(solution)/shard_map/first/pallas_call | solution.py:124
  2.9 0.1 copy-done.1
  3.1 0.7 %merged.1 = (f32[256,512]{1,0:T(8,128)S(1)}, f32[256,512]{1,0:T(8,128)S(1)}) custom-call(bf16[256,1024]{1,0:T(8,128)(2,1)S(1)} %get-tuple-element.22.acts_t, f32[1,256,1024]{2,1,0:T(8,128)S(1)} %copy-done.1, bf16[256,1024]{1,0:T(8,128)(2,1)S(1)} %get-tuple-element.23.rest_0_, bf16[256,1024]{1,0:T(8,128)(2,1)S(1)} %get-tuple-element.24.rest_1_.rest_0_, ...), custom_call_target="tpu_custom_call" | custom-call | flops 536870912 | bytes 4194304 | tf_op jit(solution)/shard_map/merged/pallas_call | solution.py:186
  3.8 0.6 %collective-permute-start.3 = (f32[256,512]{1,0:T(8,128)S(1)}, f32[256,512]{1,0:T(8,128)S(1)}, u32[]{:S(2)}, u32[]{:S(2)}) collective-permute-start(f32[256,512]{1,0:T(8,128)S(1)} %get-tuple-element.27.theirs.rest_3_), channel_id=1, source_target_pairs={{0,4},{4,0},{8,12},{12,8},{16,20},{20,16},{24,28},{28,24},{1,5},{5... | collective-permute-start | bytes 1572872 | tf_op jit(solution)/shard_map/ppermute | solution.py:409
  4.3 1.5 %collective-permute-done.3.came = f32[256,512]{1,0:T(8,128)S(1)} collective-permute-done((f32[256,512]{1,0:T(8,128)S(1)}, f32[256,512]{1,0:T(8,128)S(1)}, u32[]{:S(2)}, u32[]{:S(2)}) %collective-permute-start.3) | collective-permute-done | bytes 524320 | tf_op jit(solution)/shard_map/ppermute | solution.py:409
  5.9 0.1 begin.1
  6.0 0.0 copy-start.2
  6.0 2.9 %collective-permute-start.4 = (f32[256,256]{1,0:T(8,128)S(1)}, f32[256,256]{1,0:T(8,128)S(1)}, u32[]{:S(2)}, u32[]{:S(2)}) collective-permute-start(f32[256,256]{1,0:T(8,128)S(1)} %get-tuple-element.30), channel_id=1, source_target_pairs={{0,8},{4,20},{8,0},{12,28},{16,24},{20,4},{24,16},{28,12},{1,9},{5... | collective-permute-start | bytes 786440 | tf_op jit(solution)/shard_map/ppermute | solution.py:412
  8.9 1.6 %collective-permute-start.9 = (f32[256,256]{1,0:T(8,128)S(1)}, f32[256,256]{1,0:T(8,128)S(1)}, u32[]{:S(2)}, u32[]{:S(2)}) collective-permute-start(f32[256,256]{1,0:T(8,128)S(1)} %get-tuple-element.35), channel_id=1, source_target_pairs={{0,1},{1,3},{2,0},{3,2},{4,5},{5,7},{6,4},{7,6},{8,9},{9,11},{10,8... | collective-permute-start | bytes 786440 | tf_op jit(solution)/shard_map/ppermute | solution.py:405
  10.4 2.8 %collective-permute-done.4 = f32[256,256]{1,0:T(8,128)S(1)} collective-permute-done((f32[256,256]{1,0:T(8,128)S(1)}, f32[256,256]{1,0:T(8,128)S(1)}, u32[]{:S(2)}, u32[]{:S(2)}) %collective-permute-start.4) | collective-permute-done | bytes 262176 | tf_op jit(solution)/shard_map/ppermute | solution.py:412
  13.3 2.1 %collective-permute-start.5 = (f32[256,256]{1,0:T(8,128)S(1)}, f32[256,256]{1,0:T(8,128)S(1)}, u32[]{:S(2)}, u32[]{:S(2)}) collective-permute-start(f32[256,256]{1,0:T(8,128)S(1)} %add.11.total_a), channel_id=1, source_target_pairs={{0,16},{4,12},{8,24},{12,4},{16,0},{20,28},{24,8},{28,20},{1,17},{... | collective-permute-start | bytes 786440 | tf_op jit(solution)/shard_map/ppermute | solution.py:416
  15.4 1.0 %rest.1 = (f32[256,256]{1,0:T(8,128)S(1)}, f32[256,256]{1,0:T(8,128)S(1)}, f32[256,256]{1,0:T(8,128)S(1)}) custom-call(bf16[256,1024]{1,0:T(8,128)(2,1)S(1)} %get-tuple-element.36.high, bf16[256,1024]{1,0:T(8,128)(2,1)S(1)} %get-tuple-element.37.low, bf16[256,1024]{1,0:T(8,128)(2,1)S(1)} %get-tuple-element.24.rest_1_.rest_0_, ...), custom_call_target="tpu_custom_call" | custom-call | flops 805306368 | bytes 4194304 | tf_op jit(solution)/shard_map/rest/pallas_call | solution.py:158
  16.4 1.6 %collective-permute-start.12 = (f32[256,256]{1,0:T(8,128)S(1)}, f32[256,256]{1,0:T(8,128)S(1)}, u32[]{:S(2)}, u32[]{:S(2)}) collective-permute-start(f32[256,256]{1,0:T(8,128)S(1)} %get-tuple-element.39), channel_id=1, source_target_pairs={{0,1},{1,0},{2,3},{3,2},{4,5},{5,4},{6,7},{7,6},{8,9},{9,8},{10,11... | collective-permute-start | bytes 786440 | tf_op jit(solution)/shard_map/ppermute | solution.py:405
  18.0 0.0 copy-done.2
  18.0 0.6 %left.1 = f32[64,256]{1,0:T(8,128)S(1)} custom-call(f32[64,1024]{1,0:T(8,128)S(1)} %bitcast.1, f32[256,512]{1,0:T(8,128)S(1)} %get-tuple-element.27.theirs.rest_3_, f32[256,512]{1,0:T(8,128)S(1)} %get-tuple-element.28.mine.rest_2_), custom_call_target="tpu_custom_call" | custom-call | tf_op jit(solution)/shard_map/left/pallas_call | solution.py:236
  18.6 0.6 %collective-permute-start = (f32[64,256]{1,0:T(8,128)S(1)}, f32[64,256]{1,0:T(8,128)S(1)}, u32[]{:S(2)}, u32[]{:S(2)}) collective-permute-start(f32[64,256]{1,0:T(8,128)S(1)} %left.1), channel_id=1, source_target_pairs={{0,16},{4,12},{8,24},{12,4},{16,0},{20,28},{24,8},{28,20},{1,17},{... | collective-permute-start | bytes 196616 | tf_op jit(solution)/shard_map/ppermute | solution.py:413
  19.2 4.4 %collective-permute-start.10 = (f32[256,256]{1,0:T(8,128)S(1)}, f32[256,256]{1,0:T(8,128)S(1)}, u32[]{:S(2)}, u32[]{:S(2)}) collective-permute-start(f32[256,256]{1,0:T(8,128)S(1)} %get-tuple-element.38.block), channel_id=1, source_target_pairs={{0,3},{3,0},{4,7},{7,4},{8,11},{11,8},{12,15},{15,12},{16,19},{19,... | collective-permute-start | bytes 786440 | tf_op jit(solution)/shard_map/ppermute | solution.py:405
  23.6 0.0 collective-permute-done.9.relayed.first
  23.6 0.7 %collective-permute-start.11 = (f32[256,256]{1,0:T(8,128)S(1)}, f32[256,256]{1,0:T(8,128)S(1)}, u32[]{:S(2)}, u32[]{:S(2)}) collective-permute-start(f32[256,256]{1,0:T(8,128)S(1)} %shard_map.78), channel_id=1, source_target_pairs={{1,2},{2,1},{5,6},{6,5},{9,10},{10,9},{13,14},{14,13},{17,18},{18,... | collective-permute-start | bytes 786440 | tf_op jit(solution)/shard_map/ppermute | solution.py:405
  24.3 0.0 collective-permute-done
  24.3 1.6 %collective-permute-start.1 = (f32[64,256]{1,0:T(8,128)S(1)}, f32[64,256]{1,0:T(8,128)S(1)}, u32[]{:S(2)}, u32[]{:S(2)}) collective-permute-start(f32[64,256]{1,0:T(8,128)S(1)} %add.9), channel_id=1, source_target_pairs={{0,8},{4,20},{8,0},{12,28},{16,24},{20,4},{24,16},{28,12},{1,9},{5... | collective-permute-start | bytes 196616 | tf_op jit(solution)/shard_map/ppermute | solution.py:417
  25.9 2.8 %collective-permute-done.1 = f32[64,256]{1,0:T(8,128)S(1)} collective-permute-done((f32[64,256]{1,0:T(8,128)S(1)}, f32[64,256]{1,0:T(8,128)S(1)}, u32[]{:S(2)}, u32[]{:S(2)}) %collective-permute-start.1) | collective-permute-done | bytes 65568 | tf_op jit(solution)/shard_map/ppermute | solution.py:417
  28.7 0.1 collective-permute-start.2
  28.8 1.2 %collective-permute-done.2.b_ref.left_b = f32[64,256]{1,0:T(8,128)S(1)} collective-permute-done((f32[64,256]{1,0:T(8,128)S(1)}, f32[64,256]{1,0:T(8,128)S(1)}, u32[]{:S(2)}, u32[]{:S(2)}) %collective-permute-start.2) | collective-permute-done | bytes 65568 | tf_op jit(solution)/shard_map/ppermute | solution.py:418
  30.0 0.0 collective-permute-done.5.total_b
  30.0 0.2 right.1.rest_0_
  30.2 0.0 copy-start
  30.2 0.2 collective-permute-start.8
  30.4 1.4 %collective-permute-start.7 = (f32[64,256]{1,0:T(8,128)S(1)}, f32[64,256]{1,0:T(8,128)S(1)}, u32[]{:S(2)}, u32[]{:S(2)}) collective-permute-start(f32[64,256]{1,0:T(8,128)S(1)} %right.1.rest_0_), channel_id=1, source_target_pairs={{0,12},{4,16},{8,4},{12,24},{16,28},{20,0},{24,20},{28,8},{1,13},{... | collective-permute-start | bytes 196616 | tf_op jit(solution)/shard_map/ppermute | solution.py:439
  31.9 0.0 collective-permute-done.12.rest_2_
  31.9 0.5 %collective-permute-start.6 = (f32[64,256]{1,0:T(8,128)S(1)}, f32[64,256]{1,0:T(8,128)S(1)}, u32[]{:S(2)}, u32[]{:S(2)}) collective-permute-start(f32[64,256]{1,0:T(8,128)S(1)} %right.1.rest_0_), channel_id=1, source_target_pairs={{0,8},{4,20},{8,0},{12,28},{16,24},{20,4},{24,16},{28,12},{1,9},{5... | collective-permute-start | bytes 196616 | tf_op jit(solution)/shard_map/ppermute | solution.py:438
  32.4 3.5 %solve.1.basis = f32[64,256]{1,0:T(8,128)S(1)} custom-call(f32[64,256]{1,0:T(8,128)S(1)} %add.10.a_ref.left_a, f32[64,256]{1,0:T(8,128)S(1)} %collective-permute-done.2.b_ref.left_b), custom_call_target="tpu_custom_call" | custom-call | flops 1073741824 | bytes 1048576 | tf_op jit(solution)/shard_map/solve/pallas_call | solution.py:287
  35.9 0.0 collective-permute-done.10.rest_0_
  35.9 0.0 collective-permute-done.11.rest_1_
  35.9 0.8 %shard_map.79 = f32[256,256]{1,0:T(8,128)} custom-call(f32[256,256]{1,0:T(8,128)S(1)} %collective-permute-done.9.relayed.first, f32[256,256]{1,0:T(8,128)S(1)} %collective-permute-done.10.rest_0_, f32[256,256]{1,0:T(8,128)S(1)} %collective-permute-done.11.rest_1_, f32[256,256]{1,0:T(8,128)S(1)} %collective-permute-done.12.rest_2_, ...), custom_call_target="tpu_custom_call" | custom-call | tf_op jit(solution)/shard_map/pallas_call | solution.py:218
  36.7 0.0 collective-permute-done.8.rest_1_
  36.7 0.0 copy-done
  36.7 1.4 %shard_map.76 = (f32[256,1024]{1,0:T(8,128)}, f32[1,256,1024]{2,1,0:T(8,128)}) custom-call(f32[64,256]{1,0:T(8,128)S(1)} %solve.1.basis, f32[256,1024]{1,0:T(8,128)S(1)} %copy-done, f32[64,256]{1,0:T(8,128)S(1)} %right.1.rest_0_, f32[64,256]{1,0:T(8,128)S(1)} %collective-permute-done.8.rest_1_, f32[256,512]{1,0:T(8,128)S(1)} %get-tuple-element.28.mine.rest_2_, ...), custom_call_target="tpu_custom_call" | custom-call | tf_op jit(solution)/shard_map/pallas_call | solution.py:375
  38.1 0.0 collective-permute-done.7.rest_1_
  38.2 0.0 collective-permute-done.6.rest_0_
  38.2 1.4 %shard_map.77 = (f32[256,1024]{1,0:T(8,128)}, f32[1,256,1024]{2,1,0:T(8,128)}) custom-call(f32[64,256]{1,0:T(8,128)S(1)} %solve.1.basis, f32[256,1024]{1,0:T(8,128)S(1)} %copy-done, f32[64,256]{1,0:T(8,128)S(1)} %collective-permute-done.6.rest_0_, f32[64,256]{1,0:T(8,128)S(1)} %collective-permute-done.7.rest_1_, ...), custom_call_target="tpu_custom_call", output_to_operand_aliasing={{0}: (6, {}), {1}: (7, {})} | custom-call | tf_op jit(solution)/shard_map/pallas_call | solution.py:375
  (4 shorter events, 0.1 us)
Async XLA Ops:
  0.6 2.4 %copy-start.1 = (f32[1,256,1024]{2,1,0:T(8,128)S(1)}, f32[1,256,1024]{2,1,0:T(8,128)}, u32[]{:S(2)}) copy-start(f32[1,256,1024]{2,1,0:T(8,128)} %err.1) | copy-start | bytes 3145732
  3.8 2.1 %collective-permute-start.3 = (f32[256,512]{1,0:T(8,128)S(1)}, f32[256,512]{1,0:T(8,128)S(1)}, u32[]{:S(2)}, u32[]{:S(2)}) collective-permute-start(f32[256,512]{1,0:T(8,128)S(1)} %get-tuple-element.27.theirs.rest_3_), channel_id=1, source_target_pairs={{0,4},{4,0},{8,12},{12,8},{16,20},{20,16},{24,28},{28,24},{1,5},{5... | collective-permute-start | bytes 1572872 | tf_op jit(solution)/shard_map/ppermute | solution.py:409
  6.0 12.1 %copy-start.2 = (f32[1024,64]{0,1:T(8,128)S(1)}, f32[1024,64]{0,1:T(8,128)}, u32[]{:S(2)}) copy-start(f32[1024,64]{0,1:T(8,128)} %param.9) | copy-start | bytes 786436
  6.0 7.3 %collective-permute-start.4 = (f32[256,256]{1,0:T(8,128)S(1)}, f32[256,256]{1,0:T(8,128)S(1)}, u32[]{:S(2)}, u32[]{:S(2)}) collective-permute-start(f32[256,256]{1,0:T(8,128)S(1)} %get-tuple-element.30), channel_id=1, source_target_pairs={{0,8},{4,20},{8,0},{12,28},{16,24},{20,4},{24,16},{28,12},{1,9},{5... | collective-permute-start | bytes 786440 | tf_op jit(solution)/shard_map/ppermute | solution.py:412
  8.9 14.7 %collective-permute-start.9 = (f32[256,256]{1,0:T(8,128)S(1)}, f32[256,256]{1,0:T(8,128)S(1)}, u32[]{:S(2)}, u32[]{:S(2)}) collective-permute-start(f32[256,256]{1,0:T(8,128)S(1)} %get-tuple-element.35), channel_id=1, source_target_pairs={{0,1},{1,3},{2,0},{3,2},{4,5},{5,7},{6,4},{7,6},{8,9},{9,11},{10,8... | collective-permute-start | bytes 786440 | tf_op jit(solution)/shard_map/ppermute | solution.py:405
  13.3 16.8 %collective-permute-start.5 = (f32[256,256]{1,0:T(8,128)S(1)}, f32[256,256]{1,0:T(8,128)S(1)}, u32[]{:S(2)}, u32[]{:S(2)}) collective-permute-start(f32[256,256]{1,0:T(8,128)S(1)} %add.11.total_a), channel_id=1, source_target_pairs={{0,16},{4,12},{8,24},{12,4},{16,0},{20,28},{24,8},{28,20},{1,17},{... | collective-permute-start | bytes 786440 | tf_op jit(solution)/shard_map/ppermute | solution.py:416
  16.4 15.5 %collective-permute-start.12 = (f32[256,256]{1,0:T(8,128)S(1)}, f32[256,256]{1,0:T(8,128)S(1)}, u32[]{:S(2)}, u32[]{:S(2)}) collective-permute-start(f32[256,256]{1,0:T(8,128)S(1)} %get-tuple-element.39), channel_id=1, source_target_pairs={{0,1},{1,0},{2,3},{3,2},{4,5},{5,4},{6,7},{7,6},{8,9},{9,8},{10,11... | collective-permute-start | bytes 786440 | tf_op jit(solution)/shard_map/ppermute | solution.py:405
  18.6 5.7 %collective-permute-start = (f32[64,256]{1,0:T(8,128)S(1)}, f32[64,256]{1,0:T(8,128)S(1)}, u32[]{:S(2)}, u32[]{:S(2)}) collective-permute-start(f32[64,256]{1,0:T(8,128)S(1)} %left.1), channel_id=1, source_target_pairs={{0,16},{4,12},{8,24},{12,4},{16,0},{20,28},{24,8},{28,20},{1,17},{... | collective-permute-start | bytes 196616 | tf_op jit(solution)/shard_map/ppermute | solution.py:413
  19.2 16.7 %collective-permute-start.10 = (f32[256,256]{1,0:T(8,128)S(1)}, f32[256,256]{1,0:T(8,128)S(1)}, u32[]{:S(2)}, u32[]{:S(2)}) collective-permute-start(f32[256,256]{1,0:T(8,128)S(1)} %get-tuple-element.38.block), channel_id=1, source_target_pairs={{0,3},{3,0},{4,7},{7,4},{8,11},{11,8},{12,15},{15,12},{16,19},{19,... | collective-permute-start | bytes 786440 | tf_op jit(solution)/shard_map/ppermute | solution.py:405
  23.6 12.3 %collective-permute-start.11 = (f32[256,256]{1,0:T(8,128)S(1)}, f32[256,256]{1,0:T(8,128)S(1)}, u32[]{:S(2)}, u32[]{:S(2)}) collective-permute-start(f32[256,256]{1,0:T(8,128)S(1)} %shard_map.78), channel_id=1, source_target_pairs={{1,2},{2,1},{5,6},{6,5},{9,10},{10,9},{13,14},{14,13},{17,18},{18,... | collective-permute-start | bytes 786440 | tf_op jit(solution)/shard_map/ppermute | solution.py:405
  24.3 4.3 %collective-permute-start.1 = (f32[64,256]{1,0:T(8,128)S(1)}, f32[64,256]{1,0:T(8,128)S(1)}, u32[]{:S(2)}, u32[]{:S(2)}) collective-permute-start(f32[64,256]{1,0:T(8,128)S(1)} %add.9), channel_id=1, source_target_pairs={{0,8},{4,20},{8,0},{12,28},{16,24},{20,4},{24,16},{28,12},{1,9},{5... | collective-permute-start | bytes 196616 | tf_op jit(solution)/shard_map/ppermute | solution.py:417
  28.7 1.3 %collective-permute-start.2 = (f32[64,256]{1,0:T(8,128)S(1)}, f32[64,256]{1,0:T(8,128)S(1)}, u32[]{:S(2)}, u32[]{:S(2)}) collective-permute-start(f32[64,256]{1,0:T(8,128)S(1)} %add.10.a_ref.left_a), channel_id=1, source_target_pairs={{0,4},{4,0},{8,12},{12,8},{16,20},{20,16},{24,28},{28,24},{1,5},{5... | collective-permute-start | bytes 196616 | tf_op jit(solution)/shard_map/ppermute | solution.py:418
  30.2 6.5 %copy-start = (f32[256,1024]{1,0:T(8,128)S(1)}, f32[256,1024]{1,0:T(8,128)}, u32[]{:S(2)}) copy-start(f32[256,1024]{1,0:T(8,128)} %wt.5) | copy-start | bytes 3145732
  30.2 6.5 %collective-permute-start.8 = (f32[64,256]{1,0:T(8,128)S(1)}, f32[64,256]{1,0:T(8,128)S(1)}, u32[]{:S(2)}, u32[]{:S(2)}) collective-permute-start(f32[64,256]{1,0:T(8,128)S(1)} %right.1.rest_0_), channel_id=1, source_target_pairs={{0,4},{4,0},{8,12},{12,8},{16,20},{20,16},{24,28},{28,24},{1,5},{5... | collective-permute-start | bytes 196616 | tf_op jit(solution)/shard_map/ppermute | solution.py:437
  30.4 7.7 %collective-permute-start.7 = (f32[64,256]{1,0:T(8,128)S(1)}, f32[64,256]{1,0:T(8,128)S(1)}, u32[]{:S(2)}, u32[]{:S(2)}) collective-permute-start(f32[64,256]{1,0:T(8,128)S(1)} %right.1.rest_0_), channel_id=1, source_target_pairs={{0,12},{4,16},{8,4},{12,24},{16,28},{20,0},{24,20},{28,8},{1,13},{... | collective-permute-start | bytes 196616 | tf_op jit(solution)/shard_map/ppermute | solution.py:439
  31.9 6.3 %collective-permute-start.6 = (f32[64,256]{1,0:T(8,128)S(1)}, f32[64,256]{1,0:T(8,128)S(1)}, u32[]{:S(2)}, u32[]{:S(2)}) collective-permute-start(f32[64,256]{1,0:T(8,128)S(1)} %right.1.rest_0_), channel_id=1, source_target_pairs={{0,8},{4,20},{8,0},{12,28},{16,24},{20,4},{24,16},{28,12},{1,9},{5... | collective-permute-start | bytes 196616 | tf_op jit(solution)/shard_map/ppermute | solution.py:438

commit v6 on v4

--- a/solution.py
+++ b/solution.py
@@ -39,37 +39,26 @@
 
 
 def rounds_of(n):
-    flows = sorted(
-        ((a, b) for a in range(n) for b in range(n) if a != b),
-        key=lambda flow: (abs(flow[0] - flow[1]), flow),
-    )
-
-    def fill(chosen, order):
-        for a, b in list(flows)[::order]:
-            if a not in chosen and all(b != to for to, _ in chosen.values()):
-                chosen[a] = (b, b)
-                flows.remove((a, b))
-        return chosen
-
-    relay, last = {}, {}
-    if n >= 4:
-        for gone in ((0, n - 2), (n - 1, 1), (1, n - 2), (n - 2, 1)):
-            flows.remove(gone)
-        relay = fill({0: (1, n - 2), n - 1: (n - 2, 1)}, -1)
-        last = fill({1: (n - 2, n - 2), n - 2: (1, 1)}, -1)
-    plain = []
-    while flows:
-        plain.append(fill({}, 1))
-    rounds = [relay, last, *plain] if relay else plain
-    if len(rounds) == n - 1 and all(len(one) == n for one in rounds):
-        return rounds, bool(relay)
-    return [{a: ((a + k) % n,) * 2 for a in range(n)} for k in range(1, n)], False
+    if n % 2:
+        return [({a: ((a + k) % n,) * 2 for a in range(n)}, None) for k in range(1, n)]
+    pairs = n // 2
+
+    def member(a, k, parity):
+        return 2 * ((a // 2 + k) % pairs) + parity
+
+    give = [
+        ({a: (a ^ 1, member(a, k, 1 - a % 2)) for a in range(n)}, None) for k in range(1, pairs)
+    ]
+    onward = [
+        ({a: (member(a, k, a % 2),) * 2 for a in range(n)}, k - 1) for k in range(1, pairs)
+    ]
+    return [*give, *onward, ({a: (a ^ 1, a ^ 1) for a in range(n)}, None)]
 
 
 def pick(me, table, n):
     index = jnp.int32(0)
     for a in range(n):
-        index = jnp.where(me == a, table[a][1] if a in table else a, index)
+        index = jnp.where(me == a, table[a][1] if table else a, index)
     return index
 
 
@@ -196,27 +185,16 @@
     )(acts_t, err, *rows)
 
 
-def is_between(n_tensor):
-    me = lax.axis_index("tensor")
-    return ((me == 1) | (me == n_tensor - 2)).astype(F32)
-
-
-def onward_kernel(n_tensor, block, relayed, out):
-    out[...] = block[...] + is_between(n_tensor) * relayed[...]
-
-
-def gather_kernel(relays, first, *rest):
-    total = first[...]
-    if relays:
-        total = total * (1.0 - is_between(relays))
-    for part in rest[:-1]:
+def sum_kernel(*refs):
+    total = refs[0][...]
+    for part in refs[1:-1]:
         total = total + part[...]
-    rest[-1][...] = total
-
-
-def summed(kernel, *parts):
-    return pl.pallas_call(
-        kernel,
+    refs[-1][...] = total
+
+
+def summed(*parts):
+    return pl.pallas_call(
+        sum_kernel,
         out_shape=jax.ShapeDtypeStruct(parts[0].shape, F32),
         in_specs=[VMEM] * len(parts),
         out_specs=VMEM,
@@ -390,51 +368,49 @@
     )(basis, wt, *rights, *merged, *kept)
 
 
-def send(x, axis, pairs):
-    return lax.ppermute(x, axis, pairs)
-
-
 def step(acts, out_grad, weight, error, start_q):
     replicas = lax.axis_size("dp")
     n_tensor = lax.axis_size("tensor")
     bits = [1 << b for b in range(1, replicas.bit_length() - 1)]
     pair = swap(1, 1, replicas)
 
-    table, relays = rounds_of(n_tensor)
-    tables = [table[0], {}, *table[1:]]
-    acts_t, halves, first, rows = first_of(acts, out_grad, weight, tables)
+    rounds = rounds_of(n_tensor)
+    tables = [table for table, _ in rounds]
+    acts_t, halves, first, rows = first_of(
+        acts, out_grad, weight, [tables[0], {}, *tables[1:]]
+    )
 
     def across(block, n):
-        return send(block, "tensor", [(a, to) for a, (to, _) in sorted(table[n].items())])
+        return lax.ppermute(block, "tensor", [(a, to) for a, (to, _) in tables[n].items()])
 
     received = [across(first, 0)]
     theirs, mine = merged_of(acts_t, error, rows)
-    came = send(theirs, "dp", pair)
+    came = lax.ppermute(theirs, "dp", pair)
     left = left_of(start_q.T, theirs, mine)
     total, give = begin(mine, came, bits)
-    came = send(give, "dp", swap(bits[0], bits[-1], replicas))
-    left = left + send(left, "dp", swap(bits[-1], bits[0], replicas))
+    came = lax.ppermute(give, "dp", swap(bits[0], bits[-1], replicas))
+    left = left + lax.ppermute(left, "dp", swap(bits[-1], bits[0], replicas))
     for n, (one, other) in enumerate(zip(bits[1:], bits[-2::-1]), 2):
         total = total + came
-        came = send(total, "dp", swap(one, other, replicas))
-        left = left + send(left, "dp", swap(other, one, replicas))
-    left_came = send(left, "dp", pair)
+        came = lax.ppermute(total, "dp", swap(one, other, replicas))
+        left = left + lax.ppermute(left, "dp", swap(other, one, replicas))
+    left_came = lax.ppermute(left, "dp", pair)
 
     blocks = rest_of(halves, rows[1:])
     for n in range(1, n_tensor - 1):
-        block = blocks[n]
-        if relays and n == 1:
-            onward = functools.partial(onward_kernel, n_tensor)
-            block = summed(onward, block, received[0])
+        block, adds = blocks[n], rounds[n][1]
+        if adds is not None:
+            block = summed(block, received[adds])
         received.append(across(block, n))
-    gather = functools.partial(gather_kernel, n_tensor if relays else None)
-    input_grad = summed(gather, *received, blocks[0])
+    relayed = {adds for _, adds in rounds}
+    final = [one for n, one in enumerate(received) if n not in relayed]
+    input_grad = summed(blocks[0], *final)
 
     basis = solve(left, left_came, replicas)
     right = right_of(left, left_came, total, came, replicas)
-    beside = send(right, "dp", swap(bits[0], bits[-1], replicas))
-    diagonal = send(right, "dp", swap(bits[0] | 1, bits[-1] | 1, replicas))
-    across_pair = send(right, "dp", pair)
+    beside = lax.ppermute(right, "dp", swap(bits[0], bits[-1], replicas))
+    diagonal = lax.ppermute(right, "dp", swap(bits[0] | 1, bits[-1] | 1, replicas))
+    across_pair = lax.ppermute(right, "dp", pair)
     pieces = ((True, True), (True, False), (False, True))
     rights = (right, beside, across_pair)
     kept = back(pieces, bits, basis, weight, rights, (mine, mine, theirs))

time: 37.7 us -> 37.8 us (level)
  no operation moved by 1% of the time
where the time goes in v6:
time: 37.8 us; the launch traced here: 37.6 us
  starting transfers between devices  16.6 us (44%)
  Pallas kernels  11.8 us (31%)
  waiting for transfers between devices  8.35 us (22%)
  between operations  0.76 us (2%)
    ppermute x3, starting transfers between devices, across(): lax.ppermute(block, 'tensor', [(a, to) for a, (to, _) in tables[n].items()])  6.36 us
    pallas_call x1, Pallas kernels, solve(): pl.pallas_call(functools.partial(solve_kernel, replicas), out_shape=jax.S...  3.49 us
    ppermute x1, starting transfers between devices, step(): came = lax.ppermute(give, 'dp', swap(bits[0], bits[-1], replicas))  2.9 us
    ppermute x1, waiting for transfers between devices, step(): came = lax.ppermute(give, 'dp', swap(bits[0], bits[-1], replicas))  2.78 us
    ppermute x1, waiting for transfers between devices, step(): left = left + lax.ppermute(left, 'dp', swap(other, one, replicas))  2.77 us
    pallas_call x2, Pallas kernels, back(): pl.pallas_call(functools.partial(back_kernel, pieces, bits), out_shape=[j...  2.67 us
    pallas_call x1, Pallas kernels, first_of(): pl.pallas_call(functools.partial(first_kernel, tables, n, chunks), out_sh...  2.27 us
    ppermute x1, starting transfers between devices, step(): came = lax.ppermute(total, 'dp', swap(one, other, replicas))  2.11 us
  transfers between devices with their start and end apart: 12, of which 4 were waited for; matrix products, arithmetic and copies ran while one was open for 0% of the time, Pallas kernels for 20%

profile of v6, /device:TPU:0, one launch (start us, length us, event | category | flops | bytes accessed | tf_op | source)
XLA Modules:
  0.0 37.6 jit_solution(15071155122403858009)
XLA Ops:
  0.6 0.0 copy-start.1
  0.6 2.3 %first.1 = (bf16[256,1024]{1,0:T(8,128)(2,1)S(1)}, bf16[256,1024]{1,0:T(8,128)(2,1)S(1)}, bf16[256,1024]{1,0:T(8,128)(2,1)S(1)}, f32[256,256]{1,0:T(8,128)S(1)},...) custom-call(bf16[1024,256]{1,0:T(8,128)(2,1)} %acts.1, ...), custom_call_target="tpu_custom_call" | custom-call | flops 268435456 | bytes 4194304 | tf_op jit(solution)/shard_map/first/pallas_call | solution.py:113
  2.9 0.1 copy-done.1
  3.1 0.0 copy-start.2
  3.1 0.7 %merged.1 = (f32[256,512]{1,0:T(8,128)S(1)}, f32[256,512]{1,0:T(8,128)S(1)}) custom-call(bf16[256,1024]{1,0:T(8,128)(2,1)S(1)} %get-tuple-element.22.acts_t, f32[1,256,1024]{2,1,0:T(8,128)S(1)} %copy-done.1, bf16[256,1024]{1,0:T(8,128)(2,1)S(1)} %get-tuple-element.23.rest_0_, bf16[256,1024]{1,0:T(8,128)(2,1)S(1)} %get-tuple-element.24.rest_1_.rest_0_, ...), custom_call_target="tpu_custom_call" | custom-call | flops 536870912 | bytes 4194304 | tf_op jit(solution)/shard_map/merged/pallas_call | solution.py:175
  3.8 0.6 %collective-permute-start.3 = (f32[256,512]{1,0:T(8,128)S(1)}, f32[256,512]{1,0:T(8,128)S(1)}, u32[]{:S(2)}, u32[]{:S(2)}) collective-permute-start(f32[256,512]{1,0:T(8,128)S(1)} %get-tuple-element.27.theirs.rest_5_.rest_1_), channel_id=1, source_target_pairs={{0,4},{4,0},{8,12},{12,8},{16,20},{20,16},{24,28},{28,24},{1,5},{5... | collective-permute-start | bytes 1572872 | tf_op jit(solution)/shard_map/ppermute | solution.py:388
  4.3 1.5 %collective-permute-done.3.came = f32[256,512]{1,0:T(8,128)S(1)} collective-permute-done((f32[256,512]{1,0:T(8,128)S(1)}, f32[256,512]{1,0:T(8,128)S(1)}, u32[]{:S(2)}, u32[]{:S(2)}) %collective-permute-start.3) | collective-permute-done | bytes 524320 | tf_op jit(solution)/shard_map/ppermute | solution.py:388
  5.9 0.1 begin.1
  6.0 2.9 %collective-permute-start.4 = (f32[256,256]{1,0:T(8,128)S(1)}, f32[256,256]{1,0:T(8,128)S(1)}, u32[]{:S(2)}, u32[]{:S(2)}) collective-permute-start(f32[256,256]{1,0:T(8,128)S(1)} %get-tuple-element.30), channel_id=1, source_target_pairs={{0,8},{4,20},{8,0},{12,28},{16,24},{20,4},{24,16},{28,12},{1,9},{5... | collective-permute-start | bytes 786440 | tf_op jit(solution)/shard_map/ppermute | solution.py:391
  8.9 1.6 %collective-permute-start.9 = (f32[256,256]{1,0:T(8,128)S(1)}, f32[256,256]{1,0:T(8,128)S(1)}, u32[]{:S(2)}, u32[]{:S(2)}) collective-permute-start(f32[256,256]{1,0:T(8,128)S(1)} %get-tuple-element.39), channel_id=1, source_target_pairs={{0,1},{1,0},{2,3},{3,2},{4,5},{5,4},{6,7},{7,6},{8,9},{9,8},{10,11... | collective-permute-start | bytes 786440 | tf_op jit(solution)/shard_map/ppermute | solution.py:384
  10.4 2.8 %collective-permute-done.4 = f32[256,256]{1,0:T(8,128)S(1)} collective-permute-done((f32[256,256]{1,0:T(8,128)S(1)}, f32[256,256]{1,0:T(8,128)S(1)}, u32[]{:S(2)}, u32[]{:S(2)}) %collective-permute-start.4) | collective-permute-done | bytes 262176 | tf_op jit(solution)/shard_map/ppermute | solution.py:391
  13.2 2.1 %collective-permute-start.5 = (f32[256,256]{1,0:T(8,128)S(1)}, f32[256,256]{1,0:T(8,128)S(1)}, u32[]{:S(2)}, u32[]{:S(2)}) collective-permute-start(f32[256,256]{1,0:T(8,128)S(1)} %add.11.total_a), channel_id=1, source_target_pairs={{0,16},{4,12},{8,24},{12,4},{16,0},{20,28},{24,8},{28,20},{1,17},{... | collective-permute-start | bytes 786440 | tf_op jit(solution)/shard_map/ppermute | solution.py:395
  15.4 0.0 copy-done.2
  15.4 0.6 %left.1 = f32[64,256]{1,0:T(8,128)S(1)} custom-call(f32[64,1024]{1,0:T(8,128)S(1)} %bitcast.1, f32[256,512]{1,0:T(8,128)S(1)} %get-tuple-element.27.theirs.rest_5_.rest_1_, f32[256,512]{1,0:T(8,128)S(1)} %get-tuple-element.28.mine.rest_3_.rest_4_), custom_call_target="tpu_custom_call" | custom-call | tf_op jit(solution)/shard_map/left/pallas_call | solution.py:214
  16.0 0.1 collective-permute-start
  16.0 1.0 %rest.1 = (f32[256,256]{1,0:T(8,128)S(1)}, f32[256,256]{1,0:T(8,128)S(1)}, f32[256,256]{1,0:T(8,128)S(1)}) custom-call(bf16[256,1024]{1,0:T(8,128)(2,1)S(1)} %get-tuple-element.35.high, bf16[256,1024]{1,0:T(8,128)(2,1)S(1)} %get-tuple-element.36.low, bf16[256,1024]{1,0:T(8,128)(2,1)S(1)} %get-tuple-element.24.rest_1_.rest_0_, ...), custom_call_target="tpu_custom_call" | custom-call | flops 805306368 | bytes 4194304 | tf_op jit(solution)/shard_map/rest/pallas_call | solution.py:147
  17.1 2.1 %collective-permute-start.11 = (f32[256,256]{1,0:T(8,128)S(1)}, f32[256,256]{1,0:T(8,128)S(1)}, u32[]{:S(2)}, u32[]{:S(2)}) collective-permute-start(f32[256,256]{1,0:T(8,128)S(1)} %get-tuple-element.40), channel_id=1, source_target_pairs={{0,1},{1,0},{2,3},{3,2},{4,5},{5,4},{6,7},{7,6},{8,9},{9,8},{10,11... | collective-permute-start | bytes 786440 | tf_op jit(solution)/shard_map/ppermute | solution.py:384
  19.2 0.0 collective-permute-done.9.refs_1_
  19.2 2.7 %collective-permute-start.10 = (f32[256,256]{1,0:T(8,128)S(1)}, f32[256,256]{1,0:T(8,128)S(1)}, u32[]{:S(2)}, u32[]{:S(2)}) collective-permute-start(f32[256,256]{1,0:T(8,128)S(1)} %shard_map.78), channel_id=1, source_target_pairs={{0,2},{1,3},{2,0},{3,1},{4,6},{5,7},{6,4},{7,5},{8,10},{9,11},{10,... | collective-permute-start | bytes 786440 | tf_op jit(solution)/shard_map/ppermute | solution.py:384
  21.9 0.0 collective-permute-done
  21.9 1.6 %collective-permute-start.1 = (f32[64,256]{1,0:T(8,128)S(1)}, f32[64,256]{1,0:T(8,128)S(1)}, u32[]{:S(2)}, u32[]{:S(2)}) collective-permute-start(f32[64,256]{1,0:T(8,128)S(1)} %add.9), channel_id=1, source_target_pairs={{0,8},{4,20},{8,0},{12,28},{16,24},{20,4},{24,16},{28,12},{1,9},{5... | collective-permute-start | bytes 196616 | tf_op jit(solution)/shard_map/ppermute | solution.py:396
  23.5 2.8 %collective-permute-done.1 = f32[64,256]{1,0:T(8,128)S(1)} collective-permute-done((f32[64,256]{1,0:T(8,128)S(1)}, f32[64,256]{1,0:T(8,128)S(1)}, u32[]{:S(2)}, u32[]{:S(2)}) %collective-permute-start.1) | collective-permute-done | bytes 65568 | tf_op jit(solution)/shard_map/ppermute | solution.py:396
  26.2 0.1 collective-permute-start.2
  26.3 1.2 %collective-permute-done.2.b_ref.left_b = f32[64,256]{1,0:T(8,128)S(1)} collective-permute-done((f32[64,256]{1,0:T(8,128)S(1)}, f32[64,256]{1,0:T(8,128)S(1)}, u32[]{:S(2)}, u32[]{:S(2)}) %collective-permute-start.2) | collective-permute-done | bytes 65568 | tf_op jit(solution)/shard_map/ppermute | solution.py:397
  27.6 0.0 collective-permute-done.5.total_b
  27.6 0.2 right.1.rest_0_
  27.8 0.0 copy-start
  27.8 0.2 collective-permute-start.8
  28.0 1.5 %collective-permute-start.7 = (f32[64,256]{1,0:T(8,128)S(1)}, f32[64,256]{1,0:T(8,128)S(1)}, u32[]{:S(2)}, u32[]{:S(2)}) collective-permute-start(f32[64,256]{1,0:T(8,128)S(1)} %right.1.rest_0_), channel_id=1, source_target_pairs={{0,8},{4,20},{8,0},{12,28},{16,24},{20,4},{24,16},{28,12},{1,9},{5... | collective-permute-start | bytes 196616 | tf_op jit(solution)/shard_map/ppermute | solution.py:411
  29.5 1.2 %collective-permute-start.6 = (f32[64,256]{1,0:T(8,128)S(1)}, f32[64,256]{1,0:T(8,128)S(1)}, u32[]{:S(2)}, u32[]{:S(2)}) collective-permute-start(f32[64,256]{1,0:T(8,128)S(1)} %right.1.rest_0_), channel_id=1, source_target_pairs={{0,12},{4,16},{8,4},{12,24},{16,28},{20,0},{24,20},{28,8},{1,13},{... | collective-permute-start | bytes 196616 | tf_op jit(solution)/shard_map/ppermute | solution.py:412
  30.7 3.5 %solve.1.basis = f32[64,256]{1,0:T(8,128)S(1)} custom-call(f32[64,256]{1,0:T(8,128)S(1)} %add.10.a_ref.left_a, f32[64,256]{1,0:T(8,128)S(1)} %collective-permute-done.2.b_ref.left_b), custom_call_target="tpu_custom_call" | custom-call | flops 1073741824 | bytes 1048576 | tf_op jit(solution)/shard_map/solve/pallas_call | solution.py:265
  34.2 0.0 collective-permute-done.11.refs_2_
  34.2 0.0 collective-permute-done.10.refs_1_
  34.2 0.7 %shard_map.79 = f32[256,256]{1,0:T(8,128)} custom-call(f32[256,256]{1,0:T(8,128)S(1)} %get-tuple-element.37.refs_0_, f32[256,256]{1,0:T(8,128)S(1)} %collective-permute-done.10.refs_1_, f32[256,256]{1,0:T(8,128)S(1)} %collective-permute-done.11.refs_2_), custom_call_target="tpu_custom_call" | custom-call | tf_op jit(solution)/shard_map/pallas_call | solution.py:196
  34.9 0.0 collective-permute-done.8.rest_2_
  34.9 0.0 collective-permute-done.7.rest_1_
  35.0 0.0 copy-done
  35.0 1.5 %shard_map.76 = (f32[256,1024]{1,0:T(8,128)}, f32[1,256,1024]{2,1,0:T(8,128)}) custom-call(f32[64,256]{1,0:T(8,128)S(1)} %solve.1.basis, f32[256,1024]{1,0:T(8,128)S(1)} %copy-done, f32[64,256]{1,0:T(8,128)S(1)} %right.1.rest_0_, f32[64,256]{1,0:T(8,128)S(1)} %collective-permute-done.7.rest_1_, f32[64,256]{1,0:T(8,128)S(1)} %collective-permute-done.8.rest_2_, ...), custom_call_target="tpu_custom_call" | custom-call | tf_op jit(solution)/shard_map/pallas_call | solution.py:353
  36.5 0.0 collective-permute-done.6.rest_0_
  36.5 1.1 %shard_map.77 = (f32[256,1024]{1,0:T(8,128)}, f32[1,256,1024]{2,1,0:T(8,128)}) custom-call(f32[64,256]{1,0:T(8,128)S(1)} %solve.1.basis, f32[256,1024]{1,0:T(8,128)S(1)} %copy-done, f32[64,256]{1,0:T(8,128)S(1)} %collective-permute-done.6.rest_0_, ...), custom_call_target="tpu_custom_call", output_to_operand_aliasing={{0}: (4, {}), {1}: (5, {})} | custom-call | tf_op jit(solution)/shard_map/pallas_call | solution.py:353
  (4 shorter events, 0.1 us)
Async XLA Ops:
  0.6 2.4 %copy-start.1 = (f32[1,256,1024]{2,1,0:T(8,128)S(1)}, f32[1,256,1024]{2,1,0:T(8,128)}, u32[]{:S(2)}) copy-start(f32[1,256,1024]{2,1,0:T(8,128)} %err.1) | copy-start | bytes 3145732
  3.1 12.3 %copy-start.2 = (f32[1024,64]{0,1:T(8,128)S(1)}, f32[1024,64]{0,1:T(8,128)}, u32[]{:S(2)}) copy-start(f32[1024,64]{0,1:T(8,128)} %param.9) | copy-start | bytes 786436
  3.8 2.1 %collective-permute-start.3 = (f32[256,512]{1,0:T(8,128)S(1)}, f32[256,512]{1,0:T(8,128)S(1)}, u32[]{:S(2)}, u32[]{:S(2)}) collective-permute-start(f32[256,512]{1,0:T(8,128)S(1)} %get-tuple-element.27.theirs.rest_5_.rest_1_), channel_id=1, source_target_pairs={{0,4},{4,0},{8,12},{12,8},{16,20},{20,16},{24,28},{28,24},{1,5},{5... | collective-permute-start | bytes 1572872 | tf_op jit(solution)/shard_map/ppermute | solution.py:388
  6.0 7.3 %collective-permute-start.4 = (f32[256,256]{1,0:T(8,128)S(1)}, f32[256,256]{1,0:T(8,128)S(1)}, u32[]{:S(2)}, u32[]{:S(2)}) collective-permute-start(f32[256,256]{1,0:T(8,128)S(1)} %get-tuple-element.30), channel_id=1, source_target_pairs={{0,8},{4,20},{8,0},{12,28},{16,24},{20,4},{24,16},{28,12},{1,9},{5... | collective-permute-start | bytes 786440 | tf_op jit(solution)/shard_map/ppermute | solution.py:391
  8.9 10.3 %collective-permute-start.9 = (f32[256,256]{1,0:T(8,128)S(1)}, f32[256,256]{1,0:T(8,128)S(1)}, u32[]{:S(2)}, u32[]{:S(2)}) collective-permute-start(f32[256,256]{1,0:T(8,128)S(1)} %get-tuple-element.39), channel_id=1, source_target_pairs={{0,1},{1,0},{2,3},{3,2},{4,5},{5,4},{6,7},{7,6},{8,9},{9,8},{10,11... | collective-permute-start | bytes 786440 | tf_op jit(solution)/shard_map/ppermute | solution.py:384
  13.2 14.3 %collective-permute-start.5 = (f32[256,256]{1,0:T(8,128)S(1)}, f32[256,256]{1,0:T(8,128)S(1)}, u32[]{:S(2)}, u32[]{:S(2)}) collective-permute-start(f32[256,256]{1,0:T(8,128)S(1)} %add.11.total_a), channel_id=1, source_target_pairs={{0,16},{4,12},{8,24},{12,4},{16,0},{20,28},{24,8},{28,20},{1,17},{... | collective-permute-start | bytes 786440 | tf_op jit(solution)/shard_map/ppermute | solution.py:395
  16.0 5.9 %collective-permute-start = (f32[64,256]{1,0:T(8,128)S(1)}, f32[64,256]{1,0:T(8,128)S(1)}, u32[]{:S(2)}, u32[]{:S(2)}) collective-permute-start(f32[64,256]{1,0:T(8,128)S(1)} %left.1), channel_id=1, source_target_pairs={{0,16},{4,12},{8,24},{12,4},{16,0},{20,28},{24,8},{28,20},{1,17},{... | collective-permute-start | bytes 196616 | tf_op jit(solution)/shard_map/ppermute | solution.py:392
  17.1 17.1 %collective-permute-start.11 = (f32[256,256]{1,0:T(8,128)S(1)}, f32[256,256]{1,0:T(8,128)S(1)}, u32[]{:S(2)}, u32[]{:S(2)}) collective-permute-start(f32[256,256]{1,0:T(8,128)S(1)} %get-tuple-element.40), channel_id=1, source_target_pairs={{0,1},{1,0},{2,3},{3,2},{4,5},{5,4},{6,7},{7,6},{8,9},{9,8},{10,11... | collective-permute-start | bytes 786440 | tf_op jit(solution)/shard_map/ppermute | solution.py:384
  19.2 15.0 %collective-permute-start.10 = (f32[256,256]{1,0:T(8,128)S(1)}, f32[256,256]{1,0:T(8,128)S(1)}, u32[]{:S(2)}, u32[]{:S(2)}) collective-permute-start(f32[256,256]{1,0:T(8,128)S(1)} %shard_map.78), channel_id=1, source_target_pairs={{0,2},{1,3},{2,0},{3,1},{4,6},{5,7},{6,4},{7,5},{8,10},{9,11},{10,... | collective-permute-start | bytes 786440 | tf_op jit(solution)/shard_map/ppermute | solution.py:384
  21.9 4.3 %collective-permute-start.1 = (f32[64,256]{1,0:T(8,128)S(1)}, f32[64,256]{1,0:T(8,128)S(1)}, u32[]{:S(2)}, u32[]{:S(2)}) collective-permute-start(f32[64,256]{1,0:T(8,128)S(1)} %add.9), channel_id=1, source_target_pairs={{0,8},{4,20},{8,0},{12,28},{16,24},{20,4},{24,16},{28,12},{1,9},{5... | collective-permute-start | bytes 196616 | tf_op jit(solution)/shard_map/ppermute | solution.py:396
  26.2 1.3 %collective-permute-start.2 = (f32[64,256]{1,0:T(8,128)S(1)}, f32[64,256]{1,0:T(8,128)S(1)}, u32[]{:S(2)}, u32[]{:S(2)}) collective-permute-start(f32[64,256]{1,0:T(8,128)S(1)} %add.10.a_ref.left_a), channel_id=1, source_target_pairs={{0,4},{4,0},{8,12},{12,8},{16,20},{20,16},{24,28},{28,24},{1,5},{5... | collective-permute-start | bytes 196616 | tf_op jit(solution)/shard_map/ppermute | solution.py:397
  27.8 7.2 %copy-start = (f32[256,1024]{1,0:T(8,128)S(1)}, f32[256,1024]{1,0:T(8,128)}, u32[]{:S(2)}) copy-start(f32[256,1024]{1,0:T(8,128)} %wt.5) | copy-start | bytes 3145732
  27.8 7.2 %collective-permute-start.8 = (f32[64,256]{1,0:T(8,128)S(1)}, f32[64,256]{1,0:T(8,128)S(1)}, u32[]{:S(2)}, u32[]{:S(2)}) collective-permute-start(f32[64,256]{1,0:T(8,128)S(1)} %right.1.rest_0_), channel_id=1, source_target_pairs={{0,4},{4,0},{8,12},{12,8},{16,20},{20,16},{24,28},{28,24},{1,5},{5... | collective-permute-start | bytes 196616 | tf_op jit(solution)/shard_map/ppermute | solution.py:413
  28.0 7.0 %collective-permute-start.7 = (f32[64,256]{1,0:T(8,128)S(1)}, f32[64,256]{1,0:T(8,128)S(1)}, u32[]{:S(2)}, u32[]{:S(2)}) collective-permute-start(f32[64,256]{1,0:T(8,128)S(1)} %right.1.rest_0_), channel_id=1, source_target_pairs={{0,8},{4,20},{8,0},{12,28},{16,24},{20,4},{24,16},{28,12},{1,9},{5... | collective-permute-start | bytes 196616 | tf_op jit(solution)/shard_map/ppermute | solution.py:411
  29.5 7.0 %collective-permute-start.6 = (f32[64,256]{1,0:T(8,128)S(1)}, f32[64,256]{1,0:T(8,128)S(1)}, u32[]{:S(2)}, u32[]{:S(2)}) collective-permute-start(f32[64,256]{1,0:T(8,128)S(1)} %right.1.rest_0_), channel_id=1, source_target_pairs={{0,12},{4,16},{8,4},{12,24},{16,28},{20,0},{24,20},{28,8},{1,13},{... | collective-permute-start | bytes 196616 | tf_op jit(solution)/shard_map/ppermute | solution.py:412

commit v7 on v6

--- a/solution.py
+++ b/solution.py
@@ -408,15 +408,14 @@
 
     basis = solve(left, left_came, replicas)
     right = right_of(left, left_came, total, came, replicas)
+    across_pair = lax.ppermute(right, "dp", pair)
     beside = lax.ppermute(right, "dp", swap(bits[0], bits[-1], replicas))
     diagonal = lax.ppermute(right, "dp", swap(bits[0] | 1, bits[-1] | 1, replicas))
-    across_pair = lax.ppermute(right, "dp", pair)
-    pieces = ((True, True), (True, False), (False, True))
-    rights = (right, beside, across_pair)
-    kept = back(pieces, bits, basis, weight, rights, (mine, mine, theirs))
-    new_weight, new_error = back(
-        ((False, False),), bits, basis, weight, (diagonal,), (theirs,), *kept
-    )
+    merged = (mine, theirs)
+    pieces, rights = ((True, True), (False, True)), (right, across_pair)
+    kept = back(pieces, bits, basis, weight, rights, merged)
+    pieces, rights = ((True, False), (False, False)), (beside, diagonal)
+    new_weight, new_error = back(pieces, bits, basis, weight, rights, merged, *kept)
     return (new_weight, new_error, input_grad)
 
 

time: 37.8 us -> 37.3 us (0.987)
  starting transfers between devices: 16.6 us -> 15.9 us
    ppermute x1, starting transfers between devices: 1.49 us -> 0.53 us  [step(): beside = lax.ppermute(right, 'dp', swap(bits[0], bits[-1], replicas))]
where the time goes in v7:
time: 37.3 us; the launch traced here: 37.1 us
  starting transfers between devices  15.9 us (43%)
  Pallas kernels  11.9 us (32%)
  waiting for transfers between devices  8.35 us (22%)
  between operations  0.76 us (2%)
    ppermute x3, starting transfers between devices, across(): lax.ppermute(block, 'tensor', [(a, to) for a, (to, _) in tables[n].items()])  6.36 us
    pallas_call x1, Pallas kernels, solve(): pl.pallas_call(functools.partial(solve_kernel, replicas), out_shape=jax.S...  3.49 us
    ppermute x1, starting transfers between devices, step(): came = lax.ppermute(give, 'dp', swap(bits[0], bits[-1], replicas))  2.9 us
    pallas_call x2, Pallas kernels, back(): pl.pallas_call(functools.partial(back_kernel, pieces, bits), out_shape=[j...  2.83 us
    ppermute x1, waiting for transfers between devices, step(): came = lax.ppermute(give, 'dp', swap(bits[0], bits[-1], replicas))  2.78 us
    ppermute x1, waiting for transfers between devices, step(): left = left + lax.ppermute(left, 'dp', swap(other, one, replicas))  2.77 us
    pallas_call x1, Pallas kernels, first_of(): pl.pallas_call(functools.partial(first_kernel, tables, n, chunks), out_sh...  2.27 us
    ppermute x1, starting transfers between devices, step(): came = lax.ppermute(total, 'dp', swap(one, other, replicas))  2.11 us
  transfers between devices with their start and end apart: 12, of which 4 were waited for; matrix products, arithmetic and copies ran while one was open for 0% of the time, Pallas kernels for 20%

profile of v7, /device:TPU:0, one launch (start us, length us, event | category | flops | bytes accessed | tf_op | source)
XLA Modules:
  0.0 37.1 jit_solution(6512733594593438666)
XLA Ops:
  0.6 0.0 copy-start.1
  0.6 2.3 %first.1 = (bf16[256,1024]{1,0:T(8,128)(2,1)S(1)}, bf16[256,1024]{1,0:T(8,128)(2,1)S(1)}, bf16[256,1024]{1,0:T(8,128)(2,1)S(1)}, f32[256,256]{1,0:T(8,128)S(1)},...) custom-call(bf16[1024,256]{1,0:T(8,128)(2,1)} %acts.1, ...), custom_call_target="tpu_custom_call" | custom-call | flops 268435456 | bytes 4194304 | tf_op jit(solution)/shard_map/first/pallas_call | solution.py:113
  2.9 0.1 copy-done.1
  3.1 0.0 copy-start.2
  3.1 0.7 %merged.1 = (f32[256,512]{1,0:T(8,128)S(1)}, f32[256,512]{1,0:T(8,128)S(1)}) custom-call(bf16[256,1024]{1,0:T(8,128)(2,1)S(1)} %get-tuple-element.22.acts_t, f32[1,256,1024]{2,1,0:T(8,128)S(1)} %copy-done.1, bf16[256,1024]{1,0:T(8,128)(2,1)S(1)} %get-tuple-element.23.rest_0_, bf16[256,1024]{1,0:T(8,128)(2,1)S(1)} %get-tuple-element.24.rest_1_.rest_0_, ...), custom_call_target="tpu_custom_call" | custom-call | flops 536870912 | bytes 4194304 | tf_op jit(solution)/shard_map/merged/pallas_call | solution.py:175
  3.8 0.6 %collective-permute-start.3 = (f32[256,512]{1,0:T(8,128)S(1)}, f32[256,512]{1,0:T(8,128)S(1)}, u32[]{:S(2)}, u32[]{:S(2)}) collective-permute-start(f32[256,512]{1,0:T(8,128)S(1)} %get-tuple-element.27.theirs.rest_3_), channel_id=1, source_target_pairs={{0,4},{4,0},{8,12},{12,8},{16,20},{20,16},{24,28},{28,24},{1,5},{5... | collective-permute-start | bytes 1572872 | tf_op jit(solution)/shard_map/ppermute | solution.py:388
  4.3 1.5 %collective-permute-done.3.came = f32[256,512]{1,0:T(8,128)S(1)} collective-permute-done((f32[256,512]{1,0:T(8,128)S(1)}, f32[256,512]{1,0:T(8,128)S(1)}, u32[]{:S(2)}, u32[]{:S(2)}) %collective-permute-start.3) | collective-permute-done | bytes 524320 | tf_op jit(solution)/shard_map/ppermute | solution.py:388
  5.9 0.1 begin.1
  6.0 2.9 %collective-permute-start.4 = (f32[256,256]{1,0:T(8,128)S(1)}, f32[256,256]{1,0:T(8,128)S(1)}, u32[]{:S(2)}, u32[]{:S(2)}) collective-permute-start(f32[256,256]{1,0:T(8,128)S(1)} %get-tuple-element.30), channel_id=1, source_target_pairs={{0,8},{4,20},{8,0},{12,28},{16,24},{20,4},{24,16},{28,12},{1,9},{5... | collective-permute-start | bytes 786440 | tf_op jit(solution)/shard_map/ppermute | solution.py:391
  8.9 1.6 %collective-permute-start.9 = (f32[256,256]{1,0:T(8,128)S(1)}, f32[256,256]{1,0:T(8,128)S(1)}, u32[]{:S(2)}, u32[]{:S(2)}) collective-permute-start(f32[256,256]{1,0:T(8,128)S(1)} %get-tuple-element.39), channel_id=1, source_target_pairs={{0,1},{1,0},{2,3},{3,2},{4,5},{5,4},{6,7},{7,6},{8,9},{9,8},{10,11... | collective-permute-start | bytes 786440 | tf_op jit(solution)/shard_map/ppermute | solution.py:384
  10.4 2.8 %collective-permute-done.4 = f32[256,256]{1,0:T(8,128)S(1)} collective-permute-done((f32[256,256]{1,0:T(8,128)S(1)}, f32[256,256]{1,0:T(8,128)S(1)}, u32[]{:S(2)}, u32[]{:S(2)}) %collective-permute-start.4) | collective-permute-done | bytes 262176 | tf_op jit(solution)/shard_map/ppermute | solution.py:391
  13.2 2.1 %collective-permute-start.5 = (f32[256,256]{1,0:T(8,128)S(1)}, f32[256,256]{1,0:T(8,128)S(1)}, u32[]{:S(2)}, u32[]{:S(2)}) collective-permute-start(f32[256,256]{1,0:T(8,128)S(1)} %add.11.total_a), channel_id=1, source_target_pairs={{0,16},{4,12},{8,24},{12,4},{16,0},{20,28},{24,8},{28,20},{1,17},{... | collective-permute-start | bytes 786440 | tf_op jit(solution)/shard_map/ppermute | solution.py:395
  15.4 0.0 copy-done.2
  15.4 0.6 %left.1 = f32[64,256]{1,0:T(8,128)S(1)} custom-call(f32[64,1024]{1,0:T(8,128)S(1)} %bitcast.1, f32[256,512]{1,0:T(8,128)S(1)} %get-tuple-element.27.theirs.rest_3_, f32[256,512]{1,0:T(8,128)S(1)} %get-tuple-element.28.mine.rest_2_), custom_call_target="tpu_custom_call" | custom-call | tf_op jit(solution)/shard_map/left/pallas_call | solution.py:214
  16.0 0.1 collective-permute-start
  16.0 1.0 %rest.1 = (f32[256,256]{1,0:T(8,128)S(1)}, f32[256,256]{1,0:T(8,128)S(1)}, f32[256,256]{1,0:T(8,128)S(1)}) custom-call(bf16[256,1024]{1,0:T(8,128)(2,1)S(1)} %get-tuple-element.35.high, bf16[256,1024]{1,0:T(8,128)(2,1)S(1)} %get-tuple-element.36.low, bf16[256,1024]{1,0:T(8,128)(2,1)S(1)} %get-tuple-element.24.rest_1_.rest_0_, ...), custom_call_target="tpu_custom_call" | custom-call | flops 805306368 | bytes 4194304 | tf_op jit(solution)/shard_map/rest/pallas_call | solution.py:147
  17.1 2.1 %collective-permute-start.11 = (f32[256,256]{1,0:T(8,128)S(1)}, f32[256,256]{1,0:T(8,128)S(1)}, u32[]{:S(2)}, u32[]{:S(2)}) collective-permute-start(f32[256,256]{1,0:T(8,128)S(1)} %get-tuple-element.40), channel_id=1, source_target_pairs={{0,1},{1,0},{2,3},{3,2},{4,5},{5,4},{6,7},{7,6},{8,9},{9,8},{10,11... | collective-permute-start | bytes 786440 | tf_op jit(solution)/shard_map/ppermute | solution.py:384
  19.2 0.0 collective-permute-done.9.refs_1_
  19.2 2.7 %collective-permute-start.10 = (f32[256,256]{1,0:T(8,128)S(1)}, f32[256,256]{1,0:T(8,128)S(1)}, u32[]{:S(2)}, u32[]{:S(2)}) collective-permute-start(f32[256,256]{1,0:T(8,128)S(1)} %shard_map.78), channel_id=1, source_target_pairs={{0,2},{1,3},{2,0},{3,1},{4,6},{5,7},{6,4},{7,5},{8,10},{9,11},{10,... | collective-permute-start | bytes 786440 | tf_op jit(solution)/shard_map/ppermute | solution.py:384
  21.9 0.0 collective-permute-done
  21.9 1.6 %collective-permute-start.1 = (f32[64,256]{1,0:T(8,128)S(1)}, f32[64,256]{1,0:T(8,128)S(1)}, u32[]{:S(2)}, u32[]{:S(2)}) collective-permute-start(f32[64,256]{1,0:T(8,128)S(1)} %add.9), channel_id=1, source_target_pairs={{0,8},{4,20},{8,0},{12,28},{16,24},{20,4},{24,16},{28,12},{1,9},{5... | collective-permute-start | bytes 196616 | tf_op jit(solution)/shard_map/ppermute | solution.py:396
  23.5 2.8 %collective-permute-done.1 = f32[64,256]{1,0:T(8,128)S(1)} collective-permute-done((f32[64,256]{1,0:T(8,128)S(1)}, f32[64,256]{1,0:T(8,128)S(1)}, u32[]{:S(2)}, u32[]{:S(2)}) %collective-permute-start.1) | collective-permute-done | bytes 65568 | tf_op jit(solution)/shard_map/ppermute | solution.py:396
  26.2 0.1 collective-permute-start.2
  26.3 1.2 %collective-permute-done.2.b_ref.left_b = f32[64,256]{1,0:T(8,128)S(1)} collective-permute-done((f32[64,256]{1,0:T(8,128)S(1)}, f32[64,256]{1,0:T(8,128)S(1)}, u32[]{:S(2)}, u32[]{:S(2)}) %collective-permute-start.2) | collective-permute-done | bytes 65568 | tf_op jit(solution)/shard_map/ppermute | solution.py:397
  27.6 0.0 collective-permute-done.5.total_b
  27.6 0.2 right.1.rest_0_
  27.8 0.0 copy-start
  27.8 0.2 collective-permute-start.8
  28.0 1.4 %collective-permute-start.7 = (f32[64,256]{1,0:T(8,128)S(1)}, f32[64,256]{1,0:T(8,128)S(1)}, u32[]{:S(2)}, u32[]{:S(2)}) collective-permute-start(f32[64,256]{1,0:T(8,128)S(1)} %right.1.rest_0_), channel_id=1, source_target_pairs={{0,12},{4,16},{8,4},{12,24},{16,28},{20,0},{24,20},{28,8},{1,13},{... | collective-permute-start | bytes 196616 | tf_op jit(solution)/shard_map/ppermute | solution.py:413
  29.4 0.5 %collective-permute-start.6 = (f32[64,256]{1,0:T(8,128)S(1)}, f32[64,256]{1,0:T(8,128)S(1)}, u32[]{:S(2)}, u32[]{:S(2)}) collective-permute-start(f32[64,256]{1,0:T(8,128)S(1)} %right.1.rest_0_), channel_id=1, source_target_pairs={{0,8},{4,20},{8,0},{12,28},{16,24},{20,4},{24,16},{28,12},{1,9},{5... | collective-permute-start | bytes 196616 | tf_op jit(solution)/shard_map/ppermute | solution.py:412
  30.0 3.5 %solve.1.basis = f32[64,256]{1,0:T(8,128)S(1)} custom-call(f32[64,256]{1,0:T(8,128)S(1)} %add.10.a_ref.left_a, f32[64,256]{1,0:T(8,128)S(1)} %collective-permute-done.2.b_ref.left_b), custom_call_target="tpu_custom_call" | custom-call | flops 1073741824 | bytes 1048576 | tf_op jit(solution)/shard_map/solve/pallas_call | solution.py:265
  33.5 0.0 collective-permute-done.11.refs_2_
  33.5 0.0 collective-permute-done.10.refs_1_
  33.5 0.7 %shard_map.79 = f32[256,256]{1,0:T(8,128)} custom-call(f32[256,256]{1,0:T(8,128)S(1)} %get-tuple-element.37.refs_0_, f32[256,256]{1,0:T(8,128)S(1)} %collective-permute-done.10.refs_1_, f32[256,256]{1,0:T(8,128)S(1)} %collective-permute-done.11.refs_2_), custom_call_target="tpu_custom_call" | custom-call | tf_op jit(solution)/shard_map/pallas_call | solution.py:196
  34.2 0.0 collective-permute-done.8.rest_1_
  34.2 0.0 copy-done
  34.2 1.4 %shard_map.76 = (f32[256,1024]{1,0:T(8,128)}, f32[1,256,1024]{2,1,0:T(8,128)}) custom-call(f32[64,256]{1,0:T(8,128)S(1)} %solve.1.basis, f32[256,1024]{1,0:T(8,128)S(1)} %copy-done, f32[64,256]{1,0:T(8,128)S(1)} %right.1.rest_0_, f32[64,256]{1,0:T(8,128)S(1)} %collective-permute-done.8.rest_1_, f32[256,512]{1,0:T(8,128)S(1)} %get-tuple-element.28.mine.rest_2_, ...), custom_call_target="tpu_custom_call" | custom-call | tf_op jit(solution)/shard_map/pallas_call | solution.py:353
  35.7 0.0 collective-permute-done.7.rest_1_
  35.7 0.0 collective-permute-done.6.rest_0_
  35.7 1.4 %shard_map.77 = (f32[256,1024]{1,0:T(8,128)}, f32[1,256,1024]{2,1,0:T(8,128)}) custom-call(f32[64,256]{1,0:T(8,128)S(1)} %solve.1.basis, f32[256,1024]{1,0:T(8,128)S(1)} %copy-done, f32[64,256]{1,0:T(8,128)S(1)} %collective-permute-done.6.rest_0_, f32[64,256]{1,0:T(8,128)S(1)} %collective-permute-done.7.rest_1_, ...), custom_call_target="tpu_custom_call", output_to_operand_aliasing={{0}: (6, {}), {1}: (7, {})} | custom-call | tf_op jit(solution)/shard_map/pallas_call | solution.py:353
  (4 shorter events, 0.1 us)
Async XLA Ops:
  0.6 2.4 %copy-start.1 = (f32[1,256,1024]{2,1,0:T(8,128)S(1)}, f32[1,256,1024]{2,1,0:T(8,128)}, u32[]{:S(2)}) copy-start(f32[1,256,1024]{2,1,0:T(8,128)} %err.1) | copy-start | bytes 3145732
  3.1 12.3 %copy-start.2 = (f32[1024,64]{0,1:T(8,128)S(1)}, f32[1024,64]{0,1:T(8,128)}, u32[]{:S(2)}) copy-start(f32[1024,64]{0,1:T(8,128)} %param.9) | copy-start | bytes 786436
  3.8 2.1 %collective-permute-start.3 = (f32[256,512]{1,0:T(8,128)S(1)}, f32[256,512]{1,0:T(8,128)S(1)}, u32[]{:S(2)}, u32[]{:S(2)}) collective-permute-start(f32[256,512]{1,0:T(8,128)S(1)} %get-tuple-element.27.theirs.rest_3_), channel_id=1, source_target_pairs={{0,4},{4,0},{8,12},{12,8},{16,20},{20,16},{24,28},{28,24},{1,5},{5... | collective-permute-start | bytes 1572872 | tf_op jit(solution)/shard_map/ppermute | solution.py:388
  6.0 7.3 %collective-permute-start.4 = (f32[256,256]{1,0:T(8,128)S(1)}, f32[256,256]{1,0:T(8,128)S(1)}, u32[]{:S(2)}, u32[]{:S(2)}) collective-permute-start(f32[256,256]{1,0:T(8,128)S(1)} %get-tuple-element.30), channel_id=1, source_target_pairs={{0,8},{4,20},{8,0},{12,28},{16,24},{20,4},{24,16},{28,12},{1,9},{5... | collective-permute-start | bytes 786440 | tf_op jit(solution)/shard_map/ppermute | solution.py:391
  8.9 10.3 %collective-permute-start.9 = (f32[256,256]{1,0:T(8,128)S(1)}, f32[256,256]{1,0:T(8,128)S(1)}, u32[]{:S(2)}, u32[]{:S(2)}) collective-permute-start(f32[256,256]{1,0:T(8,128)S(1)} %get-tuple-element.39), channel_id=1, source_target_pairs={{0,1},{1,0},{2,3},{3,2},{4,5},{5,4},{6,7},{7,6},{8,9},{9,8},{10,11... | collective-permute-start | bytes 786440 | tf_op jit(solution)/shard_map/ppermute | solution.py:384
  13.2 14.3 %collective-permute-start.5 = (f32[256,256]{1,0:T(8,128)S(1)}, f32[256,256]{1,0:T(8,128)S(1)}, u32[]{:S(2)}, u32[]{:S(2)}) collective-permute-start(f32[256,256]{1,0:T(8,128)S(1)} %add.11.total_a), channel_id=1, source_target_pairs={{0,16},{4,12},{8,24},{12,4},{16,0},{20,28},{24,8},{28,20},{1,17},{... | collective-permute-start | bytes 786440 | tf_op jit(solution)/shard_map/ppermute | solution.py:395
  16.0 5.9 %collective-permute-start = (f32[64,256]{1,0:T(8,128)S(1)}, f32[64,256]{1,0:T(8,128)S(1)}, u32[]{:S(2)}, u32[]{:S(2)}) collective-permute-start(f32[64,256]{1,0:T(8,128)S(1)} %left.1), channel_id=1, source_target_pairs={{0,16},{4,12},{8,24},{12,4},{16,0},{20,28},{24,8},{28,20},{1,17},{... | collective-permute-start | bytes 196616 | tf_op jit(solution)/shard_map/ppermute | solution.py:392
  17.1 16.4 %collective-permute-start.11 = (f32[256,256]{1,0:T(8,128)S(1)}, f32[256,256]{1,0:T(8,128)S(1)}, u32[]{:S(2)}, u32[]{:S(2)}) collective-permute-start(f32[256,256]{1,0:T(8,128)S(1)} %get-tuple-element.40), channel_id=1, source_target_pairs={{0,1},{1,0},{2,3},{3,2},{4,5},{5,4},{6,7},{7,6},{8,9},{9,8},{10,11... | collective-permute-start | bytes 786440 | tf_op jit(solution)/shard_map/ppermute | solution.py:384
  19.2 14.3 %collective-permute-start.10 = (f32[256,256]{1,0:T(8,128)S(1)}, f32[256,256]{1,0:T(8,128)S(1)}, u32[]{:S(2)}, u32[]{:S(2)}) collective-permute-start(f32[256,256]{1,0:T(8,128)S(1)} %shard_map.78), channel_id=1, source_target_pairs={{0,2},{1,3},{2,0},{3,1},{4,6},{5,7},{6,4},{7,5},{8,10},{9,11},{10,... | collective-permute-start | bytes 786440 | tf_op jit(solution)/shard_map/ppermute | solution.py:384
  21.9 4.3 %collective-permute-start.1 = (f32[64,256]{1,0:T(8,128)S(1)}, f32[64,256]{1,0:T(8,128)S(1)}, u32[]{:S(2)}, u32[]{:S(2)}) collective-permute-start(f32[64,256]{1,0:T(8,128)S(1)} %add.9), channel_id=1, source_target_pairs={{0,8},{4,20},{8,0},{12,28},{16,24},{20,4},{24,16},{28,12},{1,9},{5... | collective-permute-start | bytes 196616 | tf_op jit(solution)/shard_map/ppermute | solution.py:396
  26.2 1.3 %collective-permute-start.2 = (f32[64,256]{1,0:T(8,128)S(1)}, f32[64,256]{1,0:T(8,128)S(1)}, u32[]{:S(2)}, u32[]{:S(2)}) collective-permute-start(f32[64,256]{1,0:T(8,128)S(1)} %add.10.a_ref.left_a), channel_id=1, source_target_pairs={{0,4},{4,0},{8,12},{12,8},{16,20},{20,16},{24,28},{28,24},{1,5},{5... | collective-permute-start | bytes 196616 | tf_op jit(solution)/shard_map/ppermute | solution.py:397
  27.8 6.5 %copy-start = (f32[256,1024]{1,0:T(8,128)S(1)}, f32[256,1024]{1,0:T(8,128)}, u32[]{:S(2)}) copy-start(f32[256,1024]{1,0:T(8,128)} %wt.5) | copy-start | bytes 3145732
  27.8 6.5 %collective-permute-start.8 = (f32[64,256]{1,0:T(8,128)S(1)}, f32[64,256]{1,0:T(8,128)S(1)}, u32[]{:S(2)}, u32[]{:S(2)}) collective-permute-start(f32[64,256]{1,0:T(8,128)S(1)} %right.1.rest_0_), channel_id=1, source_target_pairs={{0,4},{4,0},{8,12},{12,8},{16,20},{20,16},{24,28},{28,24},{1,5},{5... | collective-permute-start | bytes 196616 | tf_op jit(solution)/shard_map/ppermute | solution.py:411
  28.0 7.7 %collective-permute-start.7 = (f32[64,256]{1,0:T(8,128)S(1)}, f32[64,256]{1,0:T(8,128)S(1)}, u32[]{:S(2)}, u32[]{:S(2)}) collective-permute-start(f32[64,256]{1,0:T(8,128)S(1)} %right.1.rest_0_), channel_id=1, source_target_pairs={{0,12},{4,16},{8,4},{12,24},{16,28},{20,0},{24,20},{28,8},{1,13},{... | collective-permute-start | bytes 196616 | tf_op jit(solution)/shard_map/ppermute | solution.py:413
  29.4 6.2 %collective-permute-start.6 = (f32[64,256]{1,0:T(8,128)S(1)}, f32[64,256]{1,0:T(8,128)S(1)}, u32[]{:S(2)}, u32[]{:S(2)}) collective-permute-start(f32[64,256]{1,0:T(8,128)S(1)} %right.1.rest_0_), channel_id=1, source_target_pairs={{0,8},{4,20},{8,0},{12,28},{16,24},{20,4},{24,16},{28,12},{1,9},{5... | collective-permute-start | bytes 196616 | tf_op jit(solution)/shard_map/ppermute | solution.py:412

commit v8 on v7

--- a/solution.py
+++ b/solution.py
@@ -153,7 +153,6 @@
         cost_estimate=pl.CostEstimate(
             flops=4 * len(rows) * block * din * cols, bytes_accessed=4 << 20, transcendentals=0
         ),
-        name="rest",
     )(*halves, *rows)
 
 
@@ -396,15 +395,16 @@
         left = left + lax.ppermute(left, "dp", swap(other, one, replicas))
     left_came = lax.ppermute(left, "dp", pair)
 
-    blocks = rest_of(halves, rows[1:])
+    blocks = rest_of(halves, rows[2:])
     for n in range(1, n_tensor - 1):
-        block, adds = blocks[n], rounds[n][1]
+        block, adds = blocks[n - 1], rounds[n][1]
         if adds is not None:
             block = summed(block, received[adds])
         received.append(across(block, n))
     relayed = {adds for _, adds in rounds}
     final = [one for n, one in enumerate(received) if n not in relayed]
-    input_grad = summed(blocks[0], *final)
+    own = rest_of(halves, rows[1:2])[0]
+    input_grad = summed(own, *final)
 
     basis = solve(left, left_came, replicas)
     right = right_of(left, left_came, total, came, replicas)

time: 37.3 us -> 37 us (level)
  waiting for transfers between devices: 8.35 us -> 7.87 us
    ppermute x1, waiting for transfers between devices: 1.24 us -> 0.77 us  [step(): left_came = lax.ppermute(left, 'dp', pair)]
    pallas_call x1 -> x2, Pallas kernels: 1.01 us -> 1.21 us  [rest_of(): pl.pallas_call(rest_kernel, out_shape=[jax.ShapeDtypeStruct((block, din),...]
  transfers between devices with their start and end apart: 12 -> 12, of which waited for: 4 -> 4; matrix products, arithmetic and copies ran while one was open for 0% -> 0% of each run, Pallas kernels for 20% -> 21%
where the time goes in v8:
time: 37 us; the launch traced here: 36.8 us
  starting transfers between devices  15.9 us (43%)
  Pallas kernels  12.1 us (33%)
  waiting for transfers between devices  7.87 us (21%)
  between operations  0.77 us (2%)
    ppermute x3, starting transfers between devices, across(): lax.ppermute(block, 'tensor', [(a, to) for a, (to, _) in tables[n].items()])  6.35 us
    pallas_call x1, Pallas kernels, solve(): pl.pallas_call(functools.partial(solve_kernel, replicas), out_shape=jax.S...  3.49 us
    ppermute x1, starting transfers between devices, step(): came = lax.ppermute(give, 'dp', swap(bits[0], bits[-1], replicas))  2.9 us
    pallas_call x2, Pallas kernels, back(): pl.pallas_call(functools.partial(back_kernel, pieces, bits), out_shape=[j...  2.83 us
    ppermute x1, waiting for transfers between devices, step(): left = left + lax.ppermute(left, 'dp', swap(other, one, replicas))  2.78 us
    ppermute x1, waiting for transfers between devices, step(): came = lax.ppermute(give, 'dp', swap(bits[0], bits[-1], replicas))  2.78 us
    pallas_call x1, Pallas kernels, first_of(): pl.pallas_call(functools.partial(first_kernel, tables, n, chunks), out_sh...  2.27 us
    ppermute x1, starting transfers between devices, step(): came = lax.ppermute(total, 'dp', swap(one, other, replicas))  2.11 us
  transfers between devices with their start and end apart: 12, of which 4 were waited for; matrix products, arithmetic and copies ran while one was open for 0% of the time, Pallas kernels for 21%

profile of v8, /device:TPU:0, one launch (start us, length us, event | category | flops | bytes accessed | tf_op | source)
XLA Modules:
  0.0 36.8 jit_solution(11445325148872107996)
XLA Ops:
  0.6 0.0 copy-start.1
  0.6 2.3 %first.1 = (bf16[256,1024]{1,0:T(8,128)(2,1)S(1)}, bf16[256,1024]{1,0:T(8,128)(2,1)S(1)}, bf16[256,1024]{1,0:T(8,128)(2,1)S(1)}, f32[256,256]{1,0:T(8,128)S(1)},...) custom-call(bf16[1024,256]{1,0:T(8,128)(2,1)} %acts.1, ...), custom_call_target="tpu_custom_call" | custom-call | flops 268435456 | bytes 4194304 | tf_op jit(solution)/shard_map/first/pallas_call | solution.py:113
  2.9 0.1 copy-done.1
  3.1 0.0 copy-start.2
  3.1 0.7 %merged.1 = (f32[256,512]{1,0:T(8,128)S(1)}, f32[256,512]{1,0:T(8,128)S(1)}) custom-call(bf16[256,1024]{1,0:T(8,128)(2,1)S(1)} %get-tuple-element.21.acts_t, f32[1,256,1024]{2,1,0:T(8,128)S(1)} %copy-done.1, bf16[256,1024]{1,0:T(8,128)(2,1)S(1)} %get-tuple-element.22.rest_0_, bf16[256,1024]{1,0:T(8,128)(2,1)S(1)} %get-tuple-element.23.rest_1_.rest_0_, ...), custom_call_target="tpu_custom_call" | custom-call | flops 536870912 | bytes 4194304 | tf_op jit(solution)/shard_map/merged/pallas_call | solution.py:174
  3.8 0.6 %collective-permute-start.3 = (f32[256,512]{1,0:T(8,128)S(1)}, f32[256,512]{1,0:T(8,128)S(1)}, u32[]{:S(2)}, u32[]{:S(2)}) collective-permute-start(f32[256,512]{1,0:T(8,128)S(1)} %get-tuple-element.26.theirs.rest_3_), channel_id=1, source_target_pairs={{0,4},{4,0},{8,12},{12,8},{16,20},{20,16},{24,28},{28,24},{1,5},{5... | collective-permute-start | bytes 1572872 | tf_op jit(solution)/shard_map/ppermute | solution.py:387
  4.3 1.5 %collective-permute-done.3.came = f32[256,512]{1,0:T(8,128)S(1)} collective-permute-done((f32[256,512]{1,0:T(8,128)S(1)}, f32[256,512]{1,0:T(8,128)S(1)}, u32[]{:S(2)}, u32[]{:S(2)}) %collective-permute-start.3) | collective-permute-done | bytes 524320 | tf_op jit(solution)/shard_map/ppermute | solution.py:387
  5.9 0.1 begin.1
  6.0 2.9 %collective-permute-start.4 = (f32[256,256]{1,0:T(8,128)S(1)}, f32[256,256]{1,0:T(8,128)S(1)}, u32[]{:S(2)}, u32[]{:S(2)}) collective-permute-start(f32[256,256]{1,0:T(8,128)S(1)} %get-tuple-element.29), channel_id=1, source_target_pairs={{0,8},{4,20},{8,0},{12,28},{16,24},{20,4},{24,16},{28,12},{1,9},{5... | collective-permute-start | bytes 786440 | tf_op jit(solution)/shard_map/ppermute | solution.py:390
  8.9 1.6 %collective-permute-start.9 = (f32[256,256]{1,0:T(8,128)S(1)}, f32[256,256]{1,0:T(8,128)S(1)}, u32[]{:S(2)}, u32[]{:S(2)}) collective-permute-start(f32[256,256]{1,0:T(8,128)S(1)} %get-tuple-element.37), channel_id=1, source_target_pairs={{0,1},{1,0},{2,3},{3,2},{4,5},{5,4},{6,7},{7,6},{8,9},{9,8},{10,11... | collective-permute-start | bytes 786440 | tf_op jit(solution)/shard_map/ppermute | solution.py:383
  10.4 2.8 %collective-permute-done.4 = f32[256,256]{1,0:T(8,128)S(1)} collective-permute-done((f32[256,256]{1,0:T(8,128)S(1)}, f32[256,256]{1,0:T(8,128)S(1)}, u32[]{:S(2)}, u32[]{:S(2)}) %collective-permute-start.4) | collective-permute-done | bytes 262176 | tf_op jit(solution)/shard_map/ppermute | solution.py:390
  13.2 2.1 %collective-permute-start.5 = (f32[256,256]{1,0:T(8,128)S(1)}, f32[256,256]{1,0:T(8,128)S(1)}, u32[]{:S(2)}, u32[]{:S(2)}) collective-permute-start(f32[256,256]{1,0:T(8,128)S(1)} %add.11.total_a), channel_id=1, source_target_pairs={{0,16},{4,12},{8,24},{12,4},{16,0},{20,28},{24,8},{28,20},{1,17},{... | collective-permute-start | bytes 786440 | tf_op jit(solution)/shard_map/ppermute | solution.py:394
  15.4 0.0 copy-done.2
  15.4 0.6 %left.1 = f32[64,256]{1,0:T(8,128)S(1)} custom-call(f32[64,1024]{1,0:T(8,128)S(1)} %bitcast.1, f32[256,512]{1,0:T(8,128)S(1)} %get-tuple-element.26.theirs.rest_3_, f32[256,512]{1,0:T(8,128)S(1)} %get-tuple-element.27.mine.rest_2_), custom_call_target="tpu_custom_call" | custom-call | tf_op jit(solution)/shard_map/left/pallas_call | solution.py:213
  16.0 0.1 collective-permute-start
  16.0 0.7 %shard_map.79 = (f32[256,256]{1,0:T(8,128)S(1)}, f32[256,256]{1,0:T(8,128)S(1)}) custom-call(bf16[256,1024]{1,0:T(8,128)(2,1)S(1)} %get-tuple-element.34.high, bf16[256,1024]{1,0:T(8,128)(2,1)S(1)} %get-tuple-element.35.low, bf16[256,1024]{1,0:T(8,128)(2,1)S(1)} %get-tuple-element.24.rest_2_.rest_0_, bf16[256,1024]{1,0:T(8,128)(2,1)S(1)} %get-tuple-element.25.rest_3_.rest_1_), custom_call_target="tpu_custom_call" | custom-call | flops 536870912 | bytes 4194304 | tf_op jit(solution)/shard_map/pallas_call | solution.py:147
  16.8 2.1 %collective-permute-start.11 = (f32[256,256]{1,0:T(8,128)S(1)}, f32[256,256]{1,0:T(8,128)S(1)}, u32[]{:S(2)}, u32[]{:S(2)}) collective-permute-start(f32[256,256]{1,0:T(8,128)S(1)} %get-tuple-element.38), channel_id=1, source_target_pairs={{0,1},{1,0},{2,3},{3,2},{4,5},{5,4},{6,7},{7,6},{8,9},{9,8},{10,11... | collective-permute-start | bytes 786440 | tf_op jit(solution)/shard_map/ppermute | solution.py:383
  18.9 0.0 collective-permute-done.9.refs_1_
  18.9 2.7 %collective-permute-start.10 = (f32[256,256]{1,0:T(8,128)S(1)}, f32[256,256]{1,0:T(8,128)S(1)}, u32[]{:S(2)}, u32[]{:S(2)}) collective-permute-start(f32[256,256]{1,0:T(8,128)S(1)} %shard_map.80), channel_id=1, source_target_pairs={{0,2},{1,3},{2,0},{3,1},{4,6},{5,7},{6,4},{7,5},{8,10},{9,11},{10,... | collective-permute-start | bytes 786440 | tf_op jit(solution)/shard_map/ppermute | solution.py:383
  21.6 0.0 collective-permute-done
  21.6 1.6 %collective-permute-start.1 = (f32[64,256]{1,0:T(8,128)S(1)}, f32[64,256]{1,0:T(8,128)S(1)}, u32[]{:S(2)}, u32[]{:S(2)}) collective-permute-start(f32[64,256]{1,0:T(8,128)S(1)} %add.9), channel_id=1, source_target_pairs={{0,8},{4,20},{8,0},{12,28},{16,24},{20,4},{24,16},{28,12},{1,9},{5... | collective-permute-start | bytes 196616 | tf_op jit(solution)/shard_map/ppermute | solution.py:395
  23.2 2.8 %collective-permute-done.1 = f32[64,256]{1,0:T(8,128)S(1)} collective-permute-done((f32[64,256]{1,0:T(8,128)S(1)}, f32[64,256]{1,0:T(8,128)S(1)}, u32[]{:S(2)}, u32[]{:S(2)}) %collective-permute-start.1) | collective-permute-done | bytes 65568 | tf_op jit(solution)/shard_map/ppermute | solution.py:395
  26.0 0.1 collective-permute-start.2
  26.0 0.5 %shard_map.78.refs_0_ = f32[256,256]{1,0:T(8,128)S(1)} custom-call(bf16[256,1024]{1,0:T(8,128)(2,1)S(1)} %get-tuple-element.34.high, bf16[256,1024]{1,0:T(8,128)(2,1)S(1)} %get-tuple-element.35.low, bf16[256,1024]{1,0:T(8,128)(2,1)S(1)} %get-tuple-element.23.rest_1_.rest_0_), custom_call_target="tpu_custom_call" | custom-call | flops 268435456 | bytes 4194304 | tf_op jit(solution)/shard_map/pallas_call | solution.py:147
  26.5 0.8 %collective-permute-done.2.b_ref.left_b = f32[64,256]{1,0:T(8,128)S(1)} collective-permute-done((f32[64,256]{1,0:T(8,128)S(1)}, f32[64,256]{1,0:T(8,128)S(1)}, u32[]{:S(2)}, u32[]{:S(2)}) %collective-permute-start.2) | collective-permute-done | bytes 65568 | tf_op jit(solution)/shard_map/ppermute | solution.py:396
  27.3 0.0 collective-permute-done.5.total_b
  27.3 0.2 right.1.rest_0_
  27.5 0.0 copy-start
  27.5 0.2 collective-permute-start.8
  27.7 1.4 %collective-permute-start.7 = (f32[64,256]{1,0:T(8,128)S(1)}, f32[64,256]{1,0:T(8,128)S(1)}, u32[]{:S(2)}, u32[]{:S(2)}) collective-permute-start(f32[64,256]{1,0:T(8,128)S(1)} %right.1.rest_0_), channel_id=1, source_target_pairs={{0,12},{4,16},{8,4},{12,24},{16,28},{20,0},{24,20},{28,8},{1,13},{... | collective-permute-start | bytes 196616 | tf_op jit(solution)/shard_map/ppermute | solution.py:413
  29.2 0.5 %collective-permute-start.6 = (f32[64,256]{1,0:T(8,128)S(1)}, f32[64,256]{1,0:T(8,128)S(1)}, u32[]{:S(2)}, u32[]{:S(2)}) collective-permute-start(f32[64,256]{1,0:T(8,128)S(1)} %right.1.rest_0_), channel_id=1, source_target_pairs={{0,8},{4,20},{8,0},{12,28},{16,24},{20,4},{24,16},{28,12},{1,9},{5... | collective-permute-start | bytes 196616 | tf_op jit(solution)/shard_map/ppermute | solution.py:412
  29.7 3.5 %solve.1.basis = f32[64,256]{1,0:T(8,128)S(1)} custom-call(f32[64,256]{1,0:T(8,128)S(1)} %add.10.a_ref.left_a, f32[64,256]{1,0:T(8,128)S(1)} %collective-permute-done.2.b_ref.left_b), custom_call_target="tpu_custom_call" | custom-call | flops 1073741824 | bytes 1048576 | tf_op jit(solution)/shard_map/solve/pallas_call | solution.py:264
  33.2 0.0 collective-permute-done.11.refs_2_
  33.2 0.0 collective-permute-done.10.refs_1_
  33.2 0.7 %shard_map.81 = f32[256,256]{1,0:T(8,128)} custom-call(f32[256,256]{1,0:T(8,128)S(1)} %shard_map.78.refs_0_, f32[256,256]{1,0:T(8,128)S(1)} %collective-permute-done.10.refs_1_, f32[256,256]{1,0:T(8,128)S(1)} %collective-permute-done.11.refs_2_), custom_call_target="tpu_custom_call" | custom-call | tf_op jit(solution)/shard_map/pallas_call | solution.py:195
  34.0 0.0 collective-permute-done.8.rest_1_
  34.0 0.0 copy-done
  34.0 1.4 %shard_map.76 = (f32[256,1024]{1,0:T(8,128)}, f32[1,256,1024]{2,1,0:T(8,128)}) custom-call(f32[64,256]{1,0:T(8,128)S(1)} %solve.1.basis, f32[256,1024]{1,0:T(8,128)S(1)} %copy-done, f32[64,256]{1,0:T(8,128)S(1)} %right.1.rest_0_, f32[64,256]{1,0:T(8,128)S(1)} %collective-permute-done.8.rest_1_, f32[256,512]{1,0:T(8,128)S(1)} %get-tuple-element.27.mine.rest_2_, ...), custom_call_target="tpu_custom_call" | custom-call | tf_op jit(solution)/shard_map/pallas_call | solution.py:352
  35.4 0.0 collective-permute-done.7.rest_1_
  35.4 0.0 collective-permute-done.6.rest_0_
  35.4 1.4 %shard_map.77 = (f32[256,1024]{1,0:T(8,128)}, f32[1,256,1024]{2,1,0:T(8,128)}) custom-call(f32[64,256]{1,0:T(8,128)S(1)} %solve.1.basis, f32[256,1024]{1,0:T(8,128)S(1)} %copy-done, f32[64,256]{1,0:T(8,128)S(1)} %collective-permute-done.6.rest_0_, f32[64,256]{1,0:T(8,128)S(1)} %collective-permute-done.7.rest_1_, ...), custom_call_target="tpu_custom_call", output_to_operand_aliasing={{0}: (6, {}), {1}: (7, {})} | custom-call | tf_op jit(solution)/shard_map/pallas_call | solution.py:352
  (4 shorter events, 0.1 us)
Async XLA Ops:
  0.6 2.4 %copy-start.1 = (f32[1,256,1024]{2,1,0:T(8,128)S(1)}, f32[1,256,1024]{2,1,0:T(8,128)}, u32[]{:S(2)}) copy-start(f32[1,256,1024]{2,1,0:T(8,128)} %err.1) | copy-start | bytes 3145732
  3.1 12.3 %copy-start.2 = (f32[1024,64]{0,1:T(8,128)S(1)}, f32[1024,64]{0,1:T(8,128)}, u32[]{:S(2)}) copy-start(f32[1024,64]{0,1:T(8,128)} %param.9) | copy-start | bytes 786436
  3.8 2.1 %collective-permute-start.3 = (f32[256,512]{1,0:T(8,128)S(1)}, f32[256,512]{1,0:T(8,128)S(1)}, u32[]{:S(2)}, u32[]{:S(2)}) collective-permute-start(f32[256,512]{1,0:T(8,128)S(1)} %get-tuple-element.26.theirs.rest_3_), channel_id=1, source_target_pairs={{0,4},{4,0},{8,12},{12,8},{16,20},{20,16},{24,28},{28,24},{1,5},{5... | collective-permute-start | bytes 1572872 | tf_op jit(solution)/shard_map/ppermute | solution.py:387
  6.0 7.3 %collective-permute-start.4 = (f32[256,256]{1,0:T(8,128)S(1)}, f32[256,256]{1,0:T(8,128)S(1)}, u32[]{:S(2)}, u32[]{:S(2)}) collective-permute-start(f32[256,256]{1,0:T(8,128)S(1)} %get-tuple-element.29), channel_id=1, source_target_pairs={{0,8},{4,20},{8,0},{12,28},{16,24},{20,4},{24,16},{28,12},{1,9},{5... | collective-permute-start | bytes 786440 | tf_op jit(solution)/shard_map/ppermute | solution.py:390
  8.9 10.1 %collective-permute-start.9 = (f32[256,256]{1,0:T(8,128)S(1)}, f32[256,256]{1,0:T(8,128)S(1)}, u32[]{:S(2)}, u32[]{:S(2)}) collective-permute-start(f32[256,256]{1,0:T(8,128)S(1)} %get-tuple-element.37), channel_id=1, source_target_pairs={{0,1},{1,0},{2,3},{3,2},{4,5},{5,4},{6,7},{7,6},{8,9},{9,8},{10,11... | collective-permute-start | bytes 786440 | tf_op jit(solution)/shard_map/ppermute | solution.py:383
  13.2 14.0 %collective-permute-start.5 = (f32[256,256]{1,0:T(8,128)S(1)}, f32[256,256]{1,0:T(8,128)S(1)}, u32[]{:S(2)}, u32[]{:S(2)}) collective-permute-start(f32[256,256]{1,0:T(8,128)S(1)} %add.11.total_a), channel_id=1, source_target_pairs={{0,16},{4,12},{8,24},{12,4},{16,0},{20,28},{24,8},{28,20},{1,17},{... | collective-permute-start | bytes 786440 | tf_op jit(solution)/shard_map/ppermute | solution.py:394
  16.0 5.6 %collective-permute-start = (f32[64,256]{1,0:T(8,128)S(1)}, f32[64,256]{1,0:T(8,128)S(1)}, u32[]{:S(2)}, u32[]{:S(2)}) collective-permute-start(f32[64,256]{1,0:T(8,128)S(1)} %left.1), channel_id=1, source_target_pairs={{0,16},{4,12},{8,24},{12,4},{16,0},{20,28},{24,8},{28,20},{1,17},{... | collective-permute-start | bytes 196616 | tf_op jit(solution)/shard_map/ppermute | solution.py:391
  16.8 16.4 %collective-permute-start.11 = (f32[256,256]{1,0:T(8,128)S(1)}, f32[256,256]{1,0:T(8,128)S(1)}, u32[]{:S(2)}, u32[]{:S(2)}) collective-permute-start(f32[256,256]{1,0:T(8,128)S(1)} %get-tuple-element.38), channel_id=1, source_target_pairs={{0,1},{1,0},{2,3},{3,2},{4,5},{5,4},{6,7},{7,6},{8,9},{9,8},{10,11... | collective-permute-start | bytes 786440 | tf_op jit(solution)/shard_map/ppermute | solution.py:383
  18.9 14.3 %collective-permute-start.10 = (f32[256,256]{1,0:T(8,128)S(1)}, f32[256,256]{1,0:T(8,128)S(1)}, u32[]{:S(2)}, u32[]{:S(2)}) collective-permute-start(f32[256,256]{1,0:T(8,128)S(1)} %shard_map.80), channel_id=1, source_target_pairs={{0,2},{1,3},{2,0},{3,1},{4,6},{5,7},{6,4},{7,5},{8,10},{9,11},{10,... | collective-permute-start | bytes 786440 | tf_op jit(solution)/shard_map/ppermute | solution.py:383
  21.6 4.3 %collective-permute-start.1 = (f32[64,256]{1,0:T(8,128)S(1)}, f32[64,256]{1,0:T(8,128)S(1)}, u32[]{:S(2)}, u32[]{:S(2)}) collective-permute-start(f32[64,256]{1,0:T(8,128)S(1)} %add.9), channel_id=1, source_target_pairs={{0,8},{4,20},{8,0},{12,28},{16,24},{20,4},{24,16},{28,12},{1,9},{5... | collective-permute-start | bytes 196616 | tf_op jit(solution)/shard_map/ppermute | solution.py:395
  26.0 1.3 %collective-permute-start.2 = (f32[64,256]{1,0:T(8,128)S(1)}, f32[64,256]{1,0:T(8,128)S(1)}, u32[]{:S(2)}, u32[]{:S(2)}) collective-permute-start(f32[64,256]{1,0:T(8,128)S(1)} %add.10.a_ref.left_a), channel_id=1, source_target_pairs={{0,4},{4,0},{8,12},{12,8},{16,20},{20,16},{24,28},{28,24},{1,5},{5... | collective-permute-start | bytes 196616 | tf_op jit(solution)/shard_map/ppermute | solution.py:396
  27.5 6.5 %copy-start = (f32[256,1024]{1,0:T(8,128)S(1)}, f32[256,1024]{1,0:T(8,128)}, u32[]{:S(2)}) copy-start(f32[256,1024]{1,0:T(8,128)} %wt.5) | copy-start | bytes 3145732
  27.5 6.5 %collective-permute-start.8 = (f32[64,256]{1,0:T(8,128)S(1)}, f32[64,256]{1,0:T(8,128)S(1)}, u32[]{:S(2)}, u32[]{:S(2)}) collective-permute-start(f32[64,256]{1,0:T(8,128)S(1)} %right.1.rest_0_), channel_id=1, source_target_pairs={{0,4},{4,0},{8,12},{12,8},{16,20},{20,16},{24,28},{28,24},{1,5},{5... | collective-permute-start | bytes 196616 | tf_op jit(solution)/shard_map/ppermute | solution.py:411
  27.7 7.7 %collective-permute-start.7 = (f32[64,256]{1,0:T(8,128)S(1)}, f32[64,256]{1,0:T(8,128)S(1)}, u32[]{:S(2)}, u32[]{:S(2)}) collective-permute-start(f32[64,256]{1,0:T(8,128)S(1)} %right.1.rest_0_), channel_id=1, source_target_pairs={{0,12},{4,16},{8,4},{12,24},{16,28},{20,0},{24,20},{28,8},{1,13},{... | collective-permute-start | bytes 196616 | tf_op jit(solution)/shard_map/ppermute | solution.py:413
  29.2 6.2 %collective-permute-start.6 = (f32[64,256]{1,0:T(8,128)S(1)}, f32[64,256]{1,0:T(8,128)S(1)}, u32[]{:S(2)}, u32[]{:S(2)}) collective-permute-start(f32[64,256]{1,0:T(8,128)S(1)} %right.1.rest_0_), channel_id=1, source_target_pairs={{0,8},{4,20},{8,0},{12,28},{16,24},{20,4},{24,16},{28,12},{1,9},{5... | collective-permute-start | bytes 196616 | tf_op jit(solution)/shard_map/ppermute | solution.py:412
